TPU v7x, 32 devices: a whole 2x2x4 slice. The times are simulated.
32 devices in a mesh: wide: 8 (over z, x), narrow: 4 (over y, core).
Axes of the slice: x: 2, y: 2, z: 4, core: 2. Of those that a mesh axis runs over, the one named last changes fastest.
Arguments:
- right_side: float32 [4, 128, 12, 128], P('narrow', 'wide'), may hold values from -160 to 160
- hop_blocks: bfloat16 [4, 128, 9, 64, 128], P('narrow', 'wide'), may hold values from -2 to 6
- restriction: float32 [4, 128, 64, 128], P('narrow', 'wide'), may hold values from -0.25 to 0.25
Outputs:
- solution_field: float32 [4, 128, 12, 128], P('narrow', 'wide')
- coarse_residual: float32 [4, 32, 12, 128], P(None, 'wide')
All inputs are finite; a program needn't handle non-finite values.
Results may differ from a plain program's by a relative error of at most 0.0053.
Values may be sent and summed in bfloat16 or wider, within the bound.
No kernel may reach another device: no remote copies, remote signals or barrier semaphores. Data moves between devices by JAX's collectives and lax.ppermute only.
A program may use at most 64 MiB of HBM per device.

v0:
```python
import jax
import jax.numpy as jnp
from jax import lax
from jax.sharding import PartitionSpec as P

ITERS = 4
YLOC = 2
LY = 16


def from_behind(value, axis, steps):
    count = lax.axis_size(axis)
    pairs = [(source, (source + steps) % count) for source in range(count)]
    return lax.ppermute(value, axis, pairs)


def padded(cells, sides, width):
    for axis, dim in sides:
        count = lax.axis_size(axis)
        head = lax.slice_in_dim(cells, 0, width, axis=dim)
        tail = lax.slice_in_dim(cells, cells.shape[dim] - width, cells.shape[dim], axis=dim)
        cells = jnp.concatenate(
            [
                lax.ppermute(tail, axis, [(i, (i + 1) % count) for i in range(count)]),
                cells,
                lax.ppermute(head, axis, [((i + 1) % count, i) for i in range(count)]),
            ],
            axis=dim,
        )
    return cells


def complex_pair(vector):
    half = vector.shape[-1] // 2
    real_part = vector[..., :half]
    imag_part = vector[..., half:]
    first = jnp.concatenate([real_part, -imag_part], -1)
    second = jnp.concatenate([imag_part, real_part], -1)
    return (first, second)


def plane_shift(block, step):
    return from_behind(block, "wide", step)


def row_shift(block, step):
    return from_behind(block, "wide", step)


def operate(rounded, hop_blocks):
    sites = rounded.shape[1]
    rhs_count = rounded.shape[2]
    width = rounded.shape[3]
    extended = padded(rounded, (("narrow", 0),), 1)
    grid = rounded[0].reshape(YLOC, sites // YLOC, rhs_count, width)
    rows_y = LY // YLOC
    ylabel = lax.axis_index("wide") % rows_y
    lowest = grid[0:1]
    highest = grid[YLOC - 1 : YLOC]
    if lax.axis_size("wide") > rows_y:
        z_forward = plane_shift(grid, -rows_y)
        z_backward = plane_shift(grid, rows_y)
    else:
        z_forward = grid
        z_backward = grid
    fwd_plain = row_shift(lowest, -1)
    fwd_wrap = row_shift(lowest, rows_y - 1)
    back_plain = row_shift(highest, 1)
    back_wrap = row_shift(highest, -(rows_y - 1))
    fwd_row = jnp.where(ylabel == rows_y - 1, fwd_wrap, fwd_plain)
    back_row = jnp.where(ylabel == 0, back_wrap, back_plain)
    y_forward = jnp.concatenate([grid[1:], fwd_row], 0)
    y_backward = jnp.concatenate([back_row, grid[:-1]], 0)
    flat_shape = (sites, rhs_count, width)
    views = [
        grid,
        jnp.roll(grid, -1, 1),
        jnp.roll(grid, 1, 1),
        y_forward,
        y_backward,
        z_forward,
        z_backward,
    ]
    views = [view.reshape(flat_shape) for view in views] + [extended[2], extended[0]]
    stacked = jnp.stack(views)
    first, second = complex_pair(stacked)
    paired = jnp.stack([first, second])
    result = jnp.einsum(
        "sdak,pdsrk->psra", hop_blocks[0], paired, preferred_element_type=jnp.float32
    )
    return jnp.concatenate([result[0], result[1]], -1)[None]


def restrict(vector, restriction):
    sites = vector.shape[1]
    rhs_count = vector.shape[2]
    first, second = complex_pair(vector[0])
    paired = jnp.stack([first, second])
    result = jnp.einsum(
        "sak,psrk->psra",
        restriction[0],
        paired,
        precision=lax.Precision.HIGHEST,
        preferred_element_type=jnp.float32,
    )
    persite = jnp.concatenate([result[0], result[1]], -1)
    grouped = persite.reshape(YLOC, sites // (YLOC * 2), 2, rhs_count, persite.shape[-1])
    return jnp.sum(grouped, axis=(0, 2))[None]


def partials(image, residual):
    half = image.shape[-1] // 2
    inner_re = jnp.sum(image * residual, axis=(0, 1, 3))
    inner_im = jnp.sum(
        image[..., :half] * residual[..., half:] - image[..., half:] * residual[..., :half],
        axis=(0, 1, 3),
    )
    power = jnp.sum(image * image, axis=(0, 1, 3))
    return (inner_re, inner_im, power)


def combine_sums(local):
    over_time = lax.psum((local[0], local[1], local[2]), "narrow")
    return lax.psum((over_time[0], over_time[1], over_time[2]), "wide")


def coefficients(totals):
    return (totals[0] / totals[2], totals[1] / totals[2])


def cmul(alpha_re, alpha_im, vector):
    half = vector.shape[-1] // 2
    real_part = vector[..., :half]
    imag_part = vector[..., half:]
    are = alpha_re[:, None]
    aim = alpha_im[:, None]
    return jnp.concatenate(
        [are * real_part - aim * imag_part, are * imag_part + aim * real_part], -1
    )


def per_device(right_side, hop_blocks, restriction):
    solution_field = jnp.zeros_like(right_side)
    residual = right_side
    for step in range(ITERS - 1):
        image = operate(residual.astype(jnp.bfloat16), hop_blocks)
        alpha_re, alpha_im = coefficients(combine_sums(partials(image, residual)))
        solution_field = solution_field + cmul(alpha_re, alpha_im, residual)
        residual = residual - cmul(alpha_re, alpha_im, image)
    image = operate(residual.astype(jnp.bfloat16), hop_blocks)
    local = partials(image, residual)
    alpha_re, alpha_im = coefficients(combine_sums(local))
    solution_field = solution_field + cmul(alpha_re, alpha_im, residual)
    residual = residual - cmul(alpha_re, alpha_im, image)
    coarse_residual = lax.all_gather(restrict(residual, restriction), "narrow", axis=0, tiled=True)
    return (solution_field, coarse_residual)


def solution(mesh):
    placed = (
        P("narrow", "wide", None, None),
        P("narrow", "wide", None, None, None),
        P("narrow", "wide", None, None),
    )
    return jax.shard_map(
        per_device,
        mesh=mesh,
        in_specs=placed,
        out_specs=(P("narrow", "wide", None, None), P(None, "wide", None, None)),
        check_vma=False,
    )
```

profile of v0, /device:TPU:0, one launch (start us, length us, event | category | flops | bytes accessed | tf_op | source)
XLA Modules:
  0.0 167.6 jit_solution(15555616473022862928)
XLA Ops:
  0.6 1.1 constant_dynamic-update-slice_fusion.8
  1.7 0.5 collective-permute-start.3
  2.3 2.0 %collective-permute-start.2 = (bf16[1,16,12,128]{3,2,0,1:T(8,128)(2,1)S(1)}, bf16[1,16,12,128]{3,2,0,1:T(8,128)(2,1)S(1)}, u32[]{:S(2)}, u32[]{:S(2)}) collective-permute-start(bf16[1,16,12,128]{3,2,0,1:T(8,128)(2,1)S(1)} %get-tuple-element.50), channel_id=1, source_target_pairs={{1,0},{2,1},{3,2},{0,3},{5,4},{6,5},{7,6},{4,7},{9,8},{10,9},{11,1... | collective-permute-start | bytes 147464 | tf_op jit(solution)/shard_map/ppermute | solution.py:26
  4.3 2.2 %collective-permute-start.1 = (bf16[1,8,12,128]{3,2,0,1:T(8,128)(2,1)S(1)}, bf16[1,8,12,128]{3,2,0,1:T(8,128)(2,1)S(1)}, u32[]{:S(2)}, u32[]{:S(2)}) collective-permute-start(bf16[1,8,12,128]{3,2,0,1:T(8,128)(2,1)S(1)} %get-tuple-element.129), channel_id=1, source_target_pairs={{0,4},{4,8},{8,12},{12,16},{16,20},{20,24},{24,28},{28,0},{1,5},{5... | collective-permute-start | bytes 73736 | tf_op jit(solution)/shard_map/ppermute | solution.py:14
  6.5 3.1 %collective-permute-start = (bf16[1,8,12,128]{3,2,0,1:T(8,128)(2,1)S(1)}, bf16[1,8,12,128]{3,2,0,1:T(8,128)(2,1)S(1)}, u32[]{:S(2)}, u32[]{:S(2)}) collective-permute-start(bf16[1,8,12,128]{3,2,0,1:T(8,128)(2,1)S(1)} %get-tuple-element.130), channel_id=1, source_target_pairs={{0,28},{4,0},{8,4},{12,8},{16,12},{20,16},{24,20},{28,24},{1,29},{... | collective-permute-start | bytes 73736 | tf_op jit(solution)/shard_map/ppermute | solution.py:14
  9.7 1.7 %collective-permute-done.1 = bf16[1,8,12,128]{3,2,0,1:T(8,128)(2,1)S(1)} collective-permute-done((bf16[1,8,12,128]{3,2,0,1:T(8,128)(2,1)S(1)}, bf16[1,8,12,128]{3,2,0,1:T(8,128)(2,1)S(1)}, u32[]{:S(2)}, u32[]{:S(2)}) %collective-permute-start.1) | collective-permute-done | bytes 24608 | tf_op jit(solution)/shard_map/ppermute | solution.py:14
  11.7 0.3 slice_negate_fusion.4
  12.0 0.7 maximum_bitcast_fusion
  12.7 0.8 fusion.14
  13.6 0.2 fusion.36
  13.8 0.2 multiply_reduce_fusion.3
  14.0 0.2 subtract_reduce_fusion.3
  14.3 5.7 %all-reduce.7 = (f32[12]{0:T(128)S(1)}, f32[12]{0:T(128)S(1)}, f32[12]{0:T(128)S(1)}) all-reduce(f32[12]{0:T(128)S(1)} %subtract_reduce_fusion.3, f32[12]{0:T(128)S(1)} %fusion.36, f32[12]{0:T(128)S(1)} %get-tuple-element.47), channel_id=1, replica_groups=mesh['wide'=8,'narrow'=4] {'narrow'}, use_global_device_ids=true, to_apply=%region_7.8 | all-reduce | flops 36 | bytes 288 | tf_op jit(solution)/shard_map/psum | solution.py:123
  19.9 21.8 %all-reduce.3 = (f32[12]{0:T(128)S(1)}, f32[12]{0:T(128)S(1)}, f32[12]{0:T(128)S(1)}) all-reduce(f32[12]{0:T(128)S(1)} %get-tuple-element.29, f32[12]{0:T(128)S(1)} %get-tuple-element.30, f32[12]{0:T(128)S(1)} %get-tuple-element.31), channel_id=1, replica_groups=mesh['wide'=8,'narrow'=4] {'wide'}, use_global_device_ids=true, to_apply=%region_8.9 | all-reduce | flops 36 | bytes 288 | tf_op jit(solution)/shard_map/psum | solution.py:124
  41.8 0.1 multiply_subtract_fusion.6
  41.9 0.1 constant_dynamic-update-slice_fusion.17
  42.1 1.7 %collective-permute-start.6 = (bf16[1,16,12,128]{3,2,1,0:T(8,128)(2,1)S(1)}, bf16[1,16,12,128]{3,2,1,0:T(8,128)(2,1)S(1)}, u32[]{:S(2)}, u32[]{:S(2)}) collective-permute-start(bf16[1,16,12,128]{3,2,1,0:T(8,128)(2,1)S(1)} %get-tuple-element.45), channel_id=1, source_target_pairs={{1,0},{2,1},{3,2},{0,3},{5,4},{6,5},{7,6},{4,7},{9,8},{10,9},{11,1... | collective-permute-start | bytes 147464 | tf_op jit(solution)/shard_map/ppermute | solution.py:26
  43.9 4.7 %collective-permute-start.4 = (bf16[1,8,12,128]{3,2,1,0:T(8,128)(2,1)S(1)}, bf16[1,8,12,128]{3,2,1,0:T(8,128)(2,1)S(1)}, u32[]{:S(2)}, u32[]{:S(2)}) collective-permute-start(bf16[1,8,12,128]{3,2,1,0:T(8,128)(2,1)S(1)} %get-tuple-element.124), channel_id=1, source_target_pairs={{0,28},{4,0},{8,4},{12,8},{16,12},{20,16},{24,20},{28,24},{1,29},{... | collective-permute-start | bytes 73736 | tf_op jit(solution)/shard_map/ppermute | solution.py:14
  48.7 1.5 collective-permute-done.4
  50.3 0.3 collective-permute-done.5
  50.7 0.3 slice_negate_fusion.3
  50.9 0.7 maximum_bitcast_fusion.2
  51.7 0.8 fusion.24
  52.5 0.2 multiply_reduce_fusion.2
  52.7 0.3 subtract_reduce_fusion.2
  53.0 0.2 fusion.39
  53.2 5.7 %all-reduce.6 = (f32[12]{0:T(128)S(1)}, f32[12]{0:T(128)S(1)}, f32[12]{0:T(128)S(1)}) all-reduce(f32[12]{0:T(128)S(1)} %subtract_reduce_fusion.2, f32[12]{0:T(128)S(1)} %fusion.39, f32[12]{0:T(128)S(1)} %get-tuple-element.42), channel_id=1, replica_groups=mesh['wide'=8,'narrow'=4] {'narrow'}, use_global_device_ids=true, to_apply=%region_16.17 | all-reduce | flops 36 | bytes 288 | tf_op jit(solution)/shard_map/psum | solution.py:123
  58.9 21.9 %all-reduce.2 = (f32[12]{0:T(128)S(1)}, f32[12]{0:T(128)S(1)}, f32[12]{0:T(128)S(1)}) all-reduce(f32[12]{0:T(128)S(1)} %get-tuple-element.26, f32[12]{0:T(128)S(1)} %get-tuple-element.27, f32[12]{0:T(128)S(1)} %get-tuple-element.28), channel_id=1, replica_groups=mesh['wide'=8,'narrow'=4] {'wide'}, use_global_device_ids=true, to_apply=%region_17.18 | all-reduce | flops 36 | bytes 288 | tf_op jit(solution)/shard_map/psum | solution.py:124
  80.8 0.1 multiply_subtract_fusion.4
  80.9 0.1 constant_dynamic-update-slice_fusion.26
  81.1 1.7 %collective-permute-start.10 = (bf16[1,16,12,128]{3,2,1,0:T(8,128)(2,1)S(1)}, bf16[1,16,12,128]{3,2,1,0:T(8,128)(2,1)S(1)}, u32[]{:S(2)}, u32[]{:S(2)}) collective-permute-start(bf16[1,16,12,128]{3,2,1,0:T(8,128)(2,1)S(1)} %get-tuple-element.40), channel_id=1, source_target_pairs={{1,0},{2,1},{3,2},{0,3},{5,4},{6,5},{7,6},{4,7},{9,8},{10,9},{11,1... | collective-permute-start | bytes 147464 | tf_op jit(solution)/shard_map/ppermute | solution.py:26
  83.0 4.7 %collective-permute-start.8 = (bf16[1,8,12,128]{3,2,1,0:T(8,128)(2,1)S(1)}, bf16[1,8,12,128]{3,2,1,0:T(8,128)(2,1)S(1)}, u32[]{:S(2)}, u32[]{:S(2)}) collective-permute-start(bf16[1,8,12,128]{3,2,1,0:T(8,128)(2,1)S(1)} %get-tuple-element.118), channel_id=1, source_target_pairs={{0,28},{4,0},{8,4},{12,8},{16,12},{20,16},{24,20},{28,24},{1,29},{... | collective-permute-start | bytes 73736 | tf_op jit(solution)/shard_map/ppermute | solution.py:14
  87.7 1.5 collective-permute-done.8
  89.3 0.3 collective-permute-done.9
  89.7 0.3 slice_negate_fusion.2
  90.0 0.7 maximum_bitcast_fusion.4
  90.7 0.8 fusion.29
  91.5 0.2 multiply_reduce_fusion.1
  91.8 0.3 subtract_reduce_fusion.1
  92.0 0.2 fusion.40
  92.2 5.7 %all-reduce.5 = (f32[12]{0:T(128)S(1)}, f32[12]{0:T(128)S(1)}, f32[12]{0:T(128)S(1)}) all-reduce(f32[12]{0:T(128)S(1)} %subtract_reduce_fusion.1, f32[12]{0:T(128)S(1)} %fusion.40, f32[12]{0:T(128)S(1)} %get-tuple-element.37), channel_id=1, replica_groups=mesh['wide'=8,'narrow'=4] {'narrow'}, use_global_device_ids=true, to_apply=%region_25.26 | all-reduce | flops 36 | bytes 288 | tf_op jit(solution)/shard_map/psum | solution.py:123
  97.9 21.9 %all-reduce.1 = (f32[12]{0:T(128)S(1)}, f32[12]{0:T(128)S(1)}, f32[12]{0:T(128)S(1)}) all-reduce(f32[12]{0:T(128)S(1)} %get-tuple-element.23, f32[12]{0:T(128)S(1)} %get-tuple-element.24, f32[12]{0:T(128)S(1)} %get-tuple-element.25), channel_id=1, replica_groups=mesh['wide'=8,'narrow'=4] {'wide'}, use_global_device_ids=true, to_apply=%region_26.27 | all-reduce | flops 36 | bytes 288 | tf_op jit(solution)/shard_map/psum | solution.py:124
  119.8 0.1 multiply_subtract_fusion.2
  119.9 0.1 constant_dynamic-update-slice_fusion.35
  120.1 1.7 %collective-permute-start.14 = (bf16[1,16,12,128]{3,2,1,0:T(8,128)(2,1)S(1)}, bf16[1,16,12,128]{3,2,1,0:T(8,128)(2,1)S(1)}, u32[]{:S(2)}, u32[]{:S(2)}) collective-permute-start(bf16[1,16,12,128]{3,2,1,0:T(8,128)(2,1)S(1)} %get-tuple-element.35), channel_id=1, source_target_pairs={{1,0},{2,1},{3,2},{0,3},{5,4},{6,5},{7,6},{4,7},{9,8},{10,9},{11,1... | collective-permute-start | bytes 147464 | tf_op jit(solution)/shard_map/ppermute | solution.py:26
  122.0 4.7 %collective-permute-start.12 = (bf16[1,8,12,128]{3,2,1,0:T(8,128)(2,1)S(1)}, bf16[1,8,12,128]{3,2,1,0:T(8,128)(2,1)S(1)}, u32[]{:S(2)}, u32[]{:S(2)}) collective-permute-start(bf16[1,8,12,128]{3,2,1,0:T(8,128)(2,1)S(1)} %get-tuple-element.112), channel_id=1, source_target_pairs={{0,28},{4,0},{8,4},{12,8},{16,12},{20,16},{24,20},{28,24},{1,29},{... | collective-permute-start | bytes 73736 | tf_op jit(solution)/shard_map/ppermute | solution.py:14
  126.8 1.5 collective-permute-done.12
  128.3 0.3 collective-permute-done.13
  128.7 0.3 slice_negate_fusion.1
  129.0 0.7 maximum_bitcast_fusion.6
  129.7 0.8 fusion.19
  130.5 0.2 multiply_reduce_fusion
  130.8 0.3 subtract_reduce_fusion
  131.0 0.2 fusion.41
  131.2 5.7 %all-reduce.4 = (f32[12]{0:T(128)S(1)}, f32[12]{0:T(128)S(1)}, f32[12]{0:T(128)S(1)}) all-reduce(f32[12]{0:T(128)S(1)} %subtract_reduce_fusion, f32[12]{0:T(128)S(1)} %fusion.41, f32[12]{0:T(128)S(1)} %get-tuple-element.32), channel_id=1, replica_groups=mesh['wide'=8,'narrow'=4] {'narrow'}, use_global_device_ids=true, to_apply=%region_34.35 | all-reduce | flops 36 | bytes 288 | tf_op jit(solution)/shard_map/psum | solution.py:123
  136.9 21.9 %all-reduce = (f32[12]{0:T(128)S(1)}, f32[12]{0:T(128)S(1)}, f32[12]{0:T(128)S(1)}) all-reduce(f32[12]{0:T(128)S(1)} %get-tuple-element.20, f32[12]{0:T(128)S(1)} %get-tuple-element.21, f32[12]{0:T(128)S(1)} %get-tuple-element.22), channel_id=1, replica_groups=mesh['wide'=8,'narrow'=4] {'wide'}, use_global_device_ids=true, to_apply=%region_35.36 | all-reduce | flops 36 | bytes 288 | tf_op jit(solution)/shard_map/psum | solution.py:124
  158.8 0.1 multiply_subtract_fusion
  158.9 0.2 fusion.38
  159.2 0.7 copy.56
  160.1 0.1 maximum_bitcast_fusion.12
  160.2 0.9 convolution_bitcast_fusion
  161.2 0.1 maximum_reduce_fusion
  161.3 5.6 %all-gather = f32[16,12,128]{2,1,0:T(8,128)S(1)} all-gather(f32[4,12,128]{2,1,0:T(8,128)S(1)} %maximum_reduce_fusion), channel_id=2, replica_groups=mesh['wide'=8,'narrow'=4] {'narrow'}, dimensions={0}, use_global_device_ids=true | all-gather | bytes 122880 | tf_op jit(solution)/shard_map/all_gather | solution.py:155
  166.9 0.7 copy.57
  (93 shorter events, 1.7 us)
Async XLA Ops:
  0.6 12.1 %copy-start = (bf16[1,16,9,64,128]{4,3,2,1,0:T(8,128)(2,1)S(1)}, bf16[1,16,9,64,128]{4,3,2,1,0:T(8,128)(2,1)}, u32[]{:S(2)}) copy-start(bf16[1,16,9,64,128]{4,3,2,1,0:T(8,128)(2,1)} %param.4) | copy-start | bytes 7077892
  1.7 9.9 %collective-permute-start.3 = (bf16[1,16,12,128]{3,2,0,1:T(8,128)(2,1)S(1)}, bf16[1,16,12,128]{3,2,0,1:T(8,128)(2,1)S(1)}, u32[]{:S(2)}, u32[]{:S(2)}) collective-permute-start(bf16[1,16,12,128]{3,2,0,1:T(8,128)(2,1)S(1)} %get-tuple-element.50), channel_id=1, source_target_pairs={{0,1},{1,2},{2,3},{3,0},{4,5},{5,6},{6,7},{7,4},{8,9},{9,10},{10,1... | collective-permute-start | bytes 147464 | tf_op jit(solution)/shard_map/ppermute | solution.py:24
  2.3 9.4 %collective-permute-start.2 = (bf16[1,16,12,128]{3,2,0,1:T(8,128)(2,1)S(1)}, bf16[1,16,12,128]{3,2,0,1:T(8,128)(2,1)S(1)}, u32[]{:S(2)}, u32[]{:S(2)}) collective-permute-start(bf16[1,16,12,128]{3,2,0,1:T(8,128)(2,1)S(1)} %get-tuple-element.50), channel_id=1, source_target_pairs={{1,0},{2,1},{3,2},{0,3},{5,4},{6,5},{7,6},{4,7},{9,8},{10,9},{11,1... | collective-permute-start | bytes 147464 | tf_op jit(solution)/shard_map/ppermute | solution.py:26
  4.3 7.1 %collective-permute-start.1 = (bf16[1,8,12,128]{3,2,0,1:T(8,128)(2,1)S(1)}, bf16[1,8,12,128]{3,2,0,1:T(8,128)(2,1)S(1)}, u32[]{:S(2)}, u32[]{:S(2)}) collective-permute-start(bf16[1,8,12,128]{3,2,0,1:T(8,128)(2,1)S(1)} %get-tuple-element.129), channel_id=1, source_target_pairs={{0,4},{4,8},{8,12},{12,16},{16,20},{20,24},{24,28},{28,0},{1,5},{5... | collective-permute-start | bytes 73736 | tf_op jit(solution)/shard_map/ppermute | solution.py:14
  6.5 5.0 %collective-permute-start = (bf16[1,8,12,128]{3,2,0,1:T(8,128)(2,1)S(1)}, bf16[1,8,12,128]{3,2,0,1:T(8,128)(2,1)S(1)}, u32[]{:S(2)}, u32[]{:S(2)}) collective-permute-start(bf16[1,8,12,128]{3,2,0,1:T(8,128)(2,1)S(1)} %get-tuple-element.130), channel_id=1, source_target_pairs={{0,28},{4,0},{8,4},{12,8},{16,12},{20,16},{24,20},{28,24},{1,29},{... | collective-permute-start | bytes 73736 | tf_op jit(solution)/shard_map/ppermute | solution.py:14
  12.7 1.1 copy-start.1
  42.1 8.6 %collective-permute-start.7 = (bf16[1,16,12,128]{3,2,1,0:T(8,128)(2,1)S(1)}, bf16[1,16,12,128]{3,2,1,0:T(8,128)(2,1)S(1)}, u32[]{:S(2)}, u32[]{:S(2)}) collective-permute-start(bf16[1,16,12,128]{3,2,1,0:T(8,128)(2,1)S(1)} %get-tuple-element.45), channel_id=1, source_target_pairs={{0,1},{1,2},{2,3},{3,0},{4,5},{5,6},{6,7},{7,4},{8,9},{9,10},{10,1... | collective-permute-start | bytes 147464 | tf_op jit(solution)/shard_map/ppermute | solution.py:24
  42.1 8.5 %collective-permute-start.6 = (bf16[1,16,12,128]{3,2,1,0:T(8,128)(2,1)S(1)}, bf16[1,16,12,128]{3,2,1,0:T(8,128)(2,1)S(1)}, u32[]{:S(2)}, u32[]{:S(2)}) collective-permute-start(bf16[1,16,12,128]{3,2,1,0:T(8,128)(2,1)S(1)} %get-tuple-element.45), channel_id=1, source_target_pairs={{1,0},{2,1},{3,2},{0,3},{5,4},{6,5},{7,6},{4,7},{9,8},{10,9},{11,1... | collective-permute-start | bytes 147464 | tf_op jit(solution)/shard_map/ppermute | solution.py:26
  43.9 6.7 %collective-permute-start.5 = (bf16[1,8,12,128]{3,2,1,0:T(8,128)(2,1)S(1)}, bf16[1,8,12,128]{3,2,1,0:T(8,128)(2,1)S(1)}, u32[]{:S(2)}, u32[]{:S(2)}) collective-permute-start(bf16[1,8,12,128]{3,2,1,0:T(8,128)(2,1)S(1)} %get-tuple-element.123), channel_id=1, source_target_pairs={{0,4},{4,8},{8,12},{12,16},{16,20},{20,24},{24,28},{28,0},{1,5},{5... | collective-permute-start | bytes 73736 | tf_op jit(solution)/shard_map/ppermute | solution.py:14
  43.9 6.3 %collective-permute-start.4 = (bf16[1,8,12,128]{3,2,1,0:T(8,128)(2,1)S(1)}, bf16[1,8,12,128]{3,2,1,0:T(8,128)(2,1)S(1)}, u32[]{:S(2)}, u32[]{:S(2)}) collective-permute-start(bf16[1,8,12,128]{3,2,1,0:T(8,128)(2,1)S(1)} %get-tuple-element.124), channel_id=1, source_target_pairs={{0,28},{4,0},{8,4},{12,8},{16,12},{20,16},{24,20},{28,24},{1,29},{... | collective-permute-start | bytes 73736 | tf_op jit(solution)/shard_map/ppermute | solution.py:14
  81.1 8.6 %collective-permute-start.11 = (bf16[1,16,12,128]{3,2,1,0:T(8,128)(2,1)S(1)}, bf16[1,16,12,128]{3,2,1,0:T(8,128)(2,1)S(1)}, u32[]{:S(2)}, u32[]{:S(2)}) collective-permute-start(bf16[1,16,12,128]{3,2,1,0:T(8,128)(2,1)S(1)} %get-tuple-element.40), channel_id=1, source_target_pairs={{0,1},{1,2},{2,3},{3,0},{4,5},{5,6},{6,7},{7,4},{8,9},{9,10},{10,1... | collective-permute-start | bytes 147464 | tf_op jit(solution)/shard_map/ppermute | solution.py:24
  81.1 8.5 %collective-permute-start.10 = (bf16[1,16,12,128]{3,2,1,0:T(8,128)(2,1)S(1)}, bf16[1,16,12,128]{3,2,1,0:T(8,128)(2,1)S(1)}, u32[]{:S(2)}, u32[]{:S(2)}) collective-permute-start(bf16[1,16,12,128]{3,2,1,0:T(8,128)(2,1)S(1)} %get-tuple-element.40), channel_id=1, source_target_pairs={{1,0},{2,1},{3,2},{0,3},{5,4},{6,5},{7,6},{4,7},{9,8},{10,9},{11,1... | collective-permute-start | bytes 147464 | tf_op jit(solution)/shard_map/ppermute | solution.py:26
  82.9 6.7 %collective-permute-start.9 = (bf16[1,8,12,128]{3,2,1,0:T(8,128)(2,1)S(1)}, bf16[1,8,12,128]{3,2,1,0:T(8,128)(2,1)S(1)}, u32[]{:S(2)}, u32[]{:S(2)}) collective-permute-start(bf16[1,8,12,128]{3,2,1,0:T(8,128)(2,1)S(1)} %get-tuple-element.117), channel_id=1, source_target_pairs={{0,4},{4,8},{8,12},{12,16},{16,20},{20,24},{24,28},{28,0},{1,5},{5... | collective-permute-start | bytes 73736 | tf_op jit(solution)/shard_map/ppermute | solution.py:14
  83.0 6.3 %collective-permute-start.8 = (bf16[1,8,12,128]{3,2,1,0:T(8,128)(2,1)S(1)}, bf16[1,8,12,128]{3,2,1,0:T(8,128)(2,1)S(1)}, u32[]{:S(2)}, u32[]{:S(2)}) collective-permute-start(bf16[1,8,12,128]{3,2,1,0:T(8,128)(2,1)S(1)} %get-tuple-element.118), channel_id=1, source_target_pairs={{0,28},{4,0},{8,4},{12,8},{16,12},{20,16},{24,20},{28,24},{1,29},{... | collective-permute-start | bytes 73736 | tf_op jit(solution)/shard_map/ppermute | solution.py:14
  120.1 8.6 %collective-permute-start.15 = (bf16[1,16,12,128]{3,2,1,0:T(8,128)(2,1)S(1)}, bf16[1,16,12,128]{3,2,1,0:T(8,128)(2,1)S(1)}, u32[]{:S(2)}, u32[]{:S(2)}) collective-permute-start(bf16[1,16,12,128]{3,2,1,0:T(8,128)(2,1)S(1)} %get-tuple-element.35), channel_id=1, source_target_pairs={{0,1},{1,2},{2,3},{3,0},{4,5},{5,6},{6,7},{7,4},{8,9},{9,10},{10,1... | collective-permute-start | bytes 147464 | tf_op jit(solution)/shard_map/ppermute | solution.py:24
  120.1 8.5 %collective-permute-start.14 = (bf16[1,16,12,128]{3,2,1,0:T(8,128)(2,1)S(1)}, bf16[1,16,12,128]{3,2,1,0:T(8,128)(2,1)S(1)}, u32[]{:S(2)}, u32[]{:S(2)}) collective-permute-start(bf16[1,16,12,128]{3,2,1,0:T(8,128)(2,1)S(1)} %get-tuple-element.35), channel_id=1, source_target_pairs={{1,0},{2,1},{3,2},{0,3},{5,4},{6,5},{7,6},{4,7},{9,8},{10,9},{11,1... | collective-permute-start | bytes 147464 | tf_op jit(solution)/shard_map/ppermute | solution.py:26
  121.9 6.7 %collective-permute-start.13 = (bf16[1,8,12,128]{3,2,1,0:T(8,128)(2,1)S(1)}, bf16[1,8,12,128]{3,2,1,0:T(8,128)(2,1)S(1)}, u32[]{:S(2)}, u32[]{:S(2)}) collective-permute-start(bf16[1,8,12,128]{3,2,1,0:T(8,128)(2,1)S(1)} %get-tuple-element.111), channel_id=1, source_target_pairs={{0,4},{4,8},{8,12},{12,16},{16,20},{20,24},{24,28},{28,0},{1,5},{5... | collective-permute-start | bytes 73736 | tf_op jit(solution)/shard_map/ppermute | solution.py:14
  122.0 6.3 %collective-permute-start.12 = (bf16[1,8,12,128]{3,2,1,0:T(8,128)(2,1)S(1)}, bf16[1,8,12,128]{3,2,1,0:T(8,128)(2,1)S(1)}, u32[]{:S(2)}, u32[]{:S(2)}) collective-permute-start(bf16[1,8,12,128]{3,2,1,0:T(8,128)(2,1)S(1)} %get-tuple-element.112), channel_id=1, source_target_pairs={{0,28},{4,0},{8,4},{12,8},{16,12},{20,16},{24,20},{28,24},{1,29},{... | collective-permute-start | bytes 73736 | tf_op jit(solution)/shard_map/ppermute | solution.py:14
  159.2 1.1 copy-start.2
where the time goes:
time: 168 us
  blocking collectives  116 us (69%)
  starting transfers between devices  27.5 us (16%)
  other arithmetic  8.52 us (5%)
  waiting for transfers between devices  7.07 us (4%)
  matrix products  4.11 us (2%)
  local copies, waits for them, and re-layouts  3.32 us (2%)
    psum x4, blocking collectives, combine_sums(): return lax.psum((over_time[0], over_time[1], over_time[2]), 'wide')  87.5 us
    psum x4, blocking collectives, combine_sums(): over_time = lax.psum((local[0], local[1], local[2]), 'narrow')  22.7 us
    ppermute x8, starting transfers between devices, from_behind(): return lax.ppermute(value, axis, pairs)  19.6 us
    ppermute x4, starting transfers between devices, padded(): lax.ppermute(head, axis, [((i + 1) % count, i) for i in range(count)])  7.21 us
    ppermute x8, waiting for transfers between devices, from_behind(): return lax.ppermute(value, axis, pairs)  7.05 us
    all_gather x1, blocking collectives, per_device(): lax.all_gather(restrict(residual, restriction), 'narrow', axis=0, tiled=T...  5.6 us
  transfers between devices with their start and end apart: 16, of which 7 were waited for; matrix products, arithmetic and copies ran while one was open for 0% of the time, Pallas kernels for 0%

commit v1 on v0

v1 whole, which is shorter than its diff:
```python
import functools

import jax
import jax.numpy as jnp
from jax import lax
from jax.experimental import pallas as pl
from jax.experimental.pallas import tpu as pltpu
from jax.sharding import PartitionSpec as P

ITERS = 4
YLOC = 2
LY = 16
STEP_SCALE = 0.25
SLOT = 32
VMEM_LIMIT = 24 * 1024 * 1024


def tile_starts(rhs):
    starts = list(range(0, rhs - 7, 8))
    if rhs % 8:
        starts.append(rhs - 8)
    return starts


def load_site(ref, site, sites, rhs, by_rhs):
    tiles = []
    for start in tile_starts(rhs):
        if by_rhs:
            tiles.append(ref[pl.ds(start * sites + site, 8, stride=sites), :])
        else:
            tiles.append(ref[site * rhs + start : site * rhs + start + 8, :])
    return jnp.concatenate(tiles, 0)


def store_site(ref, site, sites, rhs, value, by_rhs):
    for at, start in enumerate(tile_starts(rhs)):
        tile = value[8 * at : 8 * at + 8]
        if by_rhs:
            ref[pl.ds(start * sites + site, 8, stride=sites), :] = tile
        else:
            ref[site * rhs + start : site * rhs + start + 8, :] = tile


def operand(block, sign):
    first = block * sign
    second = pltpu.roll(block, block.shape[-1] // 2, 1)
    highs = []
    lows = []
    for part in (first, second):
        high = part.astype(jnp.bfloat16)
        highs.append(high)
        lows.append((part - high.astype(jnp.float32)).astype(jnp.bfloat16))
    return jnp.concatenate(highs + lows, 0)


def lane_sign(width):
    lane = lax.broadcasted_iota(jnp.int32, (1, width), 1)
    return jnp.where(lane < width // 2, 1.0, -1.0).astype(jnp.float32)


def prepare(field_ref, table_ref, first_slot, sites, rhs, by_rhs):
    sign = lane_sign(field_ref.shape[-1])
    for site in range(sites):
        block = load_site(field_ref, site, sites, rhs, by_rhs)
        table_ref[first_slot + site] = operand(block, sign)


def site_product(slots, blocks):
    rows = slots[0].shape[0] // 4
    left = jnp.concatenate(slots, -1)
    right = jnp.concatenate(blocks, -1)
    total = lax.dot_general(
        left, right, (((1,), (1,)), ((), ())), preferred_element_type=jnp.float32
    )
    real_part = total[0:rows] + total[2 * rows : 3 * rows]
    imag_part = total[rows : 2 * rows] + total[3 * rows : 4 * rows]
    return jnp.concatenate([real_part, imag_part], -1) * STEP_SCALE


def columns_of(total, lanes, slot):
    summed = jnp.sum(total, axis=-1, keepdims=True)
    return jnp.where(lanes == slot, summed, 0.0)


def pair_slots(power):
    slots = []
    at = sum(2 * earlier + 1 for earlier in range(1, power))
    for other in range(power):
        slots.append((other, at, at + 1))
        at += 2
    slots.append((power, at, None))
    return slots


def gram_columns(power, refs, period):
    width = refs[0].shape[-1]
    rows = refs[0].shape[0]
    lanes = lax.broadcasted_iota(jnp.int32, (period, width), 1)
    sign = lane_sign(width)
    out = jnp.zeros((period, width), jnp.float32)
    for other, real_lane, imag_lane in pair_slots(power):
        real_sum = None
        imag_sum = None
        for base in range(0, rows, period):
            mine = refs[power][base : base + period, :]
            theirs = refs[other][base : base + period, :]
            real_term = mine * theirs
            real_sum = real_term if real_sum is None else real_sum + real_term
            if imag_lane is not None:
                turned = pltpu.roll(theirs, width // 2, 1)
                imag_term = mine * turned
                imag_sum = imag_term if imag_sum is None else imag_sum + imag_term
        out = out + columns_of(real_sum, lanes, real_lane)
        if imag_lane is not None:
            out = out + columns_of(imag_sum * sign, lanes, imag_lane)
    return out


def near_kernel(power, depth, rhs, wrap_z, *refs):
    fields = refs[: power + 1]
    hops = refs[power + 1]
    near_ref = refs[power + 2]
    table = refs[-1]
    sites = hops.shape[0]
    extent = sites // depth
    prepare(fields[power], table, 0, sites, rhs, power == 0)
    for site in range(sites):
        y, x = divmod(site, extent)
        chosen = [(0, site), (1, y * extent + (x + 1) % extent), (2, y * extent + (x - 1) % extent)]
        if y + 1 < depth:
            chosen.append((3, site + extent))
        if y > 0:
            chosen.append((4, site - extent))
        if wrap_z:
            chosen += [(5, site), (6, site)]
        value = site_product([table[at] for _, at in chosen], [hops[site, d] for d, _ in chosen])
        store_site(near_ref, site, sites, rhs, value, False)
    if power > 0:
        gram_ref = refs[power + 3]
        gram_ref[...] = gram_columns(power, fields, gram_ref.shape[0])
    else:
        start_ref = refs[3]
        for site in range(sites):
            block = load_site(fields[0], site, sites, rhs, True)
            store_site(start_ref, site, sites, rhs, block, False)


def far_kernel(depth, rhs, wrap_z, by_rhs, *refs):
    near_ref, hops, fwd_ref, back_ref, later_ref, earlier_ref = refs[:6]
    out_ref, table = refs[-2:]
    sites = hops.shape[0]
    extent = sites // depth
    ahead = 2 * sites
    behind = ahead + extent
    above = behind + extent
    below = above + sites
    prepare(later_ref, table, 0, sites, rhs, by_rhs)
    prepare(earlier_ref, table, sites, sites, rhs, by_rhs)
    prepare(fwd_ref, table, ahead, extent, rhs, by_rhs)
    prepare(back_ref, table, behind, extent, rhs, by_rhs)
    if not wrap_z:
        prepare(refs[6], table, above, sites, rhs, by_rhs)
        prepare(refs[7], table, below, sites, rhs, by_rhs)
    for site in range(sites):
        y, x = divmod(site, extent)
        chosen = [(7, site), (8, sites + site)]
        if y + 1 == depth:
            chosen.append((3, ahead + x))
        if y == 0:
            chosen.append((4, behind + x))
        if not wrap_z:
            chosen += [(5, above + site), (6, below + site)]
        value = site_product([table[at] for _, at in chosen], [hops[site, d] for d, _ in chosen])
        value = value + load_site(near_ref, site, sites, rhs, False)
        store_site(out_ref, site, sites, rhs, value, False)


def pack_kernel(rhs, *refs):
    fields = refs[: ITERS + 1]
    grams = refs[ITERS + 1 : -1]
    out_ref = refs[-1]
    period, width = grams[0].shape
    total = gram_columns(ITERS, fields, period)
    for gram in grams:
        total = total + gram[...]
    folded = total
    for turn in range(1, period // rhs):
        folded = folded + pltpu.roll(total, turn * rhs, 0)
    per_row = width // SLOT
    row = lax.broadcasted_iota(jnp.int32, (period, width), 0)
    spread = jnp.zeros((period, width), jnp.float32)
    for m in range(per_row):
        part = jnp.where(row % per_row == m, folded, 0.0)
        spread = spread + (pltpu.roll(part, SLOT * m, 1) if m else part)
    for q in range(-(-rhs // per_row)):
        summed = spread[q * per_row : q * per_row + 1]
        for m in range(1, min(per_row, rhs - q * per_row)):
            summed = summed + spread[q * per_row + m : q * per_row + m + 1]
        out_ref[q : q + 1, :] = summed


def cmulc(a, b):
    return (a[0] * b[0] + a[1] * b[1], a[0] * b[1] - a[1] * b[0])


def cmul(a, b):
    return (a[0] * b[0] - a[1] * b[1], a[0] * b[1] + a[1] * b[0])


def cadd(a, b):
    return (a[0] + b[0], a[1] + b[1])


def csub(a, b):
    return (a[0] - b[0], a[1] - b[1])


def final_kernel(depth, rhs, *refs):
    fields = refs[: ITERS + 1]
    packed, restriction = refs[ITERS + 1 : ITERS + 3]
    sol_ref, coarse_ref, res_ref, kept_ref = refs[ITERS + 3 :]
    width = fields[0].shape[-1]
    total_rows = fields[0].shape[0]
    period = rhs
    while period % 8:
        period *= 2
    per_row = width // SLOT
    row = lax.broadcasted_iota(jnp.int32, (period, width), 0) % rhs
    summed = packed[...]
    gram = jnp.zeros((period, width), jnp.float32)
    for r in range(rhs):
        q, m = divmod(r, per_row)
        line = jnp.broadcast_to(summed[q : q + 1], (period, width))
        if m:
            line = pltpu.roll(line, width - SLOT * m, 1)
        gram = jnp.where(row == r, line, gram)

    def column(lane):
        return gram[:, lane : lane + 1]

    def zero():
        return jnp.zeros((period, 1), jnp.float32)

    products = [[None] * (ITERS + 1) for _ in range(ITERS + 1)]
    for power in range(1, ITERS + 1):
        for other, real_lane, imag_lane in pair_slots(power):
            re = column(real_lane)
            im = column(imag_lane) if imag_lane is not None else None
            products[power][other] = (re, im)
            if other and imag_lane is not None:
                products[other][power] = (re, -im)

    def times(entry, value):
        if entry[1] is None:
            return (entry[0] * value[0], entry[0] * value[1])
        return cmul(entry, value)

    coeffs = [(jnp.ones((period, 1), jnp.float32), zero())]
    solution = []
    overlaps = [products[i][0] for i in range(1, ITERS + 1)]
    for step in range(ITERS):
        inner = None
        for i in range(step + 1):
            term = cmulc(coeffs[i], overlaps[i])
            inner = term if inner is None else cadd(inner, term)
        images = []
        for i in range(ITERS):
            value = None
            for j in range(step + 1):
                term = times(products[i + 1][j + 1], coeffs[j])
                value = term if value is None else cadd(value, term)
            images.append(value)
        power = None
        for i in range(step + 1):
            term = coeffs[i][0] * images[i][0] + coeffs[i][1] * images[i][1]
            power = term if power is None else power + term
        alpha = (inner[0] / power, inner[1] / power)
        overlaps = [csub(o, cmul(alpha, im)) for o, im in zip(overlaps, images)]
        scaled = [cmul(alpha, c) for c in coeffs]
        for i, value in enumerate(scaled):
            if i < len(solution):
                solution[i] = cadd(solution[i], value)
            else:
                solution.append(value)
        grown = []
        for i in range(step + 2):
            if i == 0:
                grown.append(coeffs[0])
            elif i <= step:
                grown.append(csub(coeffs[i], scaled[i - 1]))
            else:
                grown.append((-scaled[i - 1][0], -scaled[i - 1][1]))
        coeffs = grown
    sign = lane_sign(width)

    def spread(value, factor):
        real_part = jnp.broadcast_to(value[0] * factor, (period, width))
        imag_part = jnp.broadcast_to(value[1] * factor, (period, width)) * (-sign)
        return real_part, imag_part

    res_co = [spread(c, 1.0) for c in coeffs]
    sol_co = [spread(c, STEP_SCALE) for c in solution]
    for base in range(0, total_rows, period):
        res = None
        sol = None
        for i in range(ITERS + 1):
            value = fields[i][base : base + period, :]
            turned = pltpu.roll(value, width // 2, 1)
            if i == 0:
                res = value
            else:
                res = res + res_co[i][0] * value + res_co[i][1] * turned
            if i < ITERS:
                term = sol_co[i][0] * value + sol_co[i][1] * turned
                sol = term if sol is None else sol + term
        kept_ref[base : base + period, :] = sol
        res_ref[base : base + period, :] = res
    sites = restriction.shape[0]
    extent = sites // depth
    cells = extent // 2
    for cell in range(cells):
        lefts = []
        rights = []
        for y in range(depth):
            for site in (y * extent + 2 * cell, y * extent + 2 * cell + 1):
                block = load_site(res_ref, site, sites, rhs, False)
                turned = pltpu.roll(block, width // 2, 1)
                lefts.append(jnp.concatenate([block * sign, turned], 0))
                rights.append(restriction[site])
        total = lax.dot_general(
            jnp.concatenate(lefts, -1),
            jnp.concatenate(rights, -1),
            (((1,), (1,)), ((), ())),
            precision=lax.Precision.HIGHEST,
            preferred_element_type=jnp.float32,
        )
        half = total.shape[0] // 2
        value = jnp.concatenate([total[:half], total[half:]], -1)
        store_site(coarse_ref, cell, cells, rhs, value, True)
    for site in range(sites):
        store_site(sol_ref, site, sites, rhs, load_site(kept_ref, site, sites, rhs, False), True)


def vmem(count):
    return [pl.BlockSpec(memory_space=pltpu.VMEM)] * count


def call(kernel, outs, *args, scratch=(), name=None):
    single = not isinstance(outs, (list, tuple))
    return pl.pallas_call(
        kernel,
        out_shape=outs,
        in_specs=vmem(len(args)),
        out_specs=pl.BlockSpec(memory_space=pltpu.VMEM) if single else tuple(vmem(len(outs))),
        scratch_shapes=list(scratch),
        compiler_params=pltpu.CompilerParams(vmem_limit_bytes=VMEM_LIMIT),
        name=name,
    )(*args)


def per_device(right_side, hop_blocks, restriction):
    sites, rhs, width = right_side.shape[1:]
    extent = sites // YLOC
    rows_y = LY // YLOC
    wide = lax.axis_size("wide")
    narrow = lax.axis_size("narrow")
    wrap_z = wide <= rows_y
    period = rhs
    while period % 8:
        period *= 2
    tile_rows = 8 * len(tile_starts(rhs))
    total_rows = sites * rhs
    half = extent * rhs
    f32 = jnp.float32
    field_shape = jax.ShapeDtypeStruct((total_rows, width), f32)
    gram_shape = jax.ShapeDtypeStruct((period, width), f32)
    hops = hop_blocks[0]

    up_y = [(i, i // rows_y * rows_y + (i + 1) % rows_y) for i in range(wide)]
    down_y = [(b, a) for a, b in up_y]
    up_z = [(i, (i + rows_y) % wide) for i in range(wide)]
    down_z = [(b, a) for a, b in up_z]
    up_t = [(i, (i + 1) % narrow) for i in range(narrow)]
    down_t = [(b, a) for a, b in up_t]

    by_rhs = jnp.transpose(right_side[0], (1, 0, 2))
    field = by_rhs.reshape(total_rows, width)
    first_row = by_rhs[:, :extent].reshape(half, width)
    last_row = by_rhs[:, sites - extent :].reshape(half, width)
    fields = []
    grams = []
    for power in range(ITERS):
        if power:
            field = fields[power]
            first_row = field[:half]
            last_row = field[total_rows - half :]
        fwd = lax.ppermute(first_row, "wide", down_y)
        back = lax.ppermute(last_row, "wide", up_y)
        later = lax.ppermute(field, "narrow", down_t)
        earlier = lax.ppermute(field, "narrow", up_t)
        received = [fwd, back, later, earlier]
        if not wrap_z:
            received += [lax.ppermute(field, "wide", down_z), lax.ppermute(field, "wide", up_z)]
        near, other = call(
            functools.partial(near_kernel, power, YLOC, rhs, wrap_z),
            [field_shape, gram_shape if power else field_shape],
            *(fields if power else [field]),
            hops,
            scratch=[pltpu.VMEM((sites, 4 * tile_rows, width), jnp.bfloat16)],
            name=f"near{power}",
        )
        if power:
            grams.append(other)
        else:
            fields.append(other)
        slots = 2 * sites + 2 * extent + (0 if wrap_z else 2 * sites)
        fields.append(
            call(
                functools.partial(far_kernel, YLOC, rhs, wrap_z, power == 0),
                field_shape,
                near,
                hops,
                *received,
                scratch=[pltpu.VMEM((slots, 4 * tile_rows, width), jnp.bfloat16)],
                name=f"far{power}",
            )
        )
    per_row = width // SLOT
    packed_rows = -(-rhs // per_row)
    packed = call(
        functools.partial(pack_kernel, rhs),
        jax.ShapeDtypeStruct((packed_rows, width), f32),
        *fields,
        *grams,
        name="pack",
    )
    copies = jnp.broadcast_to(packed[None], (wide * narrow, packed_rows, width))
    swapped = lax.all_to_all(copies, ("wide", "narrow"), 0, 0)
    totals = jnp.sum(swapped, axis=0)
    cells = extent // 2
    solution_rows, coarse = call(
        functools.partial(final_kernel, YLOC, rhs),
        [field_shape, jax.ShapeDtypeStruct((rhs * cells, width), f32)],
        *fields,
        totals,
        restriction[0],
        scratch=[pltpu.VMEM((total_rows, width), f32), pltpu.VMEM((total_rows, width), f32)],
        name="final",
    )
    slices = lax.all_gather(coarse, "narrow", axis=0, tiled=True)
    coarse_residual = jnp.transpose(slices.reshape(narrow, rhs, cells, width), (0, 2, 1, 3))
    solution_field = jnp.transpose(solution_rows.reshape(rhs, sites, width), (1, 0, 2))
    return solution_field[None], coarse_residual


def solution(mesh):
    placed = (
        P("narrow", "wide", None, None),
        P("narrow", "wide", None, None, None),
        P("narrow", "wide", None, None),
    )
    return jax.shard_map(
        per_device,
        mesh=mesh,
        in_specs=placed,
        out_specs=(P("narrow", "wide", None, None), P(None, "wide", None, None)),
        check_vma=False,
    )
```

time: 168 us -> 65.2 us (0.39)
  blocking collectives: 116 us -> 18.8 us
  Pallas kernels: 0 us -> 8.69 us
  other arithmetic: 8.52 us -> 0.04 us
  matrix products: 4.11 us -> 0 us
  waiting for transfers between devices: 7.07 us -> 3.99 us
  local copies, waits for them, and re-layouts: 3.32 us -> 5.01 us
    psum x8 -> x0, blocking collectives: 110 us -> none  [the longest x4 87.5 us: combine_sums(): return lax.psum((over_time[0], over_time[1], over_time[2]), 'wide')]
    all_to_all x0 -> x1, blocking collectives: none -> 13.4 us  [per_device(): swapped = lax.all_to_all(copies, ('wide', 'narrow'), 0, 0)]
    pallas_call x0 -> x10, Pallas kernels: none -> 8.69 us  [call(): pl.pallas_call(kernel, out_shape=outs, in_specs=vmem(len(args)), out_spec...]
    dot_general x5 -> x0, matrix products: 4.11 us -> none  [the longest x4 3.18 us: operate(): jnp.einsum('sdak,pdsrk->psra', hop_blocks[0], paired, preferred_element_t...]
    ppermute x16, waiting for transfers between devices: 7.07 us -> 3.99 us  [the longest x4 3.96 us: per_device(): back = lax.ppermute(last_row, 'wide', up_y)]
    another operation x5 -> x0, other arithmetic: 3.04 us -> none  [the longest x4 2.91 us: operate(): paired = jnp.stack([first, second])]
    reduce_sum x13 -> x1, other arithmetic: 2.84 us -> 0.04 us  [per_device(): totals = jnp.sum(swapped, axis=0)]
    unnamed x37 -> x9, local copies, waits for them, and re-layouts: 2.92 us -> 4.14 us
  transfers between devices with their start and end apart: 16 -> 16, of which waited for: 7 -> 3; matrix products, arithmetic and copies ran while one was open for 0% -> 1% of each run, Pallas kernels for 0% -> 4%
where the time goes in v1:
time: 65.2 us; the launch traced here: 65 us
  starting transfers between devices  27.7 us (42%)
  blocking collectives  18.8 us (29%)
  Pallas kernels  8.69 us (13%)
  local copies, waits for them, and re-layouts  5.01 us (8%)
  waiting for transfers between devices  3.99 us (6%)
  between operations  0.75 us (1%)
    ppermute x4, starting transfers between devices, per_device(): fwd = lax.ppermute(first_row, 'wide', down_y)  17.4 us
    all_to_all x1, blocking collectives, per_device(): swapped = lax.all_to_all(copies, ('wide', 'narrow'), 0, 0)  13.4 us
    pallas_call x10, Pallas kernels, call(): pl.pallas_call(kernel, out_shape=outs, in_specs=vmem(len(args)), out_spec...  8.69 us
    ppermute x4, starting transfers between devices, per_device(): later = lax.ppermute(field, 'narrow', down_t)  7.21 us
    all_gather x1, blocking collectives, per_device(): slices = lax.all_gather(coarse, 'narrow', axis=0, tiled=True)  5.31 us
    unnamed x9, local copies, waits for them, and re-layouts  4.14 us
    ppermute x4, waiting for transfers between devices, per_device(): back = lax.ppermute(last_row, 'wide', up_y)  3.96 us
    ppermute x4, starting transfers between devices, per_device(): back = lax.ppermute(last_row, 'wide', up_y)  2.42 us
  transfers between devices with their start and end apart: 16, of which 3 were waited for; matrix products, arithmetic and copies ran while one was open for 1% of the time, Pallas kernels for 4%

profile of v1, /device:TPU:0, one launch (start us, length us, event | category | flops | bytes accessed | tf_op | source)
XLA Modules:
  0.0 65.0 jit_solution(13929847793644763128)
XLA Ops:
  0.6 0.5 collective-permute-start.3
  1.2 2.0 %collective-permute-start.2 = (f32[192,128]{1,0:T(8,128)}, f32[192,128]{1,0:T(8,128)S(1)}, u32[]{:S(2)}, u32[]{:S(2)}) collective-permute-start(f32[192,128]{1,0:T(8,128)} %bitcast.29), channel_id=1, source_target_pairs={{1,0},{2,1},{3,2},{0,3},{5,4},{6,5},{7,6},{4,7},{9,8},{10,9},{11,1... | collective-permute-start | bytes 294920 | tf_op jit(solution)/shard_map/ppermute | solution.py:399
  3.2 0.8 %slice_bitcast_fusion = (f32[96,128]{1,0:T(8,128)S(1)}, f32[96,128]{1,0:T(8,128)S(1)}) fusion(f32[12,16,128]{2,1,0:T(8,128)} %bitcast.30), kind=kLoop, calls=%fused_computation | loop fusion | bytes 196608 | tf_op jit(solution)/shard_map/reshape | solution.py:389
  4.0 2.3 %collective-permute-start.1 = (f32[96,128]{1,0:T(8,128)S(1)}, f32[96,128]{1,0:T(8,128)S(1)}, u32[]{:S(2)}, u32[]{:S(2)}) collective-permute-start(f32[96,128]{1,0:T(8,128)S(1)} %get-tuple-element.28), channel_id=1, source_target_pairs={{0,4},{4,8},{8,12},{12,16},{16,20},{20,24},{24,28},{28,0},{1,5},{5... | collective-permute-start | bytes 147464 | tf_op jit(solution)/shard_map/ppermute | solution.py:398
  6.3 3.1 %collective-permute-start = (f32[96,128]{1,0:T(8,128)S(1)}, f32[96,128]{1,0:T(8,128)S(1)}, u32[]{:S(2)}, u32[]{:S(2)}) collective-permute-start(f32[96,128]{1,0:T(8,128)S(1)} %get-tuple-element.29), channel_id=1, source_target_pairs={{4,0},{8,4},{12,8},{16,12},{20,16},{24,20},{28,24},{0,28},{5,1},{9... | collective-permute-start | bytes 147464 | tf_op jit(solution)/shard_map/ppermute | solution.py:397
  9.4 0.0 copy-start
  9.4 1.7 %copy-done = bf16[1,16,9,64,128]{4,3,2,1,0:T(8,128)(2,1)S(1)} copy-done((bf16[1,16,9,64,128]{4,3,2,1,0:T(8,128)(2,1)S(1)}, bf16[1,16,9,64,128]{4,3,2,1,0:T(8,128)(2,1)}, u32[]{:S(2)}) %copy-start) | copy-done | bytes 2359320
  11.1 0.0 copy-start.3
  11.1 0.9 %copy-done.3 = f32[1,16,12,128]{3,1,2,0:T(8,128)S(1)} copy-done((f32[1,16,12,128]{3,1,2,0:T(8,128)S(1)}, f32[1,16,12,128]{3,1,2,0:T(8,128)}, u32[]{:S(2)}) %copy-start.3) | copy-done | bytes 98328
  12.0 0.0 copy-start.1
  12.0 0.7 %near0.1 = (f32[192,128]{1,0:T(8,128)S(1)}, f32[192,128]{1,0:T(8,128)S(1)}) custom-call(f32[192,128]{1,0:T(8,128)S(1)} %bitcast.31, bf16[16,9,64,128]{3,2,1,0:T(8,128)(2,1)S(1)} %bitcast.19), custom_call_target="tpu_custom_call" | custom-call | tf_op jit(solution)/shard_map/near0/pallas_call | solution.py:350
  12.7 0.0 collective-permute-done.1.refs_3_
  12.7 0.0 collective-permute-done.refs_2_
  12.7 0.0 collective-permute-done.3.refs_5_
  12.7 0.0 collective-permute-done.2.refs_4_
  12.7 0.9 %copy-done.1 = bf16[1,16,9,64,128]{4,3,2,1,0:T(8,128)(2,1)S(1)} copy-done((bf16[1,16,9,64,128]{4,3,2,1,0:T(8,128)(2,1)S(1)}, bf16[1,16,9,64,128]{4,3,2,1,0:T(8,128)(2,1)}, u32[]{:S(2)}) %copy-start.1) | copy-done | bytes 2359320
  13.6 0.6 far0.1.refs_1_
  14.2 0.0 collective-permute-start.7
  14.2 1.7 %collective-permute-start.6 = (f32[192,128]{1,0:T(8,128)S(1)}, f32[192,128]{1,0:T(8,128)S(1)}, u32[]{:S(2)}, u32[]{:S(2)}) collective-permute-start(f32[192,128]{1,0:T(8,128)S(1)} %far0.1.refs_1_), channel_id=1, source_target_pairs={{1,0},{2,1},{3,2},{0,3},{5,4},{6,5},{7,6},{4,7},{9,8},{10,9},{11,1... | collective-permute-start | bytes 294920 | tf_op jit(solution)/shard_map/ppermute | solution.py:399
  16.0 0.1 collective-permute-start.5
  16.0 4.7 %collective-permute-start.4 = (f32[96,128]{1,0:T(8,128)S(1)}, f32[96,128]{1,0:T(8,128)S(1)}, u32[]{:S(2)}, u32[]{:S(2)}) collective-permute-start(f32[96,128]{1,0:T(8,128)S(1)} %get-tuple-element.27), channel_id=1, source_target_pairs={{4,0},{8,4},{12,8},{16,12},{20,16},{24,20},{28,24},{0,28},{5,1},{9... | collective-permute-start | bytes 147464 | tf_op jit(solution)/shard_map/ppermute | solution.py:397
  20.7 0.7 %near1.1 = (f32[192,128]{1,0:T(8,128)S(1)}, f32[24,128]{1,0:T(8,128)S(1)}) custom-call(f32[192,128]{1,0:T(8,128)S(1)} %get-tuple-element.12.refs_0_, f32[192,128]{1,0:T(8,128)S(1)} %far0.1.refs_1_, bf16[16,9,64,128]{3,2,1,0:T(8,128)(2,1)S(1)} %bitcast.21), custom_call_target="tpu_custom_call" | custom-call | tf_op jit(solution)/shard_map/near1/pallas_call | solution.py:350
  21.4 1.4 %collective-permute-done.5.refs_3_ = f32[96,128]{1,0:T(8,128)S(1)} collective-permute-done((f32[96,128]{1,0:T(8,128)S(1)}, f32[96,128]{1,0:T(8,128)S(1)}, u32[]{:S(2)}, u32[]{:S(2)}) %collective-permute-start.5) | collective-permute-done | bytes 49184 | tf_op jit(solution)/shard_map/ppermute | solution.py:398
  22.8 0.0 collective-permute-done.4.refs_2_
  22.8 0.0 collective-permute-done.7.refs_5_
  22.8 0.0 collective-permute-done.6.refs_4_
  22.8 0.6 far1.1.refs_2_
  23.4 0.0 collective-permute-start.11
  23.4 1.7 %collective-permute-start.10 = (f32[192,128]{1,0:T(8,128)S(1)}, f32[192,128]{1,0:T(8,128)S(1)}, u32[]{:S(2)}, u32[]{:S(2)}) collective-permute-start(f32[192,128]{1,0:T(8,128)S(1)} %far1.1.refs_2_), channel_id=1, source_target_pairs={{1,0},{2,1},{3,2},{0,3},{5,4},{6,5},{7,6},{4,7},{9,8},{10,9},{11,1... | collective-permute-start | bytes 294920 | tf_op jit(solution)/shard_map/ppermute | solution.py:399
  25.2 0.1 collective-permute-start.9
  25.2 4.8 %collective-permute-start.8 = (f32[96,128]{1,0:T(8,128)S(1)}, f32[96,128]{1,0:T(8,128)S(1)}, u32[]{:S(2)}, u32[]{:S(2)}) collective-permute-start(f32[96,128]{1,0:T(8,128)S(1)} %get-tuple-element.25), channel_id=1, source_target_pairs={{4,0},{8,4},{12,8},{16,12},{20,16},{24,20},{28,24},{0,28},{5,1},{9... | collective-permute-start | bytes 147464 | tf_op jit(solution)/shard_map/ppermute | solution.py:397
  30.0 0.7 %near2.1 = (f32[192,128]{1,0:T(8,128)S(1)}, f32[24,128]{1,0:T(8,128)S(1)}) custom-call(f32[192,128]{1,0:T(8,128)S(1)} %get-tuple-element.12.refs_0_, f32[192,128]{1,0:T(8,128)S(1)} %far0.1.refs_1_, f32[192,128]{1,0:T(8,128)S(1)} %far1.1.refs_2_, bf16[16,9,64,128]{3,2,1,0:T(8,128)(2,1)S(1)} %bitcast.23), custom_call_target="tpu_custom_call" | custom-call | tf_op jit(solution)/shard_map/near2/pallas_call | solution.py:350
  30.7 1.3 %collective-permute-done.9.refs_3_ = f32[96,128]{1,0:T(8,128)S(1)} collective-permute-done((f32[96,128]{1,0:T(8,128)S(1)}, f32[96,128]{1,0:T(8,128)S(1)}, u32[]{:S(2)}, u32[]{:S(2)}) %collective-permute-start.9) | collective-permute-done | bytes 49184 | tf_op jit(solution)/shard_map/ppermute | solution.py:398
  32.0 0.0 collective-permute-done.8.refs_2_
  32.0 0.0 collective-permute-done.11.refs_5_
  32.0 0.0 collective-permute-done.10.refs_4_
  32.0 0.6 far2.1.refs_3_
  32.6 0.0 collective-permute-start.15
  32.6 1.7 %collective-permute-start.14 = (f32[192,128]{1,0:T(8,128)S(1)}, f32[192,128]{1,0:T(8,128)S(1)}, u32[]{:S(2)}, u32[]{:S(2)}) collective-permute-start(f32[192,128]{1,0:T(8,128)S(1)} %far2.1.refs_3_), channel_id=1, source_target_pairs={{1,0},{2,1},{3,2},{0,3},{5,4},{6,5},{7,6},{4,7},{9,8},{10,9},{11,1... | collective-permute-start | bytes 294920 | tf_op jit(solution)/shard_map/ppermute | solution.py:399
  34.4 0.1 collective-permute-start.13
  34.4 4.8 %collective-permute-start.12 = (f32[96,128]{1,0:T(8,128)S(1)}, f32[96,128]{1,0:T(8,128)S(1)}, u32[]{:S(2)}, u32[]{:S(2)}) collective-permute-start(f32[96,128]{1,0:T(8,128)S(1)} %get-tuple-element.23), channel_id=1, source_target_pairs={{4,0},{8,4},{12,8},{16,12},{20,16},{24,20},{28,24},{0,28},{5,1},{9... | collective-permute-start | bytes 147464 | tf_op jit(solution)/shard_map/ppermute | solution.py:397
  39.3 0.7 %near3.1 = (f32[192,128]{1,0:T(8,128)S(1)}, f32[24,128]{1,0:T(8,128)S(1)}) custom-call(f32[192,128]{1,0:T(8,128)S(1)} %get-tuple-element.12.refs_0_, f32[192,128]{1,0:T(8,128)S(1)} %far0.1.refs_1_, f32[192,128]{1,0:T(8,128)S(1)} %far1.1.refs_2_, f32[192,128]{1,0:T(8,128)S(1)} %far2.1.refs_3_, bf16[16,9,64,128]{3,2,1,0:T(8,128)(2,1)S(1)} %bitcast.25), custom_call_target="tpu_custom_call" | custom-call | tf_op jit(solution)/shard_map/near3/pallas_call | solution.py:350
  40.0 0.0 copy-start.2
  40.0 1.3 %collective-permute-done.13.refs_3_ = f32[96,128]{1,0:T(8,128)S(1)} collective-permute-done((f32[96,128]{1,0:T(8,128)S(1)}, f32[96,128]{1,0:T(8,128)S(1)}, u32[]{:S(2)}, u32[]{:S(2)}) %collective-permute-start.13) | collective-permute-done | bytes 49184 | tf_op jit(solution)/shard_map/ppermute | solution.py:398
  41.3 0.0 collective-permute-done.12.refs_2_
  41.3 0.0 collective-permute-done.15.refs_5_
  41.3 0.0 collective-permute-done.14.refs_4_
  41.3 0.6 far3.1.refs_4_
  41.8 0.4 pack.1
  42.2 13.4 %all_to_all.5 = f32[32,3,128]{2,1,0:T(4,128)S(1)} all-to-all(f32[32,3,128]{2,1,0:T(4,128)S(1)} %broadcast_in_dim.4), channel_id=1, replica_groups=mesh['wide'=8,'narrow'=4] {'wide','narrow'}, dimensions={0} | all-to-all | bytes 98304 | tf_op jit(solution)/shard_map/all_to_all | solution.py:438
  55.7 0.0 copy-done.2
  55.7 3.3 %final.1 = (f32[192,128]{1,0:T(8,128)}, f32[48,128]{1,0:T(8,128)S(1)}) custom-call(f32[192,128]{1,0:T(8,128)S(1)} %get-tuple-element.12.refs_0_, f32[192,128]{1,0:T(8,128)S(1)} %far0.1.refs_1_, f32[192,128]{1,0:T(8,128)S(1)} %far1.1.refs_2_, f32[192,128]{1,0:T(8,128)S(1)} %far2.1.refs_3_, f32[192,128]{1,0:T(8,128)S(1)} %far3.1.refs_4_, ...), custom_call_target="tpu_custom_call" | custom-call | tf_op jit(solution)/shard_map/final/pallas_call | solution.py:350
  59.0 5.3 %all_gather.3 = f32[192,128]{1,0:T(8,128)S(1)} all-gather(f32[48,128]{1,0:T(8,128)S(1)} %get-tuple-element.21), channel_id=1, replica_groups=mesh['wide'=8,'narrow'=4] {'narrow'}, dimensions={0}, use_global_device_ids=true | all-gather | bytes 122880 | tf_op jit(solution)/shard_map/all_gather | solution.py:450
  64.3 0.6 copy.8
  (5 shorter events, 0.1 us)
Async XLA Ops:
  0.6 12.0 %collective-permute-start.3 = (f32[192,128]{1,0:T(8,128)}, f32[192,128]{1,0:T(8,128)S(1)}, u32[]{:S(2)}, u32[]{:S(2)}) collective-permute-start(f32[192,128]{1,0:T(8,128)} %bitcast.28), channel_id=1, source_target_pairs={{0,1},{1,2},{2,3},{3,0},{4,5},{5,6},{6,7},{7,4},{8,9},{9,10},{10,1... | collective-permute-start | bytes 294920 | tf_op jit(solution)/shard_map/ppermute | solution.py:400
  1.2 11.5 %collective-permute-start.2 = (f32[192,128]{1,0:T(8,128)}, f32[192,128]{1,0:T(8,128)S(1)}, u32[]{:S(2)}, u32[]{:S(2)}) collective-permute-start(f32[192,128]{1,0:T(8,128)} %bitcast.29), channel_id=1, source_target_pairs={{1,0},{2,1},{3,2},{0,3},{5,4},{6,5},{7,6},{4,7},{9,8},{10,9},{11,1... | collective-permute-start | bytes 294920 | tf_op jit(solution)/shard_map/ppermute | solution.py:399
  4.0 8.6 %collective-permute-start.1 = (f32[96,128]{1,0:T(8,128)S(1)}, f32[96,128]{1,0:T(8,128)S(1)}, u32[]{:S(2)}, u32[]{:S(2)}) collective-permute-start(f32[96,128]{1,0:T(8,128)S(1)} %get-tuple-element.28), channel_id=1, source_target_pairs={{0,4},{4,8},{8,12},{12,16},{16,20},{20,24},{24,28},{28,0},{1,5},{5... | collective-permute-start | bytes 147464 | tf_op jit(solution)/shard_map/ppermute | solution.py:398
  6.3 6.4 %collective-permute-start = (f32[96,128]{1,0:T(8,128)S(1)}, f32[96,128]{1,0:T(8,128)S(1)}, u32[]{:S(2)}, u32[]{:S(2)}) collective-permute-start(f32[96,128]{1,0:T(8,128)S(1)} %get-tuple-element.29), channel_id=1, source_target_pairs={{4,0},{8,4},{12,8},{16,12},{20,16},{24,20},{28,24},{0,28},{5,1},{9... | collective-permute-start | bytes 147464 | tf_op jit(solution)/shard_map/ppermute | solution.py:397
  9.4 1.7 %copy-start = (bf16[1,16,9,64,128]{4,3,2,1,0:T(8,128)(2,1)S(1)}, bf16[1,16,9,64,128]{4,3,2,1,0:T(8,128)(2,1)}, u32[]{:S(2)}) copy-start(bf16[1,16,9,64,128]{4,3,2,1,0:T(8,128)(2,1)} %param.4) | copy-start | bytes 7077892
  11.1 0.9 %copy-start.3 = (f32[1,16,12,128]{3,1,2,0:T(8,128)S(1)}, f32[1,16,12,128]{3,1,2,0:T(8,128)}, u32[]{:S(2)}) copy-start(f32[1,16,12,128]{3,1,2,0:T(8,128)} %param.3) | copy-start | bytes 294916
  12.0 1.7 %copy-start.1 = (bf16[1,16,9,64,128]{4,3,2,1,0:T(8,128)(2,1)S(1)}, bf16[1,16,9,64,128]{4,3,2,1,0:T(8,128)(2,1)}, u32[]{:S(2)}) copy-start(bf16[1,16,9,64,128]{4,3,2,1,0:T(8,128)(2,1)} %param.4) | copy-start | bytes 7077892
  14.2 8.6 %collective-permute-start.7 = (f32[192,128]{1,0:T(8,128)S(1)}, f32[192,128]{1,0:T(8,128)S(1)}, u32[]{:S(2)}, u32[]{:S(2)}) collective-permute-start(f32[192,128]{1,0:T(8,128)S(1)} %far0.1.refs_1_), channel_id=1, source_target_pairs={{0,1},{1,2},{2,3},{3,0},{4,5},{5,6},{6,7},{7,4},{8,9},{9,10},{10,1... | collective-permute-start | bytes 294920 | tf_op jit(solution)/shard_map/ppermute | solution.py:400
  14.2 8.6 %collective-permute-start.6 = (f32[192,128]{1,0:T(8,128)S(1)}, f32[192,128]{1,0:T(8,128)S(1)}, u32[]{:S(2)}, u32[]{:S(2)}) collective-permute-start(f32[192,128]{1,0:T(8,128)S(1)} %far0.1.refs_1_), channel_id=1, source_target_pairs={{1,0},{2,1},{3,2},{0,3},{5,4},{6,5},{7,6},{4,7},{9,8},{10,9},{11,1... | collective-permute-start | bytes 294920 | tf_op jit(solution)/shard_map/ppermute | solution.py:399
  16.0 6.8 %collective-permute-start.5 = (f32[96,128]{1,0:T(8,128)S(1)}, f32[96,128]{1,0:T(8,128)S(1)}, u32[]{:S(2)}, u32[]{:S(2)}) collective-permute-start(f32[96,128]{1,0:T(8,128)S(1)} %get-tuple-element.26), channel_id=1, source_target_pairs={{0,4},{4,8},{8,12},{12,16},{16,20},{20,24},{24,28},{28,0},{1,5},{5... | collective-permute-start | bytes 147464 | tf_op jit(solution)/shard_map/ppermute | solution.py:398
  16.0 6.8 %collective-permute-start.4 = (f32[96,128]{1,0:T(8,128)S(1)}, f32[96,128]{1,0:T(8,128)S(1)}, u32[]{:S(2)}, u32[]{:S(2)}) collective-permute-start(f32[96,128]{1,0:T(8,128)S(1)} %get-tuple-element.27), channel_id=1, source_target_pairs={{4,0},{8,4},{12,8},{16,12},{20,16},{24,20},{28,24},{0,28},{5,1},{9... | collective-permute-start | bytes 147464 | tf_op jit(solution)/shard_map/ppermute | solution.py:397
  23.4 8.6 %collective-permute-start.11 = (f32[192,128]{1,0:T(8,128)S(1)}, f32[192,128]{1,0:T(8,128)S(1)}, u32[]{:S(2)}, u32[]{:S(2)}) collective-permute-start(f32[192,128]{1,0:T(8,128)S(1)} %far1.1.refs_2_), channel_id=1, source_target_pairs={{0,1},{1,2},{2,3},{3,0},{4,5},{5,6},{6,7},{7,4},{8,9},{9,10},{10,1... | collective-permute-start | bytes 294920 | tf_op jit(solution)/shard_map/ppermute | solution.py:400
  23.4 8.6 %collective-permute-start.10 = (f32[192,128]{1,0:T(8,128)S(1)}, f32[192,128]{1,0:T(8,128)S(1)}, u32[]{:S(2)}, u32[]{:S(2)}) collective-permute-start(f32[192,128]{1,0:T(8,128)S(1)} %far1.1.refs_2_), channel_id=1, source_target_pairs={{1,0},{2,1},{3,2},{0,3},{5,4},{6,5},{7,6},{4,7},{9,8},{10,9},{11,1... | collective-permute-start | bytes 294920 | tf_op jit(solution)/shard_map/ppermute | solution.py:399
  25.2 6.8 %collective-permute-start.9 = (f32[96,128]{1,0:T(8,128)S(1)}, f32[96,128]{1,0:T(8,128)S(1)}, u32[]{:S(2)}, u32[]{:S(2)}) collective-permute-start(f32[96,128]{1,0:T(8,128)S(1)} %get-tuple-element.24), channel_id=1, source_target_pairs={{0,4},{4,8},{8,12},{12,16},{16,20},{20,24},{24,28},{28,0},{1,5},{5... | collective-permute-start | bytes 147464 | tf_op jit(solution)/shard_map/ppermute | solution.py:398
  25.2 6.8 %collective-permute-start.8 = (f32[96,128]{1,0:T(8,128)S(1)}, f32[96,128]{1,0:T(8,128)S(1)}, u32[]{:S(2)}, u32[]{:S(2)}) collective-permute-start(f32[96,128]{1,0:T(8,128)S(1)} %get-tuple-element.25), channel_id=1, source_target_pairs={{4,0},{8,4},{12,8},{16,12},{20,16},{24,20},{28,24},{0,28},{5,1},{9... | collective-permute-start | bytes 147464 | tf_op jit(solution)/shard_map/ppermute | solution.py:397
  32.6 8.7 %collective-permute-start.15 = (f32[192,128]{1,0:T(8,128)S(1)}, f32[192,128]{1,0:T(8,128)S(1)}, u32[]{:S(2)}, u32[]{:S(2)}) collective-permute-start(f32[192,128]{1,0:T(8,128)S(1)} %far2.1.refs_3_), channel_id=1, source_target_pairs={{0,1},{1,2},{2,3},{3,0},{4,5},{5,6},{6,7},{7,4},{8,9},{9,10},{10,1... | collective-permute-start | bytes 294920 | tf_op jit(solution)/shard_map/ppermute | solution.py:400
  32.6 8.6 %collective-permute-start.14 = (f32[192,128]{1,0:T(8,128)S(1)}, f32[192,128]{1,0:T(8,128)S(1)}, u32[]{:S(2)}, u32[]{:S(2)}) collective-permute-start(f32[192,128]{1,0:T(8,128)S(1)} %far2.1.refs_3_), channel_id=1, source_target_pairs={{1,0},{2,1},{3,2},{0,3},{5,4},{6,5},{7,6},{4,7},{9,8},{10,9},{11,1... | collective-permute-start | bytes 294920 | tf_op jit(solution)/shard_map/ppermute | solution.py:399
  34.4 6.9 %collective-permute-start.13 = (f32[96,128]{1,0:T(8,128)S(1)}, f32[96,128]{1,0:T(8,128)S(1)}, u32[]{:S(2)}, u32[]{:S(2)}) collective-permute-start(f32[96,128]{1,0:T(8,128)S(1)} %get-tuple-element.22), channel_id=1, source_target_pairs={{0,4},{4,8},{8,12},{12,16},{16,20},{20,24},{24,28},{28,0},{1,5},{5... | collective-permute-start | bytes 147464 | tf_op jit(solution)/shard_map/ppermute | solution.py:398
  34.4 6.8 %collective-permute-start.12 = (f32[96,128]{1,0:T(8,128)S(1)}, f32[96,128]{1,0:T(8,128)S(1)}, u32[]{:S(2)}, u32[]{:S(2)}) collective-permute-start(f32[96,128]{1,0:T(8,128)S(1)} %get-tuple-element.23), channel_id=1, source_target_pairs={{4,0},{8,4},{12,8},{16,12},{20,16},{24,20},{28,24},{0,28},{5,1},{9... | collective-permute-start | bytes 147464 | tf_op jit(solution)/shard_map/ppermute | solution.py:397
  40.0 15.8 %copy-start.2 = (f32[1,16,64,128]{3,2,1,0:T(8,128)S(1)}, f32[1,16,64,128]{3,2,1,0:T(8,128)}, u32[]{:S(2)}) copy-start(f32[1,16,64,128]{3,2,1,0:T(8,128)} %param.5) | copy-start | bytes 1572868

commit v2 on v1

--- a/solution.py
+++ b/solution.py
@@ -7,10 +7,12 @@
 from jax.experimental.pallas import tpu as pltpu
 from jax.sharding import PartitionSpec as P
 
+
 ITERS = 4
 YLOC = 2
 LY = 16
 STEP_SCALE = 0.25
+LANES_EACH = 8
 SLOT = 32
 VMEM_LIMIT = 24 * 1024 * 1024
 
@@ -62,6 +64,17 @@
     sign = lane_sign(field_ref.shape[-1])
     for site in range(sites):
         block = load_site(field_ref, site, sites, rhs, by_rhs)
+        table_ref[first_slot + site] = operand(block, sign)
+
+
+def prepare_pair(odd, even_ref, odd_ref, table_ref, first_slot, sites, rhs, by_rhs):
+    sign = lane_sign(even_ref.shape[-1])
+    for site in range(sites):
+        block = jnp.where(
+            odd,
+            load_site(odd_ref, site, sites, rhs, by_rhs),
+            load_site(even_ref, site, sites, rhs, by_rhs),
+        )
         table_ref[first_slot + site] = operand(block, sign)
 
 
@@ -116,15 +129,11 @@
     return out
 
 
-def near_kernel(power, depth, rhs, wrap_z, *refs):
-    fields = refs[: power + 1]
-    hops = refs[power + 1]
-    near_ref = refs[power + 2]
-    table = refs[-1]
-    sites = hops.shape[0]
+def near_sites(hops_ref, table, near_ref, depth, rhs, wrap_z, ready):
+    sites = hops_ref.shape[1]
     extent = sites // depth
-    prepare(fields[power], table, 0, sites, rhs, power == 0)
     for site in range(sites):
+        ready(site)
         y, x = divmod(site, extent)
         chosen = [(0, site), (1, y * extent + (x + 1) % extent), (2, y * extent + (x - 1) % extent)]
         if y + 1 < depth:
@@ -133,52 +142,76 @@
             chosen.append((4, site - extent))
         if wrap_z:
             chosen += [(5, site), (6, site)]
-        value = site_product([table[at] for _, at in chosen], [hops[site, d] for d, _ in chosen])
+        value = site_product(
+            [table[at] for _, at in chosen], [hops_ref[0, site, d] for d, _ in chosen]
+        )
         store_site(near_ref, site, sites, rhs, value, False)
-    if power > 0:
-        gram_ref = refs[power + 3]
-        gram_ref[...] = gram_columns(power, fields, gram_ref.shape[0])
-    else:
-        start_ref = refs[3]
-        for site in range(sites):
-            block = load_site(fields[0], site, sites, rhs, True)
-            store_site(start_ref, site, sites, rhs, block, False)
-
-
-def far_kernel(depth, rhs, wrap_z, by_rhs, *refs):
-    near_ref, hops, fwd_ref, back_ref, later_ref, earlier_ref = refs[:6]
-    out_ref, table = refs[-2:]
-    sites = hops.shape[0]
+
+
+def first_near_kernel(depth, rhs, wrap_z, field_hbm, hops_hbm, near_ref, start_ref, hops_ref, table, field_ref, field_sem, hops_sem):
+    sites = hops_hbm.shape[1]
+    field_copy = pltpu.make_async_copy(field_hbm, field_ref, field_sem)
+    field_copy.start()
+    copies = [
+        pltpu.make_async_copy(hops_hbm.at[0, site], hops_ref.at[0, site], hops_sem.at[site])
+        for site in range(sites)
+    ]
+    for copy in copies:
+        copy.start()
+    field_copy.wait()
+    prepare(field_ref, table, 0, sites, rhs, True)
+    for site in range(sites):
+        store_site(start_ref, site, sites, rhs, load_site(field_ref, site, sites, rhs, True), False)
+    near_sites(hops_ref, table, near_ref, depth, rhs, wrap_z, lambda site: copies[site].wait())
+
+
+def near_kernel(power, depth, rhs, wrap_z, *refs):
+    fields = refs[: power + 1]
+    hops_ref, near_ref, gram_ref, table = refs[power + 1 :]
+    prepare(fields[power], table, 0, hops_ref.shape[1], rhs, False)
+    near_sites(hops_ref, table, near_ref, depth, rhs, wrap_z, lambda site: None)
+    gram_ref[...] = gram_columns(power, fields, gram_ref.shape[0])
+
+
+def far_kernel(depth, rhs, wrap_z, by_rhs, last, *refs):
+    near_ref, hops, side_a, side_b, time_a, time_b = refs[:6]
+    table = refs[-1]
+    extra = refs[6:-1]
+    sites = hops.shape[1]
     extent = sites // depth
     ahead = 2 * sites
     behind = ahead + extent
     above = behind + extent
     below = above + sites
-    prepare(later_ref, table, 0, sites, rhs, by_rhs)
-    prepare(earlier_ref, table, sites, sites, rhs, by_rhs)
-    prepare(fwd_ref, table, ahead, extent, rhs, by_rhs)
-    prepare(back_ref, table, behind, extent, rhs, by_rhs)
+    odd_row = lax.rem(lax.axis_index("wide"), 2) == 1
+    odd_time = lax.rem(lax.axis_index("narrow"), 2)
+    prepare_pair(odd_row, side_a, side_b, table, ahead, extent, rhs, by_rhs)
+    prepare_pair(odd_row, side_b, side_a, table, behind, extent, rhs, by_rhs)
+    prepare(time_a, table, 0, sites, rhs, by_rhs)
+    prepare(time_b, table, sites, sites, rhs, by_rhs)
     if not wrap_z:
-        prepare(refs[6], table, above, sites, rhs, by_rhs)
-        prepare(refs[7], table, below, sites, rhs, by_rhs)
+        prepare(extra[0], table, above, sites, rhs, by_rhs)
+        prepare(extra[1], table, below, sites, rhs, by_rhs)
+        extra = extra[2:]
+    out_ref = extra[ITERS * 2 - 1] if last else extra[0]
     for site in range(sites):
         y, x = divmod(site, extent)
-        chosen = [(7, site), (8, sites + site)]
+        chosen = [(7 + odd_time, site), (8 - odd_time, sites + site)]
         if y + 1 == depth:
             chosen.append((3, ahead + x))
         if y == 0:
             chosen.append((4, behind + x))
         if not wrap_z:
             chosen += [(5, above + site), (6, below + site)]
-        value = site_product([table[at] for _, at in chosen], [hops[site, d] for d, _ in chosen])
+        value = site_product([table[at] for _, at in chosen], [hops[0, site, d] for d, _ in chosen])
         value = value + load_site(near_ref, site, sites, rhs, False)
         store_site(out_ref, site, sites, rhs, value, False)
-
-
-def pack_kernel(rhs, *refs):
-    fields = refs[: ITERS + 1]
-    grams = refs[ITERS + 1 : -1]
-    out_ref = refs[-1]
+    if last:
+        fields = list(extra[:ITERS]) + [out_ref]
+        pack(rhs, fields, extra[ITERS : 2 * ITERS - 1], extra[2 * ITERS])
+
+
+def pack(rhs, fields, grams, out_ref):
     period, width = grams[0].shape
     total = gram_columns(ITERS, fields, period)
     for gram in grams:
@@ -215,48 +248,16 @@
     return (a[0] - b[0], a[1] - b[1])
 
 
-def final_kernel(depth, rhs, *refs):
-    fields = refs[: ITERS + 1]
-    packed, restriction = refs[ITERS + 1 : ITERS + 3]
-    sol_ref, coarse_ref, res_ref, kept_ref = refs[ITERS + 3 :]
-    width = fields[0].shape[-1]
-    total_rows = fields[0].shape[0]
-    period = rhs
-    while period % 8:
-        period *= 2
-    per_row = width // SLOT
-    row = lax.broadcasted_iota(jnp.int32, (period, width), 0) % rhs
-    summed = packed[...]
-    gram = jnp.zeros((period, width), jnp.float32)
-    for r in range(rhs):
-        q, m = divmod(r, per_row)
-        line = jnp.broadcast_to(summed[q : q + 1], (period, width))
-        if m:
-            line = pltpu.roll(line, width - SLOT * m, 1)
-        gram = jnp.where(row == r, line, gram)
-
-    def column(lane):
-        return gram[:, lane : lane + 1]
-
-    def zero():
-        return jnp.zeros((period, 1), jnp.float32)
-
-    products = [[None] * (ITERS + 1) for _ in range(ITERS + 1)]
-    for power in range(1, ITERS + 1):
-        for other, real_lane, imag_lane in pair_slots(power):
-            re = column(real_lane)
-            im = column(imag_lane) if imag_lane is not None else None
-            products[power][other] = (re, im)
-            if other and imag_lane is not None:
-                products[other][power] = (re, -im)
+def step_coefficients(products):
+    one = jnp.ones_like(products[1][0][0])
 
     def times(entry, value):
         if entry[1] is None:
             return (entry[0] * value[0], entry[0] * value[1])
         return cmul(entry, value)
 
-    coeffs = [(jnp.ones((period, 1), jnp.float32), zero())]
-    solution = []
+    coeffs = [(one, jnp.zeros_like(one))]
+    combined = []
     overlaps = [products[i][0] for i in range(1, ITERS + 1)]
     for step in range(ITERS):
         inner = None
@@ -278,43 +279,89 @@
         overlaps = [csub(o, cmul(alpha, im)) for o, im in zip(overlaps, images)]
         scaled = [cmul(alpha, c) for c in coeffs]
         for i, value in enumerate(scaled):
-            if i < len(solution):
-                solution[i] = cadd(solution[i], value)
+            if i < len(combined):
+                combined[i] = cadd(combined[i], value)
             else:
-                solution.append(value)
-        grown = []
-        for i in range(step + 2):
-            if i == 0:
-                grown.append(coeffs[0])
-            elif i <= step:
-                grown.append(csub(coeffs[i], scaled[i - 1]))
-            else:
-                grown.append((-scaled[i - 1][0], -scaled[i - 1][1]))
+                combined.append(value)
+        grown = [coeffs[0]]
+        for i in range(1, step + 1):
+            grown.append(csub(coeffs[i], scaled[i - 1]))
+        grown.append((-scaled[step][0], -scaled[step][1]))
         coeffs = grown
+    return coeffs, combined
+
+
+def final_kernel(depth, rhs, *refs):
+    fields = refs[: ITERS + 1]
+    packed, restriction = refs[ITERS + 1 : ITERS + 3]
+    sol_ref, coarse_ref, res_ref, kept_ref, turn_ref, line_ref, rows_ref = refs[ITERS + 3 :]
+    width = fields[0].shape[-1]
+    total_rows = fields[0].shape[0]
+    period = rhs
+    while period % 8:
+        period *= 2
+    per_row = width // SLOT
+    packed_rows = packed.shape[0]
+    turn_ref[...] = jnp.zeros_like(turn_ref)
+    turn_ref[0:packed_rows, :] = packed[...]
+    turned = jnp.transpose(turn_ref[...])
+    lane = lax.broadcasted_iota(jnp.int32, (SLOT, width), 1)
+    quantities = jnp.zeros((SLOT, width), jnp.float32)
+    for m in range(per_row):
+        part = turned[SLOT * m : SLOT * m + SLOT]
+        moved = pltpu.roll(part, LANES_EACH * m, 1) if m else part
+        inside = (lane >= LANES_EACH * m) & (lane < LANES_EACH * m + LANES_EACH)
+        quantities = jnp.where(inside, moved, quantities)
+
+    def quantity(at):
+        return jnp.broadcast_to(quantities[at : at + 1], (8, width))
+
+    products = [[None] * (ITERS + 1) for _ in range(ITERS + 1)]
+    for power in range(1, ITERS + 1):
+        for other, real_lane, imag_lane in pair_slots(power):
+            re = quantity(real_lane)
+            im = quantity(imag_lane) if imag_lane is not None else None
+            products[power][other] = (re, im)
+            if other and imag_lane is not None:
+                products[other][power] = (re, -im)
+    coeffs, combined = step_coefficients(products)
+    parts = []
+    for value in coeffs[1:]:
+        parts += [value[0], value[1]]
+    for value in combined:
+        parts += [value[0] * STEP_SCALE, value[1] * STEP_SCALE]
+    line_ref[...] = jnp.zeros_like(line_ref)
+    for at, part in enumerate(parts):
+        line_ref[at : at + 1, :] = part[0:1]
+    turn_ref[...] = jnp.transpose(line_ref[...])
+    for r in range(rhs):
+        j, m = divmod(r, per_row)
+        source = turn_ref[LANES_EACH * m + j : LANES_EACH * m + j + 1, :]
+        for at in range(r, period, rhs):
+            rows_ref[at : at + 1, :] = source
+    columns = rows_ref[...]
+    spread = [jnp.broadcast_to(columns[:, at : at + 1], (period, width)) for at in range(len(parts))]
     sign = lane_sign(width)
-
-    def spread(value, factor):
-        real_part = jnp.broadcast_to(value[0] * factor, (period, width))
-        imag_part = jnp.broadcast_to(value[1] * factor, (period, width)) * (-sign)
-        return real_part, imag_part
-
-    res_co = [spread(c, 1.0) for c in coeffs]
-    sol_co = [spread(c, STEP_SCALE) for c in solution]
     for base in range(0, total_rows, period):
-        res = None
+        res = fields[0][base : base + period, :]
+        res_turn = None
         sol = None
+        sol_turn = None
         for i in range(ITERS + 1):
             value = fields[i][base : base + period, :]
-            turned = pltpu.roll(value, width // 2, 1)
-            if i == 0:
-                res = value
-            else:
-                res = res + res_co[i][0] * value + res_co[i][1] * turned
+            if i:
+                at = 2 * (i - 1)
+                res = res + spread[at] * value
+                term = spread[at + 1] * value
+                res_turn = term if res_turn is None else res_turn + term
             if i < ITERS:
-                term = sol_co[i][0] * value + sol_co[i][1] * turned
+                at = 2 * ITERS + 2 * i
+                term = spread[at] * value
                 sol = term if sol is None else sol + term
-        kept_ref[base : base + period, :] = sol
-        res_ref[base : base + period, :] = res
+                term = spread[at + 1] * value
+                sol_turn = term if sol_turn is None else sol_turn + term
+        res_ref[base : base + period, :] = res - sign * pltpu.roll(res_turn, width // 2, 1)
+        kept_ref[base : base + period, :] = sol - sign * pltpu.roll(sol_turn, width // 2, 1)
     sites = restriction.shape[0]
     extent = sites // depth
     cells = extent // 2
@@ -341,21 +388,38 @@
         store_site(sol_ref, site, sites, rhs, load_site(kept_ref, site, sites, rhs, False), True)
 
 
+def assemble_kernel(own_ref, *refs):
+    out_ref = refs[-1]
+    me = lax.axis_index("narrow")
+    out_ref[me] = own_ref[...]
+    for k, ref in enumerate(refs[:-1]):
+        out_ref[jnp.bitwise_xor(me, k + 1)] = ref[...]
+
+
 def vmem(count):
     return [pl.BlockSpec(memory_space=pltpu.VMEM)] * count
 
 
-def call(kernel, outs, *args, scratch=(), name=None):
+def call(kernel, outs, *args, scratch=(), in_specs=None):
     single = not isinstance(outs, (list, tuple))
     return pl.pallas_call(
         kernel,
         out_shape=outs,
-        in_specs=vmem(len(args)),
+        in_specs=vmem(len(args)) if in_specs is None else in_specs,
         out_specs=pl.BlockSpec(memory_space=pltpu.VMEM) if single else tuple(vmem(len(outs))),
         scratch_shapes=list(scratch),
         compiler_params=pltpu.CompilerParams(vmem_limit_bytes=VMEM_LIMIT),
-        name=name,
     )(*args)
+
+
+def swap_pairs(size, offset, span=None):
+    span = size if span is None else span
+    pairs = []
+    for first in range(0, size, span):
+        for i in range(offset, span + offset, 2):
+            a, b = first + i % span, first + (i + 1) % span
+            pairs += [(a, b), (b, a)]
+    return pairs
 
 
 def per_device(right_side, hop_blocks, restriction):
@@ -374,14 +438,13 @@
     f32 = jnp.float32
     field_shape = jax.ShapeDtypeStruct((total_rows, width), f32)
     gram_shape = jax.ShapeDtypeStruct((period, width), f32)
-    hops = hop_blocks[0]
-
-    up_y = [(i, i // rows_y * rows_y + (i + 1) % rows_y) for i in range(wide)]
-    down_y = [(b, a) for a, b in up_y]
+    hops = hop_blocks
+
+    if rows_y % 2 or narrow % 2 or narrow & (narrow - 1):
+        raise ValueError("odd ring")
     up_z = [(i, (i + rows_y) % wide) for i in range(wide)]
     down_z = [(b, a) for a, b in up_z]
-    up_t = [(i, (i + 1) % narrow) for i in range(narrow)]
-    down_t = [(b, a) for a, b in up_t]
+    odd_row = lax.axis_index("wide") % 2 == 1
 
     by_rhs = jnp.transpose(right_side[0], (1, 0, 2))
     field = by_rhs.reshape(total_rows, width)
@@ -389,65 +452,86 @@
     last_row = by_rhs[:, sites - extent :].reshape(half, width)
     fields = []
     grams = []
+    hops = None
+    table = pltpu.VMEM((sites, 4 * tile_rows, width), jnp.bfloat16)
     for power in range(ITERS):
         if power:
             field = fields[power]
             first_row = field[:half]
             last_row = field[total_rows - half :]
-        fwd = lax.ppermute(first_row, "wide", down_y)
-        back = lax.ppermute(last_row, "wide", up_y)
-        later = lax.ppermute(field, "narrow", down_t)
-        earlier = lax.ppermute(field, "narrow", up_t)
-        received = [fwd, back, later, earlier]
+        up_send = jnp.where(odd_row, first_row, last_row)
+        down_send = jnp.where(odd_row, last_row, first_row)
+        side_b = lax.ppermute(down_send, "wide", swap_pairs(wide, 1, rows_y))
+        side_a = lax.ppermute(up_send, "wide", swap_pairs(wide, 0, rows_y))
+        time_b = lax.ppermute(field, "narrow", swap_pairs(narrow, 1))
+        time_a = lax.ppermute(field, "narrow", swap_pairs(narrow, 0))
+        received = [side_a, side_b, time_a, time_b]
         if not wrap_z:
             received += [lax.ppermute(field, "wide", down_z), lax.ppermute(field, "wide", up_z)]
-        near, other = call(
-            functools.partial(near_kernel, power, YLOC, rhs, wrap_z),
-            [field_shape, gram_shape if power else field_shape],
-            *(fields if power else [field]),
+        if power == 0:
+            near, start, hops = call(
+                functools.partial(first_near_kernel, YLOC, rhs, wrap_z),
+                [field_shape, field_shape, jax.ShapeDtypeStruct(hop_blocks.shape, hop_blocks.dtype)],
+                field,
+                hop_blocks,
+                in_specs=[pl.BlockSpec(memory_space=pl.ANY)] * 2,
+                scratch=[
+                    table,
+                    pltpu.VMEM((total_rows, width), f32),
+                    pltpu.SemaphoreType.DMA(()),
+                    pltpu.SemaphoreType.DMA((sites,)),
+                ],
+            )
+            fields.append(start)
+        else:
+            near, gram = call(
+                functools.partial(near_kernel, power, YLOC, rhs, wrap_z),
+                [field_shape, gram_shape],
+                *fields,
+                hops,
+                scratch=[table],
+            )
+            grams.append(gram)
+        last = power + 1 == ITERS
+        slots = 2 * sites + 2 * extent + (0 if wrap_z else 2 * sites)
+        per_row = width // SLOT
+        packed_rows = -(-rhs // per_row)
+        outs = call(
+            functools.partial(far_kernel, YLOC, rhs, wrap_z, power == 0, last),
+            [field_shape] + ([jax.ShapeDtypeStruct((packed_rows, width), f32)] if last else []),
+            near,
             hops,
-            scratch=[pltpu.VMEM((sites, 4 * tile_rows, width), jnp.bfloat16)],
-            name=f"near{power}",
+            *received,
+            *(fields + grams if last else []),
+            scratch=[pltpu.VMEM((slots, 4 * tile_rows, width), jnp.bfloat16)],
         )
-        if power:
-            grams.append(other)
-        else:
-            fields.append(other)
-        slots = 2 * sites + 2 * extent + (0 if wrap_z else 2 * sites)
-        fields.append(
-            call(
-                functools.partial(far_kernel, YLOC, rhs, wrap_z, power == 0),
-                field_shape,
-                near,
-                hops,
-                *received,
-                scratch=[pltpu.VMEM((slots, 4 * tile_rows, width), jnp.bfloat16)],
-                name=f"far{power}",
-            )
-        )
-    per_row = width // SLOT
-    packed_rows = -(-rhs // per_row)
-    packed = call(
-        functools.partial(pack_kernel, rhs),
-        jax.ShapeDtypeStruct((packed_rows, width), f32),
-        *fields,
-        *grams,
-        name="pack",
-    )
+        fields.append(outs[0])
+    packed = outs[1]
     copies = jnp.broadcast_to(packed[None], (wide * narrow, packed_rows, width))
     swapped = lax.all_to_all(copies, ("wide", "narrow"), 0, 0)
     totals = jnp.sum(swapped, axis=0)
     cells = extent // 2
+    square = pltpu.VMEM((width, width), f32)
     solution_rows, coarse = call(
         functools.partial(final_kernel, YLOC, rhs),
         [field_shape, jax.ShapeDtypeStruct((rhs * cells, width), f32)],
         *fields,
         totals,
         restriction[0],
-        scratch=[pltpu.VMEM((total_rows, width), f32), pltpu.VMEM((total_rows, width), f32)],
-        name="final",
+        scratch=[
+            pltpu.VMEM((total_rows, width), f32),
+            pltpu.VMEM((total_rows, width), f32),
+            square,
+            square,
+            pltpu.VMEM((period, width), f32),
+        ],
     )
-    slices = lax.all_gather(coarse, "narrow", axis=0, tiled=True)
+    others = []
+    for k in range(1, narrow):
+        others.append(lax.ppermute(coarse, "narrow", [(i, i ^ k) for i in range(narrow)]))
+    slices = call(
+        assemble_kernel, jax.ShapeDtypeStruct((narrow,) + coarse.shape, f32), coarse, *others
+    )
     coarse_residual = jnp.transpose(slices.reshape(narrow, rhs, cells, width), (0, 2, 1, 3))
     solution_field = jnp.transpose(solution_rows.reshape(rhs, sites, width), (1, 0, 2))
     return solution_field[None], coarse_residual

time: 65.2 us -> 63.6 us (0.975)
  waiting for transfers between devices: 3.99 us -> 14.1 us
  starting transfers between devices: 27.7 us -> 19.7 us
  blocking collectives: 18.8 us -> 10.9 us
  Pallas kernels: 8.69 us -> 14.5 us
  local copies, waits for them, and re-layouts: 5.01 us -> 2.57 us
  other arithmetic: 0.04 us -> 0.9 us
    ppermute x16 -> x19, waiting for transfers between devices: 3.99 us -> 14.1 us  [the longest x4 11.6 us: per_device(): side_b = lax.ppermute(down_send, 'wide', swap_pairs(wide, 1, rows_y))]
    ppermute x16 -> x19, starting transfers between devices: 27.7 us -> 19.7 us  [the longest x4 11.4 us: per_device(): side_b = lax.ppermute(down_send, 'wide', swap_pairs(wide, 1, rows_y))]
    pallas_call x10, Pallas kernels: 8.69 us -> 14.5 us  [call(): pl.pallas_call(kernel, out_shape=outs, in_specs=vmem(len(args)) if in_spe...]
    all_gather x1 -> x0, blocking collectives: 5.31 us -> none  [per_device(): slices = lax.all_gather(coarse, 'narrow', axis=0, tiled=True)]
    all_to_all x1, blocking collectives: 13.4 us -> 10.9 us  [per_device(): swapped = lax.all_to_all(copies, ('wide', 'narrow'), 0, 0)]
    unnamed x9 -> x6, local copies, waits for them, and re-layouts: 4.14 us -> 2.56 us
    select_n x0 -> x4, other arithmetic: none -> 0.86 us  [per_device(): down_send = jnp.where(odd_row, last_row, first_row)]
    reshape x1 -> x0, local copies, waits for them, and re-layouts: 0.84 us -> none  [per_device(): last_row = by_rhs[:, sites - extent:].reshape(half, width)]
  transfers between devices with their start and end apart: 16 -> 19, of which waited for: 3 -> 8; matrix products, arithmetic and copies ran while one was open for 1% -> 1% of each run, Pallas kernels for 4% -> 15%
where the time goes in v2:
time: 63.6 us; the launch traced here: 63.3 us
  starting transfers between devices  19.7 us (31%)
  Pallas kernels  14.5 us (23%)
  waiting for transfers between devices  14.1 us (22%)
  blocking collectives  10.9 us (17%)
  local copies, waits for them, and re-layouts  2.57 us (4%)
  other arithmetic  0.9 us (1%)
  between operations  0.74 us (1%)
    pallas_call x10, Pallas kernels, call(): pl.pallas_call(kernel, out_shape=outs, in_specs=vmem(len(args)) if in_spe...  14.5 us
    ppermute x4, waiting for transfers between devices, per_device(): side_b = lax.ppermute(down_send, 'wide', swap_pairs(wide, 1, rows_y))  11.6 us
    ppermute x4, starting transfers between devices, per_device(): side_b = lax.ppermute(down_send, 'wide', swap_pairs(wide, 1, rows_y))  11.4 us
    all_to_all x1, blocking collectives, per_device(): swapped = lax.all_to_all(copies, ('wide', 'narrow'), 0, 0)  10.9 us
    ppermute x4, starting transfers between devices, per_device(): time_a = lax.ppermute(field, 'narrow', swap_pairs(narrow, 0))  3.52 us
    ppermute x4, starting transfers between devices, per_device(): time_b = lax.ppermute(field, 'narrow', swap_pairs(narrow, 1))  2.67 us
    unnamed x6, local copies, waits for them, and re-layouts  2.56 us
    ppermute x3, waiting for transfers between devices, per_device(): lax.ppermute(coarse, 'narrow', [(i, i ^ k) for i in range(narrow)])  2.18 us
  transfers between devices with their start and end apart: 19, of which 8 were waited for; matrix products, arithmetic and copies ran while one was open for 1% of the time, Pallas kernels for 15%

profile of v2, /device:TPU:0, one launch (start us, length us, event | category | flops | bytes accessed | tf_op | source)
XLA Modules:
  0.0 63.3 jit_solution(15496760504968769177)
XLA Ops:
  0.6 2.5 %collective-permute-start.3 = (f32[192,128]{1,0:T(8,128)}, f32[192,128]{1,0:T(8,128)S(1)}, u32[]{:S(2)}, u32[]{:S(2)}) collective-permute-start(f32[192,128]{1,0:T(8,128)} %bitcast.19), channel_id=1, source_target_pairs={{1,2},{2,1},{3,0},{0,3},{5,6},{6,5},{7,4},{4,7},{9,10},{10,9},{11,... | collective-permute-start | bytes 294920 | tf_op jit(solution)/shard_map/ppermute | solution.py:466
  3.1 0.7 %collective-permute-start.2 = (f32[192,128]{1,0:T(8,128)}, f32[192,128]{1,0:T(8,128)S(1)}, u32[]{:S(2)}, u32[]{:S(2)}) collective-permute-start(f32[192,128]{1,0:T(8,128)} %bitcast.20), channel_id=1, source_target_pairs={{0,1},{1,0},{2,3},{3,2},{4,5},{5,4},{6,7},{7,6},{8,9},{9,8},{10,11... | collective-permute-start | bytes 294920 | tf_op jit(solution)/shard_map/ppermute | solution.py:467
  3.8 0.8 %select_bitcast_fusion = (f32[96,128]{1,0:T(8,128)S(1)}, f32[96,128]{1,0:T(8,128)S(1)}) fusion(f32[12,16,128]{2,1,0:T(8,128)} %bitcast.21, pred[]{:T(512)S(6)} %eq.5), kind=kLoop, calls=%fused_computation | loop fusion | flops 24576 | bytes 196609 | tf_op jit(solution)/shard_map/jit(_where)/select_n | solution.py:463
  4.6 4.6 %collective-permute-start.1 = (f32[96,128]{1,0:T(8,128)S(1)}, f32[96,128]{1,0:T(8,128)S(1)}, u32[]{:S(2)}, u32[]{:S(2)}) collective-permute-start(f32[96,128]{1,0:T(8,128)S(1)} %get-tuple-element.34), channel_id=1, source_target_pairs={{4,8},{8,4},{12,16},{16,12},{20,24},{24,20},{28,0},{0,28},{5,9},{9... | collective-permute-start | bytes 147464 | tf_op jit(solution)/shard_map/ppermute | solution.py:464
  9.2 0.0 collective-permute-start
  9.2 0.0 copy-start
  9.2 1.7 %copy-done = bf16[1,16,9,64,128]{4,3,2,1,0:T(8,128)(2,1)S(1)} copy-done((bf16[1,16,9,64,128]{4,3,2,1,0:T(8,128)(2,1)S(1)}, bf16[1,16,9,64,128]{4,3,2,1,0:T(8,128)(2,1)}, u32[]{:S(2)}) %copy-start) | copy-done | bytes 2359320
  10.9 0.0 copy-start.2
  10.9 0.9 %copy-done.2 = f32[1,16,12,128]{3,1,2,0:T(8,128)S(1)} copy-done((f32[1,16,12,128]{3,1,2,0:T(8,128)S(1)}, f32[1,16,12,128]{3,1,2,0:T(8,128)}, u32[]{:S(2)}) %copy-start.2) | copy-done | bytes 98328
  11.8 7.6 %shard_map.50 = (f32[192,128]{1,0:T(8,128)S(1)}, f32[192,128]{1,0:T(8,128)S(1)}, bf16[1,16,9,64,128]{4,3,2,1,0:T(8,128)(2,1)S(1)}) custom-call(f32[192,128]{1,0:T(8,128)S(1)} %bitcast.22, bf16[1,16,9,64,128]{4,3,2,1,0:T(8,128)(2,1)S(1)} %copy-done), custom_call_target="tpu_custom_call" | custom-call | tf_op jit(solution)/shard_map/pallas_call | solution.py:405
  19.4 0.0 collective-permute-done.1.refs_3_
  19.4 0.0 collective-permute-done.refs_2_
  19.4 0.0 collective-permute-done.3.refs_5_
  19.4 0.0 collective-permute-done.2.refs_4_
  19.4 0.6 shard_map.51.refs_1_.refs_7_
  20.0 0.1 collective-permute-start.7
  20.1 0.6 collective-permute-start.6
  20.7 2.0 %collective-permute-start.5 = (f32[96,128]{1,0:T(8,128)S(1)}, f32[96,128]{1,0:T(8,128)S(1)}, u32[]{:S(2)}, u32[]{:S(2)}) collective-permute-start(f32[96,128]{1,0:T(8,128)S(1)} %get-tuple-element.32), channel_id=1, source_target_pairs={{4,8},{8,4},{12,16},{16,12},{20,24},{24,20},{28,0},{0,28},{5,9},{9... | collective-permute-start | bytes 147464 | tf_op jit(solution)/shard_map/ppermute | solution.py:464
  22.7 0.2 collective-permute-start.4
  22.9 0.7 %shard_map.52 = (f32[192,128]{1,0:T(8,128)S(1)}, f32[24,128]{1,0:T(8,128)S(1)}) custom-call(f32[192,128]{1,0:T(8,128)S(1)} %get-tuple-element.15.refs_0_.refs_6_, f32[192,128]{1,0:T(8,128)S(1)} %shard_map.51.refs_1_.refs_7_, bf16[1,16,9,64,128]{4,3,2,1,0:T(8,128)(2,1)S(1)} %get-tuple-element.17.refs_1_.refs_2_.refs_3_.refs_4_), custom_call_target="tpu_custom_call" | custom-call | tf_op jit(solution)/shard_map/pallas_call | solution.py:405
  23.5 4.0 %collective-permute-done.5.refs_3_ = f32[96,128]{1,0:T(8,128)S(1)} collective-permute-done((f32[96,128]{1,0:T(8,128)S(1)}, f32[96,128]{1,0:T(8,128)S(1)}, u32[]{:S(2)}, u32[]{:S(2)}) %collective-permute-start.5) | collective-permute-done | bytes 49184 | tf_op jit(solution)/shard_map/ppermute | solution.py:464
  27.5 0.1 collective-permute-done.4.refs_2_
  27.6 0.0 collective-permute-done.7.refs_5_
  27.6 0.0 collective-permute-done.6.refs_4_
  27.6 0.6 shard_map.53.refs_2_.refs_8_
  28.2 0.1 collective-permute-start.11
  28.3 1.6 %collective-permute-start.10 = (f32[192,128]{1,0:T(8,128)S(1)}, f32[192,128]{1,0:T(8,128)S(1)}, u32[]{:S(2)}, u32[]{:S(2)}) collective-permute-start(f32[192,128]{1,0:T(8,128)S(1)} %shard_map.53.refs_2_.refs_8_), channel_id=1, source_target_pairs={{0,1},{1,0},{2,3},{3,2},{4,5},{5,4},{6,7},{7,6},{8,9},{9,8},{10,11... | collective-permute-start | bytes 294920 | tf_op jit(solution)/shard_map/ppermute | solution.py:467
  29.9 2.4 %collective-permute-start.9 = (f32[96,128]{1,0:T(8,128)S(1)}, f32[96,128]{1,0:T(8,128)S(1)}, u32[]{:S(2)}, u32[]{:S(2)}) collective-permute-start(f32[96,128]{1,0:T(8,128)S(1)} %get-tuple-element.30), channel_id=1, source_target_pairs={{4,8},{8,4},{12,16},{16,12},{20,24},{24,20},{28,0},{0,28},{5,9},{9... | collective-permute-start | bytes 147464 | tf_op jit(solution)/shard_map/ppermute | solution.py:464
  32.3 0.0 collective-permute-start.8
  32.3 0.7 %shard_map.54 = (f32[192,128]{1,0:T(8,128)S(1)}, f32[24,128]{1,0:T(8,128)S(1)}) custom-call(f32[192,128]{1,0:T(8,128)S(1)} %get-tuple-element.15.refs_0_.refs_6_, f32[192,128]{1,0:T(8,128)S(1)} %shard_map.51.refs_1_.refs_7_, f32[192,128]{1,0:T(8,128)S(1)} %shard_map.53.refs_2_.refs_8_, ...), custom_call_target="tpu_custom_call" | custom-call | tf_op jit(solution)/shard_map/pallas_call | solution.py:405
  33.0 3.8 %collective-permute-done.9.refs_3_ = f32[96,128]{1,0:T(8,128)S(1)} collective-permute-done((f32[96,128]{1,0:T(8,128)S(1)}, f32[96,128]{1,0:T(8,128)S(1)}, u32[]{:S(2)}, u32[]{:S(2)}) %collective-permute-start.9) | collective-permute-done | bytes 49184 | tf_op jit(solution)/shard_map/ppermute | solution.py:464
  36.8 0.1 collective-permute-done.8.refs_2_
  36.9 0.0 collective-permute-done.11.refs_5_
  36.9 0.0 collective-permute-done.10.refs_4_
  36.9 0.6 shard_map.55.refs_3_.refs_9_
  37.5 0.1 collective-permute-start.15
  37.6 0.6 collective-permute-start.14
  38.2 2.4 %collective-permute-start.13 = (f32[96,128]{1,0:T(8,128)S(1)}, f32[96,128]{1,0:T(8,128)S(1)}, u32[]{:S(2)}, u32[]{:S(2)}) collective-permute-start(f32[96,128]{1,0:T(8,128)S(1)} %get-tuple-element.28), channel_id=1, source_target_pairs={{4,8},{8,4},{12,16},{16,12},{20,24},{24,20},{28,0},{0,28},{5,9},{9... | collective-permute-start | bytes 147464 | tf_op jit(solution)/shard_map/ppermute | solution.py:464
  40.6 0.0 collective-permute-start.12
  40.6 0.7 %shard_map.56 = (f32[192,128]{1,0:T(8,128)S(1)}, f32[24,128]{1,0:T(8,128)S(1)}) custom-call(f32[192,128]{1,0:T(8,128)S(1)} %get-tuple-element.15.refs_0_.refs_6_, f32[192,128]{1,0:T(8,128)S(1)} %shard_map.51.refs_1_.refs_7_, f32[192,128]{1,0:T(8,128)S(1)} %shard_map.53.refs_2_.refs_8_, f32[192,128]{1,0:T(8,128)S(1)} %shard_map.55.refs_3_.refs_9_, ...), custom_call_target="tpu_custom_call" | custom-call | tf_op jit(solution)/shard_map/pallas_call | solution.py:405
  41.3 0.0 copy-start.1
  41.3 3.8 %collective-permute-done.13.refs_3_ = f32[96,128]{1,0:T(8,128)S(1)} collective-permute-done((f32[96,128]{1,0:T(8,128)S(1)}, f32[96,128]{1,0:T(8,128)S(1)}, u32[]{:S(2)}, u32[]{:S(2)}) %collective-permute-start.13) | collective-permute-done | bytes 49184 | tf_op jit(solution)/shard_map/ppermute | solution.py:464
  45.1 0.1 collective-permute-done.12.refs_2_
  45.2 0.0 collective-permute-done.15.refs_5_
  45.2 0.0 collective-permute-done.14.refs_4_
  45.2 0.8 %shard_map.57 = (f32[192,128]{1,0:T(8,128)S(1)}, f32[3,128]{1,0:T(4,128)S(1)}) custom-call(f32[192,128]{1,0:T(8,128)S(1)} %get-tuple-element.20.refs_0_, bf16[1,16,9,64,128]{4,3,2,1,0:T(8,128)(2,1)S(1)} %get-tuple-element.17.refs_1_.refs_2_.refs_3_.refs_4_, f32[96,128]{1,0:T(8,128)S(1)} %collective-permute-done.12.refs_2_, ...), custom_call_target="tpu_custom_call" | custom-call | tf_op jit(solution)/shard_map/pallas_call | solution.py:405
  46.0 10.9 %all_to_all.5 = f32[32,3,128]{2,1,0:T(4,128)S(1)} all-to-all(f32[32,3,128]{2,1,0:T(4,128)S(1)} %broadcast_in_dim.4), channel_id=1, replica_groups=mesh['wide'=8,'narrow'=4] {'wide','narrow'}, dimensions={0} | all-to-all | bytes 98304 | tf_op jit(solution)/shard_map/all_to_all | solution.py:511
  57.0 0.0 copy-done.1
  57.0 1.7 %shard_map.58 = (f32[192,128]{1,0:T(8,128)}, f32[48,128]{1,0:T(8,128)S(1)}) custom-call(f32[192,128]{1,0:T(8,128)S(1)} %get-tuple-element.15.refs_0_.refs_6_, f32[192,128]{1,0:T(8,128)S(1)} %shard_map.51.refs_1_.refs_7_, f32[192,128]{1,0:T(8,128)S(1)} %shard_map.53.refs_2_.refs_8_, f32[192,128]{1,0:T(8,128)S(1)} %shard_map.55.refs_3_.refs_9_, ...), custom_call_target="tpu_custom_call" | custom-call | tf_op jit(solution)/shard_map/pallas_call | solution.py:405
  58.6 0.2 collective-permute-start.18
  58.8 1.6 %collective-permute-start.17 = (f32[48,128]{1,0:T(8,128)S(1)}, f32[48,128]{1,0:T(8,128)S(1)}, u32[]{:S(2)}, u32[]{:S(2)}) collective-permute-start(f32[48,128]{1,0:T(8,128)S(1)} %get-tuple-element.27.own_ref), channel_id=1, source_target_pairs={{0,2},{1,3},{2,0},{3,1},{4,6},{5,7},{6,4},{7,5},{8,10},{9,11},{10,... | collective-permute-start | bytes 73736 | tf_op jit(solution)/shard_map/ppermute | solution.py:531
  60.4 0.1 collective-permute-start.16
  60.5 1.4 %collective-permute-done.18.refs_2_ = f32[48,128]{1,0:T(8,128)S(1)} collective-permute-done((f32[48,128]{1,0:T(8,128)S(1)}, f32[48,128]{1,0:T(8,128)S(1)}, u32[]{:S(2)}, u32[]{:S(2)}) %collective-permute-start.18) | collective-permute-done | bytes 24608 | tf_op jit(solution)/shard_map/ppermute | solution.py:531
  61.9 0.8 %collective-permute-done.17.refs_1_ = f32[48,128]{1,0:T(8,128)S(1)} collective-permute-done((f32[48,128]{1,0:T(8,128)S(1)}, f32[48,128]{1,0:T(8,128)S(1)}, u32[]{:S(2)}, u32[]{:S(2)}) %collective-permute-start.17) | collective-permute-done | bytes 24608 | tf_op jit(solution)/shard_map/ppermute | solution.py:531
  62.7 0.0 collective-permute-done.16.refs_0_
  62.7 0.7 %shard_map.59 = f32[4,48,128]{2,1,0:T(8,128)} custom-call(f32[48,128]{1,0:T(8,128)S(1)} %get-tuple-element.27.own_ref, f32[48,128]{1,0:T(8,128)S(1)} %collective-permute-done.16.refs_0_, f32[48,128]{1,0:T(8,128)S(1)} %collective-permute-done.17.refs_1_, f32[48,128]{1,0:T(8,128)S(1)} %collective-permute-done.18.refs_2_), custom_call_target="tpu_custom_call" | custom-call | tf_op jit(solution)/shard_map/pallas_call | solution.py:405
  (5 shorter events, 0.1 us)
Async XLA Ops:
  0.6 18.8 %collective-permute-start.3 = (f32[192,128]{1,0:T(8,128)}, f32[192,128]{1,0:T(8,128)S(1)}, u32[]{:S(2)}, u32[]{:S(2)}) collective-permute-start(f32[192,128]{1,0:T(8,128)} %bitcast.19), channel_id=1, source_target_pairs={{1,2},{2,1},{3,0},{0,3},{5,6},{6,5},{7,4},{4,7},{9,10},{10,9},{11,... | collective-permute-start | bytes 294920 | tf_op jit(solution)/shard_map/ppermute | solution.py:466
  3.1 16.3 %collective-permute-start.2 = (f32[192,128]{1,0:T(8,128)}, f32[192,128]{1,0:T(8,128)S(1)}, u32[]{:S(2)}, u32[]{:S(2)}) collective-permute-start(f32[192,128]{1,0:T(8,128)} %bitcast.20), channel_id=1, source_target_pairs={{0,1},{1,0},{2,3},{3,2},{4,5},{5,4},{6,7},{7,6},{8,9},{9,8},{10,11... | collective-permute-start | bytes 294920 | tf_op jit(solution)/shard_map/ppermute | solution.py:467
  4.6 14.7 %collective-permute-start.1 = (f32[96,128]{1,0:T(8,128)S(1)}, f32[96,128]{1,0:T(8,128)S(1)}, u32[]{:S(2)}, u32[]{:S(2)}) collective-permute-start(f32[96,128]{1,0:T(8,128)S(1)} %get-tuple-element.34), channel_id=1, source_target_pairs={{4,8},{8,4},{12,16},{16,12},{20,24},{24,20},{28,0},{0,28},{5,9},{9... | collective-permute-start | bytes 147464 | tf_op jit(solution)/shard_map/ppermute | solution.py:464
  9.2 10.2 %collective-permute-start = (f32[96,128]{1,0:T(8,128)S(1)}, f32[96,128]{1,0:T(8,128)S(1)}, u32[]{:S(2)}, u32[]{:S(2)}) collective-permute-start(f32[96,128]{1,0:T(8,128)S(1)} %get-tuple-element.35), channel_id=1, source_target_pairs={{0,4},{4,0},{8,12},{12,8},{16,20},{20,16},{24,28},{28,24},{1,5},{5... | collective-permute-start | bytes 147464 | tf_op jit(solution)/shard_map/ppermute | solution.py:465
  9.2 1.7 %copy-start = (bf16[1,16,9,64,128]{4,3,2,1,0:T(8,128)(2,1)S(1)}, bf16[1,16,9,64,128]{4,3,2,1,0:T(8,128)(2,1)}, u32[]{:S(2)}) copy-start(bf16[1,16,9,64,128]{4,3,2,1,0:T(8,128)(2,1)} %hops_hbm.1) | copy-start | bytes 7077892
  10.9 0.9 %copy-start.2 = (f32[1,16,12,128]{3,1,2,0:T(8,128)S(1)}, f32[1,16,12,128]{3,1,2,0:T(8,128)}, u32[]{:S(2)}) copy-start(f32[1,16,12,128]{3,1,2,0:T(8,128)} %param.3) | copy-start | bytes 294916
  20.0 7.6 %collective-permute-start.7 = (f32[192,128]{1,0:T(8,128)S(1)}, f32[192,128]{1,0:T(8,128)S(1)}, u32[]{:S(2)}, u32[]{:S(2)}) collective-permute-start(f32[192,128]{1,0:T(8,128)S(1)} %shard_map.51.refs_1_.refs_7_), channel_id=1, source_target_pairs={{1,2},{2,1},{3,0},{0,3},{5,6},{6,5},{7,4},{4,7},{9,10},{10,9},{11,... | collective-permute-start | bytes 294920 | tf_op jit(solution)/shard_map/ppermute | solution.py:466
  20.1 7.6 %collective-permute-start.6 = (f32[192,128]{1,0:T(8,128)S(1)}, f32[192,128]{1,0:T(8,128)S(1)}, u32[]{:S(2)}, u32[]{:S(2)}) collective-permute-start(f32[192,128]{1,0:T(8,128)S(1)} %shard_map.51.refs_1_.refs_7_), channel_id=1, source_target_pairs={{0,1},{1,0},{2,3},{3,2},{4,5},{5,4},{6,7},{7,6},{8,9},{9,8},{10,11... | collective-permute-start | bytes 294920 | tf_op jit(solution)/shard_map/ppermute | solution.py:467
  20.7 6.9 %collective-permute-start.5 = (f32[96,128]{1,0:T(8,128)S(1)}, f32[96,128]{1,0:T(8,128)S(1)}, u32[]{:S(2)}, u32[]{:S(2)}) collective-permute-start(f32[96,128]{1,0:T(8,128)S(1)} %get-tuple-element.32), channel_id=1, source_target_pairs={{4,8},{8,4},{12,16},{16,12},{20,24},{24,20},{28,0},{0,28},{5,9},{9... | collective-permute-start | bytes 147464 | tf_op jit(solution)/shard_map/ppermute | solution.py:464
  22.7 5.0 %collective-permute-start.4 = (f32[96,128]{1,0:T(8,128)S(1)}, f32[96,128]{1,0:T(8,128)S(1)}, u32[]{:S(2)}, u32[]{:S(2)}) collective-permute-start(f32[96,128]{1,0:T(8,128)S(1)} %get-tuple-element.33), channel_id=1, source_target_pairs={{0,4},{4,0},{8,12},{12,8},{16,20},{20,16},{24,28},{28,24},{1,5},{5... | collective-permute-start | bytes 147464 | tf_op jit(solution)/shard_map/ppermute | solution.py:465
  28.2 8.7 %collective-permute-start.11 = (f32[192,128]{1,0:T(8,128)S(1)}, f32[192,128]{1,0:T(8,128)S(1)}, u32[]{:S(2)}, u32[]{:S(2)}) collective-permute-start(f32[192,128]{1,0:T(8,128)S(1)} %shard_map.53.refs_2_.refs_8_), channel_id=1, source_target_pairs={{1,2},{2,1},{3,0},{0,3},{5,6},{6,5},{7,4},{4,7},{9,10},{10,9},{11,... | collective-permute-start | bytes 294920 | tf_op jit(solution)/shard_map/ppermute | solution.py:466
  28.3 8.7 %collective-permute-start.10 = (f32[192,128]{1,0:T(8,128)S(1)}, f32[192,128]{1,0:T(8,128)S(1)}, u32[]{:S(2)}, u32[]{:S(2)}) collective-permute-start(f32[192,128]{1,0:T(8,128)S(1)} %shard_map.53.refs_2_.refs_8_), channel_id=1, source_target_pairs={{0,1},{1,0},{2,3},{3,2},{4,5},{5,4},{6,7},{7,6},{8,9},{9,8},{10,11... | collective-permute-start | bytes 294920 | tf_op jit(solution)/shard_map/ppermute | solution.py:467
  29.9 7.0 %collective-permute-start.9 = (f32[96,128]{1,0:T(8,128)S(1)}, f32[96,128]{1,0:T(8,128)S(1)}, u32[]{:S(2)}, u32[]{:S(2)}) collective-permute-start(f32[96,128]{1,0:T(8,128)S(1)} %get-tuple-element.30), channel_id=1, source_target_pairs={{4,8},{8,4},{12,16},{16,12},{20,24},{24,20},{28,0},{0,28},{5,9},{9... | collective-permute-start | bytes 147464 | tf_op jit(solution)/shard_map/ppermute | solution.py:464
  32.3 4.6 %collective-permute-start.8 = (f32[96,128]{1,0:T(8,128)S(1)}, f32[96,128]{1,0:T(8,128)S(1)}, u32[]{:S(2)}, u32[]{:S(2)}) collective-permute-start(f32[96,128]{1,0:T(8,128)S(1)} %get-tuple-element.31), channel_id=1, source_target_pairs={{0,4},{4,0},{8,12},{12,8},{16,20},{20,16},{24,28},{28,24},{1,5},{5... | collective-permute-start | bytes 147464 | tf_op jit(solution)/shard_map/ppermute | solution.py:465
  37.5 7.7 %collective-permute-start.15 = (f32[192,128]{1,0:T(8,128)S(1)}, f32[192,128]{1,0:T(8,128)S(1)}, u32[]{:S(2)}, u32[]{:S(2)}) collective-permute-start(f32[192,128]{1,0:T(8,128)S(1)} %shard_map.55.refs_3_.refs_9_), channel_id=1, source_target_pairs={{1,2},{2,1},{3,0},{0,3},{5,6},{6,5},{7,4},{4,7},{9,10},{10,9},{11,... | collective-permute-start | bytes 294920 | tf_op jit(solution)/shard_map/ppermute | solution.py:466
  37.6 7.7 %collective-permute-start.14 = (f32[192,128]{1,0:T(8,128)S(1)}, f32[192,128]{1,0:T(8,128)S(1)}, u32[]{:S(2)}, u32[]{:S(2)}) collective-permute-start(f32[192,128]{1,0:T(8,128)S(1)} %shard_map.55.refs_3_.refs_9_), channel_id=1, source_target_pairs={{0,1},{1,0},{2,3},{3,2},{4,5},{5,4},{6,7},{7,6},{8,9},{9,8},{10,11... | collective-permute-start | bytes 294920 | tf_op jit(solution)/shard_map/ppermute | solution.py:467
  38.2 7.0 %collective-permute-start.13 = (f32[96,128]{1,0:T(8,128)S(1)}, f32[96,128]{1,0:T(8,128)S(1)}, u32[]{:S(2)}, u32[]{:S(2)}) collective-permute-start(f32[96,128]{1,0:T(8,128)S(1)} %get-tuple-element.28), channel_id=1, source_target_pairs={{4,8},{8,4},{12,16},{16,12},{20,24},{24,20},{28,0},{0,28},{5,9},{9... | collective-permute-start | bytes 147464 | tf_op jit(solution)/shard_map/ppermute | solution.py:464
  40.6 4.6 %collective-permute-start.12 = (f32[96,128]{1,0:T(8,128)S(1)}, f32[96,128]{1,0:T(8,128)S(1)}, u32[]{:S(2)}, u32[]{:S(2)}) collective-permute-start(f32[96,128]{1,0:T(8,128)S(1)} %get-tuple-element.29), channel_id=1, source_target_pairs={{0,4},{4,0},{8,12},{12,8},{16,20},{20,16},{24,28},{28,24},{1,5},{5... | collective-permute-start | bytes 147464 | tf_op jit(solution)/shard_map/ppermute | solution.py:465
  41.3 15.6 %copy-start.1 = (f32[1,16,64,128]{3,2,1,0:T(8,128)S(1)}, f32[1,16,64,128]{3,2,1,0:T(8,128)}, u32[]{:S(2)}) copy-start(f32[1,16,64,128]{3,2,1,0:T(8,128)} %param.5) | copy-start | bytes 1572868
  58.6 3.3 %collective-permute-start.18 = (f32[48,128]{1,0:T(8,128)S(1)}, f32[48,128]{1,0:T(8,128)S(1)}, u32[]{:S(2)}, u32[]{:S(2)}) collective-permute-start(f32[48,128]{1,0:T(8,128)S(1)} %get-tuple-element.27.own_ref), channel_id=1, source_target_pairs={{0,3},{1,2},{2,1},{3,0},{4,7},{5,6},{6,5},{7,4},{8,11},{9,10},{10,... | collective-permute-start | bytes 73736 | tf_op jit(solution)/shard_map/ppermute | solution.py:531
  58.8 3.9 %collective-permute-start.17 = (f32[48,128]{1,0:T(8,128)S(1)}, f32[48,128]{1,0:T(8,128)S(1)}, u32[]{:S(2)}, u32[]{:S(2)}) collective-permute-start(f32[48,128]{1,0:T(8,128)S(1)} %get-tuple-element.27.own_ref), channel_id=1, source_target_pairs={{0,2},{1,3},{2,0},{3,1},{4,6},{5,7},{6,4},{7,5},{8,10},{9,11},{10,... | collective-permute-start | bytes 73736 | tf_op jit(solution)/shard_map/ppermute | solution.py:531
  60.4 2.3 %collective-permute-start.16 = (f32[48,128]{1,0:T(8,128)S(1)}, f32[48,128]{1,0:T(8,128)S(1)}, u32[]{:S(2)}, u32[]{:S(2)}) collective-permute-start(f32[48,128]{1,0:T(8,128)S(1)} %get-tuple-element.27.own_ref), channel_id=1, source_target_pairs={{0,1},{1,0},{2,3},{3,2},{4,5},{5,4},{6,7},{7,6},{8,9},{9,8},{10,11... | collective-permute-start | bytes 73736 | tf_op jit(solution)/shard_map/ppermute | solution.py:531

commit v3 on v2

--- a/solution.py
+++ b/solution.py
@@ -148,21 +148,32 @@
         store_site(near_ref, site, sites, rhs, value, False)
 
 
-def first_near_kernel(depth, rhs, wrap_z, field_hbm, hops_hbm, near_ref, start_ref, hops_ref, table, field_ref, field_sem, hops_sem):
-    sites = hops_hbm.shape[1]
-    field_copy = pltpu.make_async_copy(field_hbm, field_ref, field_sem)
-    field_copy.start()
-    copies = [
-        pltpu.make_async_copy(hops_hbm.at[0, site], hops_ref.at[0, site], hops_sem.at[site])
-        for site in range(sites)
-    ]
-    for copy in copies:
-        copy.start()
-    field_copy.wait()
-    prepare(field_ref, table, 0, sites, rhs, True)
+def open_kernel(extent, right_ref, field_ref, up_ref, down_ref):
+    rhs, sites, width = right_ref.shape
+    flat = right_ref.reshape(rhs * sites, width)
     for site in range(sites):
-        store_site(start_ref, site, sites, rhs, load_site(field_ref, site, sites, rhs, True), False)
-    near_sites(hops_ref, table, near_ref, depth, rhs, wrap_z, lambda site: copies[site].wait())
+        store_site(field_ref, site, sites, rhs, load_site(flat, site, sites, rhs, True), False)
+    half = extent * rhs
+    choose_sends(field_ref, up_ref, down_ref, half)
+
+
+def choose_sends(field_ref, up_ref, down_ref, half):
+    odd = lax.rem(lax.axis_index("wide"), 2) == 1
+    rows = field_ref.shape[0]
+    first = field_ref[0:half, :]
+    last = field_ref[rows - half : rows, :]
+    up_ref[...] = jnp.where(odd, first, last)
+    down_ref[...] = jnp.where(odd, last, first)
+
+
+def first_near_kernel(depth, rhs, wrap_z, field_ref, hops_ref, near_ref, kept_ref, table):
+    sites = hops_ref.shape[1]
+    prepare(field_ref, table, 0, sites, rhs, False)
+
+    def keep(site):
+        kept_ref[0, site] = hops_ref[0, site]
+
+    near_sites(hops_ref, table, near_ref, depth, rhs, wrap_z, keep)
 
 
 def near_kernel(power, depth, rhs, wrap_z, *refs):
@@ -173,7 +184,7 @@
     gram_ref[...] = gram_columns(power, fields, gram_ref.shape[0])
 
 
-def far_kernel(depth, rhs, wrap_z, by_rhs, last, *refs):
+def far_kernel(depth, rhs, wrap_z, last, *refs):
     near_ref, hops, side_a, side_b, time_a, time_b = refs[:6]
     table = refs[-1]
     extra = refs[6:-1]
@@ -185,13 +196,13 @@
     below = above + sites
     odd_row = lax.rem(lax.axis_index("wide"), 2) == 1
     odd_time = lax.rem(lax.axis_index("narrow"), 2)
-    prepare_pair(odd_row, side_a, side_b, table, ahead, extent, rhs, by_rhs)
-    prepare_pair(odd_row, side_b, side_a, table, behind, extent, rhs, by_rhs)
-    prepare(time_a, table, 0, sites, rhs, by_rhs)
-    prepare(time_b, table, sites, sites, rhs, by_rhs)
+    prepare_pair(odd_row, side_a, side_b, table, ahead, extent, rhs, False)
+    prepare_pair(odd_row, side_b, side_a, table, behind, extent, rhs, False)
+    prepare(time_a, table, 0, sites, rhs, False)
+    prepare(time_b, table, sites, sites, rhs, False)
     if not wrap_z:
-        prepare(extra[0], table, above, sites, rhs, by_rhs)
-        prepare(extra[1], table, below, sites, rhs, by_rhs)
+        prepare(extra[0], table, above, sites, rhs, False)
+        prepare(extra[1], table, below, sites, rhs, False)
         extra = extra[2:]
     out_ref = extra[ITERS * 2 - 1] if last else extra[0]
     for site in range(sites):
@@ -206,7 +217,9 @@
         value = site_product([table[at] for _, at in chosen], [hops[0, site, d] for d, _ in chosen])
         value = value + load_site(near_ref, site, sites, rhs, False)
         store_site(out_ref, site, sites, rhs, value, False)
-    if last:
+    if not last:
+        choose_sends(out_ref, extra[1], extra[2], extent * rhs)
+    else:
         fields = list(extra[:ITERS]) + [out_ref]
         pack(rhs, fields, extra[ITERS : 2 * ITERS - 1], extra[2 * ITERS])
 
@@ -400,15 +413,16 @@
     return [pl.BlockSpec(memory_space=pltpu.VMEM)] * count
 
 
-def call(kernel, outs, *args, scratch=(), in_specs=None):
+def call(kernel, outs, *args, scratch=(), cost=None):
     single = not isinstance(outs, (list, tuple))
     return pl.pallas_call(
         kernel,
         out_shape=outs,
-        in_specs=vmem(len(args)) if in_specs is None else in_specs,
+        in_specs=vmem(len(args)),
         out_specs=pl.BlockSpec(memory_space=pltpu.VMEM) if single else tuple(vmem(len(outs))),
         scratch_shapes=list(scratch),
         compiler_params=pltpu.CompilerParams(vmem_limit_bytes=VMEM_LIMIT),
+        cost_estimate=cost,
     )(*args)
 
 
@@ -444,23 +458,19 @@
         raise ValueError("odd ring")
     up_z = [(i, (i + rows_y) % wide) for i in range(wide)]
     down_z = [(b, a) for a, b in up_z]
-    odd_row = lax.axis_index("wide") % 2 == 1
-
-    by_rhs = jnp.transpose(right_side[0], (1, 0, 2))
-    field = by_rhs.reshape(total_rows, width)
-    first_row = by_rhs[:, :extent].reshape(half, width)
-    last_row = by_rhs[:, sites - extent :].reshape(half, width)
-    fields = []
+    half_shape = jax.ShapeDtypeStruct((half, width), f32)
+    block_bytes = hop_blocks.size * hop_blocks.dtype.itemsize
+    field, up_send, down_send = call(
+        functools.partial(open_kernel, extent),
+        [field_shape, half_shape, half_shape],
+        jnp.transpose(right_side[0], (1, 0, 2)),
+        cost=pl.CostEstimate(flops=0, transcendentals=0, bytes_accessed=2 * block_bytes),
+    )
+    fields = [field]
     grams = []
     hops = None
     table = pltpu.VMEM((sites, 4 * tile_rows, width), jnp.bfloat16)
     for power in range(ITERS):
-        if power:
-            field = fields[power]
-            first_row = field[:half]
-            last_row = field[total_rows - half :]
-        up_send = jnp.where(odd_row, first_row, last_row)
-        down_send = jnp.where(odd_row, last_row, first_row)
         side_b = lax.ppermute(down_send, "wide", swap_pairs(wide, 1, rows_y))
         side_a = lax.ppermute(up_send, "wide", swap_pairs(wide, 0, rows_y))
         time_b = lax.ppermute(field, "narrow", swap_pairs(narrow, 1))
@@ -469,20 +479,13 @@
         if not wrap_z:
             received += [lax.ppermute(field, "wide", down_z), lax.ppermute(field, "wide", up_z)]
         if power == 0:
-            near, start, hops = call(
+            near, hops = call(
                 functools.partial(first_near_kernel, YLOC, rhs, wrap_z),
-                [field_shape, field_shape, jax.ShapeDtypeStruct(hop_blocks.shape, hop_blocks.dtype)],
+                [field_shape, jax.ShapeDtypeStruct(hop_blocks.shape, hop_blocks.dtype)],
                 field,
                 hop_blocks,
-                in_specs=[pl.BlockSpec(memory_space=pl.ANY)] * 2,
-                scratch=[
-                    table,
-                    pltpu.VMEM((total_rows, width), f32),
-                    pltpu.SemaphoreType.DMA(()),
-                    pltpu.SemaphoreType.DMA((sites,)),
-                ],
+                scratch=[table],
             )
-            fields.append(start)
         else:
             near, gram = call(
                 functools.partial(near_kernel, power, YLOC, rhs, wrap_z),
@@ -497,15 +500,19 @@
         per_row = width // SLOT
         packed_rows = -(-rhs // per_row)
         outs = call(
-            functools.partial(far_kernel, YLOC, rhs, wrap_z, power == 0, last),
-            [field_shape] + ([jax.ShapeDtypeStruct((packed_rows, width), f32)] if last else []),
+            functools.partial(far_kernel, YLOC, rhs, wrap_z, last),
+            [field_shape]
+            + ([jax.ShapeDtypeStruct((packed_rows, width), f32)] if last else [half_shape] * 2),
             near,
             hops,
             *received,
             *(fields + grams if last else []),
             scratch=[pltpu.VMEM((slots, 4 * tile_rows, width), jnp.bfloat16)],
         )
-        fields.append(outs[0])
+        field = outs[0]
+        fields.append(field)
+        if not last:
+            up_send, down_send = outs[1:]
     packed = outs[1]
     copies = jnp.broadcast_to(packed[None], (wide * narrow, packed_rows, width))
     swapped = lax.all_to_all(copies, ("wide", "narrow"), 0, 0)

time: 63.6 us -> 57.9 us (0.910)
  Pallas kernels: 14.5 us -> 7.73 us
  starting transfers between devices: 19.7 us -> 24.1 us
  waiting for transfers between devices: 14.1 us -> 10.5 us
  blocking collectives: 10.9 us -> 12.1 us
  other arithmetic: 0.9 us -> 0.04 us
    pallas_call x10 -> x11, Pallas kernels: 14.5 us -> 7.73 us  [call(): pl.pallas_call(kernel, out_shape=outs, in_specs=vmem(len(args)), out_spec...]
    ppermute x4, waiting for transfers between devices: 11.6 us -> 8.26 us  [per_device(): side_b = lax.ppermute(down_send, 'wide', swap_pairs(wide, 1, rows_y))]
    ppermute x4, starting transfers between devices: 11.4 us -> 14.3 us  [per_device(): side_b = lax.ppermute(down_send, 'wide', swap_pairs(wide, 1, rows_y))]
    ppermute x4, starting transfers between devices: 0.2 us -> 1.72 us  [per_device(): side_a = lax.ppermute(up_send, 'wide', swap_pairs(wide, 0, rows_y))]
    all_to_all x1, blocking collectives: 10.9 us -> 12.1 us  [per_device(): swapped = lax.all_to_all(copies, ('wide', 'narrow'), 0, 0)]
    select_n x4 -> x0, other arithmetic: 0.86 us -> none  [per_device(): down_send = jnp.where(odd_row, last_row, first_row)]
  transfers between devices with their start and end apart: 19 -> 19, of which waited for: 8 -> 6; matrix products, arithmetic and copies ran while one was open for 1% -> 0% of each run, Pallas kernels for 15% -> 5%
where the time goes in v3:
time: 57.9 us; the launch traced here: 57.7 us
  starting transfers between devices  24.1 us (42%)
  blocking collectives  12.1 us (21%)
  waiting for transfers between devices  10.5 us (18%)
  Pallas kernels  7.73 us (13%)
  local copies, waits for them, and re-layouts  2.57 us (4%)
  between operations  0.71 us (1%)
    ppermute x4, starting transfers between devices, per_device(): side_b = lax.ppermute(down_send, 'wide', swap_pairs(wide, 1, rows_y))  14.3 us
    all_to_all x1, blocking collectives, per_device(): swapped = lax.all_to_all(copies, ('wide', 'narrow'), 0, 0)  12.1 us
    ppermute x4, waiting for transfers between devices, per_device(): side_b = lax.ppermute(down_send, 'wide', swap_pairs(wide, 1, rows_y))  8.26 us
    pallas_call x11, Pallas kernels, call(): pl.pallas_call(kernel, out_shape=outs, in_specs=vmem(len(args)), out_spec...  7.73 us
    ppermute x4, starting transfers between devices, per_device(): time_a = lax.ppermute(field, 'narrow', swap_pairs(narrow, 0))  3.51 us
    ppermute x4, starting transfers between devices, per_device(): time_b = lax.ppermute(field, 'narrow', swap_pairs(narrow, 1))  2.7 us
    unnamed x6, local copies, waits for them, and re-layouts  2.55 us
    ppermute x3, waiting for transfers between devices, per_device(): lax.ppermute(coarse, 'narrow', [(i, i ^ k) for i in range(narrow)])  2.18 us
  transfers between devices with their start and end apart: 19, of which 6 were waited for; matrix products, arithmetic and copies ran while one was open for 0% of the time, Pallas kernels for 5%

profile of v3, /device:TPU:0, one launch (start us, length us, event | category | flops | bytes accessed | tf_op | source)
XLA Modules:
  0.0 57.7 jit_solution(8145042644230301692)
XLA Ops:
  0.6 0.0 copy-start.2
  0.6 0.9 %copy-done.2 = f32[1,16,12,128]{3,1,2,0:T(8,128)S(1)} copy-done((f32[1,16,12,128]{3,1,2,0:T(8,128)S(1)}, f32[1,16,12,128]{3,1,2,0:T(8,128)}, u32[]{:S(2)}) %copy-start.2) | copy-done | bytes 98328
  1.5 0.1 shard_map.50
  1.6 2.5 %collective-permute-start.3 = (f32[192,128]{1,0:T(8,128)S(1)}, f32[192,128]{1,0:T(8,128)S(1)}, u32[]{:S(2)}, u32[]{:S(2)}) collective-permute-start(f32[192,128]{1,0:T(8,128)S(1)} %get-tuple-element.26.field_ref.refs_0_.refs_6_), channel_id=1, source_target_pairs={{1,2},{2,1},{3,0},{0,3},{5,6},{6,5},{7,4},{4,7},{9,10},{10,9},{11,... | collective-permute-start | bytes 294920 | tf_op jit(solution)/shard_map/ppermute | solution.py:476
  4.1 0.7 %collective-permute-start.2 = (f32[192,128]{1,0:T(8,128)S(1)}, f32[192,128]{1,0:T(8,128)S(1)}, u32[]{:S(2)}, u32[]{:S(2)}) collective-permute-start(f32[192,128]{1,0:T(8,128)S(1)} %get-tuple-element.26.field_ref.refs_0_.refs_6_), channel_id=1, source_target_pairs={{0,1},{1,0},{2,3},{3,2},{4,5},{5,4},{6,7},{7,6},{8,9},{9,8},{10,11... | collective-permute-start | bytes 294920 | tf_op jit(solution)/shard_map/ppermute | solution.py:477
  4.8 1.5 %collective-permute-start = (f32[96,128]{1,0:T(8,128)S(1)}, f32[96,128]{1,0:T(8,128)S(1)}, u32[]{:S(2)}, u32[]{:S(2)}) collective-permute-start(f32[96,128]{1,0:T(8,128)S(1)} %get-tuple-element.29), channel_id=1, source_target_pairs={{0,4},{4,0},{8,12},{12,8},{16,20},{20,16},{24,28},{28,24},{1,5},{5... | collective-permute-start | bytes 147464 | tf_op jit(solution)/shard_map/ppermute | solution.py:475
  6.2 3.6 %collective-permute-start.1 = (f32[96,128]{1,0:T(8,128)S(1)}, f32[96,128]{1,0:T(8,128)S(1)}, u32[]{:S(2)}, u32[]{:S(2)}) collective-permute-start(f32[96,128]{1,0:T(8,128)S(1)} %get-tuple-element.30), channel_id=1, source_target_pairs={{4,8},{8,4},{12,16},{16,12},{20,24},{24,20},{28,0},{0,28},{5,9},{9... | collective-permute-start | bytes 147464 | tf_op jit(solution)/shard_map/ppermute | solution.py:474
  9.8 0.0 copy-start
  9.8 1.7 %copy-done = bf16[1,16,9,64,128]{4,3,2,1,0:T(8,128)(2,1)S(1)} copy-done((bf16[1,16,9,64,128]{4,3,2,1,0:T(8,128)(2,1)S(1)}, bf16[1,16,9,64,128]{4,3,2,1,0:T(8,128)(2,1)}, u32[]{:S(2)}) %copy-start) | copy-done | bytes 2359320
  11.5 0.8 %shard_map.51 = (f32[192,128]{1,0:T(8,128)S(1)}, bf16[1,16,9,64,128]{4,3,2,1,0:T(8,128)(2,1)S(1)}) custom-call(f32[192,128]{1,0:T(8,128)S(1)} %get-tuple-element.26.field_ref.refs_0_.refs_6_, bf16[1,16,9,64,128]{4,3,2,1,0:T(8,128)(2,1)S(1)} %copy-done), custom_call_target="tpu_custom_call" | custom-call | tf_op jit(solution)/shard_map/pallas_call | solution.py:418
  12.3 0.0 collective-permute-done.refs_2_
  12.3 0.8 %collective-permute-done.1.refs_3_ = f32[96,128]{1,0:T(8,128)S(1)} collective-permute-done((f32[96,128]{1,0:T(8,128)S(1)}, f32[96,128]{1,0:T(8,128)S(1)}, u32[]{:S(2)}, u32[]{:S(2)}) %collective-permute-start.1) | collective-permute-done | bytes 49184 | tf_op jit(solution)/shard_map/ppermute | solution.py:474
  13.0 0.0 collective-permute-done.3.refs_5_
  13.0 0.0 collective-permute-done.2.refs_4_
  13.0 0.6 shard_map.52
  13.6 0.1 collective-permute-start.7
  13.7 0.6 %collective-permute-start.6 = (f32[192,128]{1,0:T(8,128)S(1)}, f32[192,128]{1,0:T(8,128)S(1)}, u32[]{:S(2)}, u32[]{:S(2)}) collective-permute-start(f32[192,128]{1,0:T(8,128)S(1)} %get-tuple-element.31.refs_1_.refs_7_), channel_id=1, source_target_pairs={{0,1},{1,0},{2,3},{3,2},{4,5},{5,4},{6,7},{7,6},{8,9},{9,8},{10,11... | collective-permute-start | bytes 294920 | tf_op jit(solution)/shard_map/ppermute | solution.py:477
  14.3 0.0 collective-permute-start.4
  14.3 3.6 %collective-permute-start.5 = (f32[96,128]{1,0:T(8,128)S(1)}, f32[96,128]{1,0:T(8,128)S(1)}, u32[]{:S(2)}, u32[]{:S(2)}) collective-permute-start(f32[96,128]{1,0:T(8,128)S(1)} %get-tuple-element.34), channel_id=1, source_target_pairs={{4,8},{8,4},{12,16},{16,12},{20,24},{24,20},{28,0},{0,28},{5,9},{9... | collective-permute-start | bytes 147464 | tf_op jit(solution)/shard_map/ppermute | solution.py:474
  17.9 0.7 %shard_map.53 = (f32[192,128]{1,0:T(8,128)S(1)}, f32[24,128]{1,0:T(8,128)S(1)}) custom-call(f32[192,128]{1,0:T(8,128)S(1)} %get-tuple-element.26.field_ref.refs_0_.refs_6_, f32[192,128]{1,0:T(8,128)S(1)} %get-tuple-element.31.refs_1_.refs_7_, bf16[1,16,9,64,128]{4,3,2,1,0:T(8,128)(2,1)S(1)} %get-tuple-element.28.refs_1_.refs_2_.refs_3_.refs_4_), custom_call_target="tpu_custom_call" | custom-call | tf_op jit(solution)/shard_map/pallas_call | solution.py:418
  18.5 0.0 collective-permute-done.4.refs_2_
  18.5 2.5 %collective-permute-done.5.refs_3_ = f32[96,128]{1,0:T(8,128)S(1)} collective-permute-done((f32[96,128]{1,0:T(8,128)S(1)}, f32[96,128]{1,0:T(8,128)S(1)}, u32[]{:S(2)}, u32[]{:S(2)}) %collective-permute-start.5) | collective-permute-done | bytes 49184 | tf_op jit(solution)/shard_map/ppermute | solution.py:474
  21.1 0.0 collective-permute-done.7.refs_5_
  21.1 0.0 collective-permute-done.6.refs_4_
  21.1 0.6 shard_map.54
  21.6 0.1 collective-permute-start.11
  21.7 1.6 %collective-permute-start.10 = (f32[192,128]{1,0:T(8,128)S(1)}, f32[192,128]{1,0:T(8,128)S(1)}, u32[]{:S(2)}, u32[]{:S(2)}) collective-permute-start(f32[192,128]{1,0:T(8,128)S(1)} %get-tuple-element.35.refs_2_.refs_8_), channel_id=1, source_target_pairs={{0,1},{1,0},{2,3},{3,2},{4,5},{5,4},{6,7},{7,6},{8,9},{9,8},{10,11... | collective-permute-start | bytes 294920 | tf_op jit(solution)/shard_map/ppermute | solution.py:477
  23.3 0.2 collective-permute-start.8
  23.6 3.6 %collective-permute-start.9 = (f32[96,128]{1,0:T(8,128)S(1)}, f32[96,128]{1,0:T(8,128)S(1)}, u32[]{:S(2)}, u32[]{:S(2)}) collective-permute-start(f32[96,128]{1,0:T(8,128)S(1)} %get-tuple-element.38), channel_id=1, source_target_pairs={{4,8},{8,4},{12,16},{16,12},{20,24},{24,20},{28,0},{0,28},{5,9},{9... | collective-permute-start | bytes 147464 | tf_op jit(solution)/shard_map/ppermute | solution.py:474
  27.1 0.7 %shard_map.55 = (f32[192,128]{1,0:T(8,128)S(1)}, f32[24,128]{1,0:T(8,128)S(1)}) custom-call(f32[192,128]{1,0:T(8,128)S(1)} %get-tuple-element.26.field_ref.refs_0_.refs_6_, f32[192,128]{1,0:T(8,128)S(1)} %get-tuple-element.31.refs_1_.refs_7_, f32[192,128]{1,0:T(8,128)S(1)} %get-tuple-element.35.refs_2_.refs_8_, ...), custom_call_target="tpu_custom_call" | custom-call | tf_op jit(solution)/shard_map/pallas_call | solution.py:418
  27.9 0.0 collective-permute-done.8.refs_2_
  27.9 2.5 %collective-permute-done.9.refs_3_ = f32[96,128]{1,0:T(8,128)S(1)} collective-permute-done((f32[96,128]{1,0:T(8,128)S(1)}, f32[96,128]{1,0:T(8,128)S(1)}, u32[]{:S(2)}, u32[]{:S(2)}) %collective-permute-start.9) | collective-permute-done | bytes 49184 | tf_op jit(solution)/shard_map/ppermute | solution.py:474
  30.4 0.0 collective-permute-done.11.refs_5_
  30.4 0.0 collective-permute-done.10.refs_4_
  30.4 0.6 shard_map.56
  30.9 0.1 collective-permute-start.15
  31.0 0.6 %collective-permute-start.14 = (f32[192,128]{1,0:T(8,128)S(1)}, f32[192,128]{1,0:T(8,128)S(1)}, u32[]{:S(2)}, u32[]{:S(2)}) collective-permute-start(f32[192,128]{1,0:T(8,128)S(1)} %get-tuple-element.39.refs_3_.refs_9_), channel_id=1, source_target_pairs={{0,1},{1,0},{2,3},{3,2},{4,5},{5,4},{6,7},{7,6},{8,9},{9,8},{10,11... | collective-permute-start | bytes 294920 | tf_op jit(solution)/shard_map/ppermute | solution.py:477
  31.6 0.0 collective-permute-start.12
  31.6 3.6 %collective-permute-start.13 = (f32[96,128]{1,0:T(8,128)S(1)}, f32[96,128]{1,0:T(8,128)S(1)}, u32[]{:S(2)}, u32[]{:S(2)}) collective-permute-start(f32[96,128]{1,0:T(8,128)S(1)} %get-tuple-element.42), channel_id=1, source_target_pairs={{4,8},{8,4},{12,16},{16,12},{20,24},{24,20},{28,0},{0,28},{5,9},{9... | collective-permute-start | bytes 147464 | tf_op jit(solution)/shard_map/ppermute | solution.py:474
  35.2 0.7 %shard_map.57 = (f32[192,128]{1,0:T(8,128)S(1)}, f32[24,128]{1,0:T(8,128)S(1)}) custom-call(f32[192,128]{1,0:T(8,128)S(1)} %get-tuple-element.26.field_ref.refs_0_.refs_6_, f32[192,128]{1,0:T(8,128)S(1)} %get-tuple-element.31.refs_1_.refs_7_, f32[192,128]{1,0:T(8,128)S(1)} %get-tuple-element.35.refs_2_.refs_8_, ...), custom_call_target="tpu_custom_call" | custom-call | tf_op jit(solution)/shard_map/pallas_call | solution.py:418
  35.9 0.0 copy-start.1
  35.9 0.0 collective-permute-done.12.refs_2_
  35.9 2.5 %collective-permute-done.13.refs_3_ = f32[96,128]{1,0:T(8,128)S(1)} collective-permute-done((f32[96,128]{1,0:T(8,128)S(1)}, f32[96,128]{1,0:T(8,128)S(1)}, u32[]{:S(2)}, u32[]{:S(2)}) %collective-permute-start.13) | collective-permute-done | bytes 49184 | tf_op jit(solution)/shard_map/ppermute | solution.py:474
  38.4 0.0 collective-permute-done.15.refs_5_
  38.4 0.0 collective-permute-done.14.refs_4_
  38.4 0.8 %shard_map.58 = (f32[192,128]{1,0:T(8,128)S(1)}, f32[3,128]{1,0:T(4,128)S(1)}) custom-call(f32[192,128]{1,0:T(8,128)S(1)} %get-tuple-element.40.refs_0_, bf16[1,16,9,64,128]{4,3,2,1,0:T(8,128)(2,1)S(1)} %get-tuple-element.28.refs_1_.refs_2_.refs_3_.refs_4_, f32[96,128]{1,0:T(8,128)S(1)} %collective-permute-done.12.refs_2_, ...), custom_call_target="tpu_custom_call" | custom-call | tf_op jit(solution)/shard_map/pallas_call | solution.py:418
  39.2 12.1 %all_to_all.5 = f32[32,3,128]{2,1,0:T(4,128)S(1)} all-to-all(f32[32,3,128]{2,1,0:T(4,128)S(1)} %broadcast_in_dim.4), channel_id=1, replica_groups=mesh['wide'=8,'narrow'=4] {'wide','narrow'}, dimensions={0} | all-to-all | bytes 98304 | tf_op jit(solution)/shard_map/all_to_all | solution.py:518
  51.3 0.0 copy-done.1
  51.3 1.7 %shard_map.59 = (f32[192,128]{1,0:T(8,128)}, f32[48,128]{1,0:T(8,128)S(1)}) custom-call(f32[192,128]{1,0:T(8,128)S(1)} %get-tuple-element.26.field_ref.refs_0_.refs_6_, f32[192,128]{1,0:T(8,128)S(1)} %get-tuple-element.31.refs_1_.refs_7_, f32[192,128]{1,0:T(8,128)S(1)} %get-tuple-element.35.refs_2_.refs_8_, ...), custom_call_target="tpu_custom_call" | custom-call | tf_op jit(solution)/shard_map/pallas_call | solution.py:418
  53.0 0.2 collective-permute-start.18
  53.2 1.6 %collective-permute-start.17 = (f32[48,128]{1,0:T(8,128)S(1)}, f32[48,128]{1,0:T(8,128)S(1)}, u32[]{:S(2)}, u32[]{:S(2)}) collective-permute-start(f32[48,128]{1,0:T(8,128)S(1)} %get-tuple-element.49.own_ref), channel_id=1, source_target_pairs={{0,2},{1,3},{2,0},{3,1},{4,6},{5,7},{6,4},{7,5},{8,10},{9,11},{10,... | collective-permute-start | bytes 73736 | tf_op jit(solution)/shard_map/ppermute | solution.py:538
  54.8 0.1 collective-permute-start.16
  54.9 1.4 %collective-permute-done.18.refs_2_ = f32[48,128]{1,0:T(8,128)S(1)} collective-permute-done((f32[48,128]{1,0:T(8,128)S(1)}, f32[48,128]{1,0:T(8,128)S(1)}, u32[]{:S(2)}, u32[]{:S(2)}) %collective-permute-start.18) | collective-permute-done | bytes 24608 | tf_op jit(solution)/shard_map/ppermute | solution.py:538
  56.3 0.8 %collective-permute-done.17.refs_1_ = f32[48,128]{1,0:T(8,128)S(1)} collective-permute-done((f32[48,128]{1,0:T(8,128)S(1)}, f32[48,128]{1,0:T(8,128)S(1)}, u32[]{:S(2)}, u32[]{:S(2)}) %collective-permute-start.17) | collective-permute-done | bytes 24608 | tf_op jit(solution)/shard_map/ppermute | solution.py:538
  57.1 0.0 collective-permute-done.16.refs_0_
  57.1 0.7 %shard_map.60 = f32[4,48,128]{2,1,0:T(8,128)} custom-call(f32[48,128]{1,0:T(8,128)S(1)} %get-tuple-element.49.own_ref, f32[48,128]{1,0:T(8,128)S(1)} %collective-permute-done.16.refs_0_, f32[48,128]{1,0:T(8,128)S(1)} %collective-permute-done.17.refs_1_, f32[48,128]{1,0:T(8,128)S(1)} %collective-permute-done.18.refs_2_), custom_call_target="tpu_custom_call" | custom-call | tf_op jit(solution)/shard_map/pallas_call | solution.py:418
  (2 shorter events, 0.1 us)
Async XLA Ops:
  0.6 0.9 %copy-start.2 = (f32[1,16,12,128]{3,1,2,0:T(8,128)S(1)}, f32[1,16,12,128]{3,1,2,0:T(8,128)}, u32[]{:S(2)}) copy-start(f32[1,16,12,128]{3,1,2,0:T(8,128)} %param.3) | copy-start | bytes 294916
  1.6 11.5 %collective-permute-start.3 = (f32[192,128]{1,0:T(8,128)S(1)}, f32[192,128]{1,0:T(8,128)S(1)}, u32[]{:S(2)}, u32[]{:S(2)}) collective-permute-start(f32[192,128]{1,0:T(8,128)S(1)} %get-tuple-element.26.field_ref.refs_0_.refs_6_), channel_id=1, source_target_pairs={{1,2},{2,1},{3,0},{0,3},{5,6},{6,5},{7,4},{4,7},{9,10},{10,9},{11,... | collective-permute-start | bytes 294920 | tf_op jit(solution)/shard_map/ppermute | solution.py:476
  4.1 9.0 %collective-permute-start.2 = (f32[192,128]{1,0:T(8,128)S(1)}, f32[192,128]{1,0:T(8,128)S(1)}, u32[]{:S(2)}, u32[]{:S(2)}) collective-permute-start(f32[192,128]{1,0:T(8,128)S(1)} %get-tuple-element.26.field_ref.refs_0_.refs_6_), channel_id=1, source_target_pairs={{0,1},{1,0},{2,3},{3,2},{4,5},{5,4},{6,7},{7,6},{8,9},{9,8},{10,11... | collective-permute-start | bytes 294920 | tf_op jit(solution)/shard_map/ppermute | solution.py:477
  4.8 7.5 %collective-permute-start = (f32[96,128]{1,0:T(8,128)S(1)}, f32[96,128]{1,0:T(8,128)S(1)}, u32[]{:S(2)}, u32[]{:S(2)}) collective-permute-start(f32[96,128]{1,0:T(8,128)S(1)} %get-tuple-element.29), channel_id=1, source_target_pairs={{0,4},{4,0},{8,12},{12,8},{16,20},{20,16},{24,28},{28,24},{1,5},{5... | collective-permute-start | bytes 147464 | tf_op jit(solution)/shard_map/ppermute | solution.py:475
  6.2 6.8 %collective-permute-start.1 = (f32[96,128]{1,0:T(8,128)S(1)}, f32[96,128]{1,0:T(8,128)S(1)}, u32[]{:S(2)}, u32[]{:S(2)}) collective-permute-start(f32[96,128]{1,0:T(8,128)S(1)} %get-tuple-element.30), channel_id=1, source_target_pairs={{4,8},{8,4},{12,16},{16,12},{20,24},{24,20},{28,0},{0,28},{5,9},{9... | collective-permute-start | bytes 147464 | tf_op jit(solution)/shard_map/ppermute | solution.py:474
  9.8 1.7 %copy-start = (bf16[1,16,9,64,128]{4,3,2,1,0:T(8,128)(2,1)S(1)}, bf16[1,16,9,64,128]{4,3,2,1,0:T(8,128)(2,1)}, u32[]{:S(2)}) copy-start(bf16[1,16,9,64,128]{4,3,2,1,0:T(8,128)(2,1)} %hops_ref.1) | copy-start | bytes 7077892
  13.6 7.5 %collective-permute-start.7 = (f32[192,128]{1,0:T(8,128)S(1)}, f32[192,128]{1,0:T(8,128)S(1)}, u32[]{:S(2)}, u32[]{:S(2)}) collective-permute-start(f32[192,128]{1,0:T(8,128)S(1)} %get-tuple-element.31.refs_1_.refs_7_), channel_id=1, source_target_pairs={{1,2},{2,1},{3,0},{0,3},{5,6},{6,5},{7,4},{4,7},{9,10},{10,9},{11,... | collective-permute-start | bytes 294920 | tf_op jit(solution)/shard_map/ppermute | solution.py:476
  13.7 7.4 %collective-permute-start.6 = (f32[192,128]{1,0:T(8,128)S(1)}, f32[192,128]{1,0:T(8,128)S(1)}, u32[]{:S(2)}, u32[]{:S(2)}) collective-permute-start(f32[192,128]{1,0:T(8,128)S(1)} %get-tuple-element.31.refs_1_.refs_7_), channel_id=1, source_target_pairs={{0,1},{1,0},{2,3},{3,2},{4,5},{5,4},{6,7},{7,6},{8,9},{9,8},{10,11... | collective-permute-start | bytes 294920 | tf_op jit(solution)/shard_map/ppermute | solution.py:477
  14.3 4.3 %collective-permute-start.4 = (f32[96,128]{1,0:T(8,128)S(1)}, f32[96,128]{1,0:T(8,128)S(1)}, u32[]{:S(2)}, u32[]{:S(2)}) collective-permute-start(f32[96,128]{1,0:T(8,128)S(1)} %get-tuple-element.33), channel_id=1, source_target_pairs={{0,4},{4,0},{8,12},{12,8},{16,20},{20,16},{24,28},{28,24},{1,5},{5... | collective-permute-start | bytes 147464 | tf_op jit(solution)/shard_map/ppermute | solution.py:475
  14.3 6.8 %collective-permute-start.5 = (f32[96,128]{1,0:T(8,128)S(1)}, f32[96,128]{1,0:T(8,128)S(1)}, u32[]{:S(2)}, u32[]{:S(2)}) collective-permute-start(f32[96,128]{1,0:T(8,128)S(1)} %get-tuple-element.34), channel_id=1, source_target_pairs={{4,8},{8,4},{12,16},{16,12},{20,24},{24,20},{28,0},{0,28},{5,9},{9... | collective-permute-start | bytes 147464 | tf_op jit(solution)/shard_map/ppermute | solution.py:474
  21.6 8.7 %collective-permute-start.11 = (f32[192,128]{1,0:T(8,128)S(1)}, f32[192,128]{1,0:T(8,128)S(1)}, u32[]{:S(2)}, u32[]{:S(2)}) collective-permute-start(f32[192,128]{1,0:T(8,128)S(1)} %get-tuple-element.35.refs_2_.refs_8_), channel_id=1, source_target_pairs={{1,2},{2,1},{3,0},{0,3},{5,6},{6,5},{7,4},{4,7},{9,10},{10,9},{11,... | collective-permute-start | bytes 294920 | tf_op jit(solution)/shard_map/ppermute | solution.py:476
  21.7 8.6 %collective-permute-start.10 = (f32[192,128]{1,0:T(8,128)S(1)}, f32[192,128]{1,0:T(8,128)S(1)}, u32[]{:S(2)}, u32[]{:S(2)}) collective-permute-start(f32[192,128]{1,0:T(8,128)S(1)} %get-tuple-element.35.refs_2_.refs_8_), channel_id=1, source_target_pairs={{0,1},{1,0},{2,3},{3,2},{4,5},{5,4},{6,7},{7,6},{8,9},{9,8},{10,11... | collective-permute-start | bytes 294920 | tf_op jit(solution)/shard_map/ppermute | solution.py:477
  23.3 4.5 %collective-permute-start.8 = (f32[96,128]{1,0:T(8,128)S(1)}, f32[96,128]{1,0:T(8,128)S(1)}, u32[]{:S(2)}, u32[]{:S(2)}) collective-permute-start(f32[96,128]{1,0:T(8,128)S(1)} %get-tuple-element.37), channel_id=1, source_target_pairs={{0,4},{4,0},{8,12},{12,8},{16,20},{20,16},{24,28},{28,24},{1,5},{5... | collective-permute-start | bytes 147464 | tf_op jit(solution)/shard_map/ppermute | solution.py:475
  23.6 6.8 %collective-permute-start.9 = (f32[96,128]{1,0:T(8,128)S(1)}, f32[96,128]{1,0:T(8,128)S(1)}, u32[]{:S(2)}, u32[]{:S(2)}) collective-permute-start(f32[96,128]{1,0:T(8,128)S(1)} %get-tuple-element.38), channel_id=1, source_target_pairs={{4,8},{8,4},{12,16},{16,12},{20,24},{24,20},{28,0},{0,28},{5,9},{9... | collective-permute-start | bytes 147464 | tf_op jit(solution)/shard_map/ppermute | solution.py:474
  30.9 7.5 %collective-permute-start.15 = (f32[192,128]{1,0:T(8,128)S(1)}, f32[192,128]{1,0:T(8,128)S(1)}, u32[]{:S(2)}, u32[]{:S(2)}) collective-permute-start(f32[192,128]{1,0:T(8,128)S(1)} %get-tuple-element.39.refs_3_.refs_9_), channel_id=1, source_target_pairs={{1,2},{2,1},{3,0},{0,3},{5,6},{6,5},{7,4},{4,7},{9,10},{10,9},{11,... | collective-permute-start | bytes 294920 | tf_op jit(solution)/shard_map/ppermute | solution.py:476
  31.0 7.4 %collective-permute-start.14 = (f32[192,128]{1,0:T(8,128)S(1)}, f32[192,128]{1,0:T(8,128)S(1)}, u32[]{:S(2)}, u32[]{:S(2)}) collective-permute-start(f32[192,128]{1,0:T(8,128)S(1)} %get-tuple-element.39.refs_3_.refs_9_), channel_id=1, source_target_pairs={{0,1},{1,0},{2,3},{3,2},{4,5},{5,4},{6,7},{7,6},{8,9},{9,8},{10,11... | collective-permute-start | bytes 294920 | tf_op jit(solution)/shard_map/ppermute | solution.py:477
  31.6 4.3 %collective-permute-start.12 = (f32[96,128]{1,0:T(8,128)S(1)}, f32[96,128]{1,0:T(8,128)S(1)}, u32[]{:S(2)}, u32[]{:S(2)}) collective-permute-start(f32[96,128]{1,0:T(8,128)S(1)} %get-tuple-element.41), channel_id=1, source_target_pairs={{0,4},{4,0},{8,12},{12,8},{16,20},{20,16},{24,28},{28,24},{1,5},{5... | collective-permute-start | bytes 147464 | tf_op jit(solution)/shard_map/ppermute | solution.py:475
  31.6 6.8 %collective-permute-start.13 = (f32[96,128]{1,0:T(8,128)S(1)}, f32[96,128]{1,0:T(8,128)S(1)}, u32[]{:S(2)}, u32[]{:S(2)}) collective-permute-start(f32[96,128]{1,0:T(8,128)S(1)} %get-tuple-element.42), channel_id=1, source_target_pairs={{4,8},{8,4},{12,16},{16,12},{20,24},{24,20},{28,0},{0,28},{5,9},{9... | collective-permute-start | bytes 147464 | tf_op jit(solution)/shard_map/ppermute | solution.py:474
  35.9 15.4 %copy-start.1 = (f32[1,16,64,128]{3,2,1,0:T(8,128)S(1)}, f32[1,16,64,128]{3,2,1,0:T(8,128)}, u32[]{:S(2)}) copy-start(f32[1,16,64,128]{3,2,1,0:T(8,128)} %param.5) | copy-start | bytes 1572868
  53.0 3.3 %collective-permute-start.18 = (f32[48,128]{1,0:T(8,128)S(1)}, f32[48,128]{1,0:T(8,128)S(1)}, u32[]{:S(2)}, u32[]{:S(2)}) collective-permute-start(f32[48,128]{1,0:T(8,128)S(1)} %get-tuple-element.49.own_ref), channel_id=1, source_target_pairs={{0,3},{1,2},{2,1},{3,0},{4,7},{5,6},{6,5},{7,4},{8,11},{9,10},{10,... | collective-permute-start | bytes 73736 | tf_op jit(solution)/shard_map/ppermute | solution.py:538
  53.2 3.9 %collective-permute-start.17 = (f32[48,128]{1,0:T(8,128)S(1)}, f32[48,128]{1,0:T(8,128)S(1)}, u32[]{:S(2)}, u32[]{:S(2)}) collective-permute-start(f32[48,128]{1,0:T(8,128)S(1)} %get-tuple-element.49.own_ref), channel_id=1, source_target_pairs={{0,2},{1,3},{2,0},{3,1},{4,6},{5,7},{6,4},{7,5},{8,10},{9,11},{10,... | collective-permute-start | bytes 73736 | tf_op jit(solution)/shard_map/ppermute | solution.py:538
  54.8 2.3 %collective-permute-start.16 = (f32[48,128]{1,0:T(8,128)S(1)}, f32[48,128]{1,0:T(8,128)S(1)}, u32[]{:S(2)}, u32[]{:S(2)}) collective-permute-start(f32[48,128]{1,0:T(8,128)S(1)} %get-tuple-element.49.own_ref), channel_id=1, source_target_pairs={{0,1},{1,0},{2,3},{3,2},{4,5},{5,4},{6,7},{7,6},{8,9},{9,8},{10,11... | collective-permute-start | bytes 73736 | tf_op jit(solution)/shard_map/ppermute | solution.py:538

commit v4 on v3

--- a/solution.py
+++ b/solution.py
@@ -12,6 +12,7 @@
 YLOC = 2
 LY = 16
 STEP_SCALE = 0.25
+FIRST_SEND = 3
 LANES_EACH = 8
 SLOT = 32
 VMEM_LIMIT = 24 * 1024 * 1024
@@ -129,6 +130,33 @@
     return out
 
 
+def restrict_field(field_ref, restriction, depth, rhs, out_ref, base):
+    width = field_ref.shape[-1]
+    sign = lane_sign(width)
+    extent = restriction.shape[0] // depth
+    for cell in range(extent // 2):
+        lefts = []
+        rights = []
+        for y in range(depth):
+            for site in (y * extent + 2 * cell, y * extent + 2 * cell + 1):
+                block = load_site(field_ref, site, 0, rhs, False)
+                turned = pltpu.roll(block, width // 2, 1)
+                lefts.append(jnp.concatenate([block * sign, turned], 0))
+                rights.append(restriction[site])
+        total = lax.dot_general(
+            jnp.concatenate(lefts, -1),
+            jnp.concatenate(rights, -1),
+            (((1,), (1,)), ((), ())),
+            precision=lax.Precision.HIGHEST,
+            preferred_element_type=jnp.float32,
+        )
+        half = total.shape[0] // 2
+        value = jnp.concatenate([total[:half], total[half:]], -1)
+        for at, start in enumerate(tile_starts(rhs)):
+            row = base + cell * rhs + start
+            out_ref[row : row + 8, :] = value[8 * at : 8 * at + 8]
+
+
 def near_sites(hops_ref, table, near_ref, depth, rhs, wrap_z, ready):
     sites = hops_ref.shape[1]
     extent = sites // depth
@@ -166,22 +194,31 @@
     down_ref[...] = jnp.where(odd, last, first)
 
 
-def first_near_kernel(depth, rhs, wrap_z, field_ref, hops_ref, near_ref, kept_ref, table):
-    sites = hops_ref.shape[1]
-    prepare(field_ref, table, 0, sites, rhs, False)
-
-    def keep(site):
-        kept_ref[0, site] = hops_ref[0, site]
-
-    near_sites(hops_ref, table, near_ref, depth, rhs, wrap_z, keep)
-
-
 def near_kernel(power, depth, rhs, wrap_z, *refs):
     fields = refs[: power + 1]
-    hops_ref, near_ref, gram_ref, table = refs[power + 1 :]
+    hops_ref = refs[power + 1]
+    if power:
+        near_ref, coarse_ref, other_ref, table = refs[-4:]
+    else:
+        near_ref, other_ref, table = refs[-3:]
     prepare(fields[power], table, 0, hops_ref.shape[1], rhs, False)
-    near_sites(hops_ref, table, near_ref, depth, rhs, wrap_z, lambda site: None)
-    gram_ref[...] = gram_columns(power, fields, gram_ref.shape[0])
+
+    def keep(site):
+        if power == 0:
+            other_ref[0, site] = hops_ref[0, site]
+
+    near_sites(hops_ref, table, near_ref, depth, rhs, wrap_z, keep)
+    if power:
+        restriction = refs[power + 2]
+        earlier = refs[power + 3 : -4]
+        base = 0
+        for ref in earlier:
+            coarse_ref[base : base + ref.shape[0], :] = ref[...]
+            base += ref.shape[0]
+        for field_ref in fields if power == 1 else fields[power:]:
+            restrict_field(field_ref, restriction, depth, rhs, coarse_ref, base)
+            base += restriction.shape[0] // depth // 2 * rhs
+        other_ref[...] = gram_columns(power, fields, other_ref.shape[0])
 
 
 def far_kernel(depth, rhs, wrap_z, last, *refs):
@@ -242,7 +279,12 @@
         summed = spread[q * per_row : q * per_row + 1]
         for m in range(1, min(per_row, rhs - q * per_row)):
             summed = summed + spread[q * per_row + m : q * per_row + m + 1]
-        out_ref[q : q + 1, :] = summed
+        for copy in range(out_ref.shape[0]):
+            out_ref[copy, q : q + 1, :] = summed
+
+
+def tail_kernel(depth, rhs, field_ref, restriction, coarse_ref):
+    restrict_field(field_ref, restriction, depth, rhs, coarse_ref, 0)
 
 
 def cmulc(a, b):
@@ -304,10 +346,11 @@
     return coeffs, combined
 
 
-def final_kernel(depth, rhs, *refs):
-    fields = refs[: ITERS + 1]
-    packed, restriction = refs[ITERS + 1 : ITERS + 3]
-    sol_ref, coarse_ref, res_ref, kept_ref, turn_ref, line_ref, rows_ref = refs[ITERS + 3 :]
+def final_kernel(sites, rhs, groups, *refs):
+    fields = refs[:ITERS]
+    packed = refs[ITERS]
+    coarse_refs = refs[ITERS + 1 : -7]
+    sol_ref, coarse_ref, kept_ref, slice_ref, turn_ref, line_ref, rows_ref = refs[-7:]
     width = fields[0].shape[-1]
     total_rows = fields[0].shape[0]
     period = rhs
@@ -355,58 +398,42 @@
     columns = rows_ref[...]
     spread = [jnp.broadcast_to(columns[:, at : at + 1], (period, width)) for at in range(len(parts))]
     sign = lane_sign(width)
+    half_width = width // 2
     for base in range(0, total_rows, period):
-        res = fields[0][base : base + period, :]
-        res_turn = None
-        sol = None
-        sol_turn = None
-        for i in range(ITERS + 1):
+        straight = None
+        across = None
+        for i in range(ITERS):
             value = fields[i][base : base + period, :]
-            if i:
-                at = 2 * (i - 1)
-                res = res + spread[at] * value
-                term = spread[at + 1] * value
-                res_turn = term if res_turn is None else res_turn + term
-            if i < ITERS:
-                at = 2 * ITERS + 2 * i
-                term = spread[at] * value
-                sol = term if sol is None else sol + term
-                term = spread[at + 1] * value
-                sol_turn = term if sol_turn is None else sol_turn + term
-        res_ref[base : base + period, :] = res - sign * pltpu.roll(res_turn, width // 2, 1)
-        kept_ref[base : base + period, :] = sol - sign * pltpu.roll(sol_turn, width // 2, 1)
-    sites = restriction.shape[0]
-    extent = sites // depth
-    cells = extent // 2
-    for cell in range(cells):
-        lefts = []
-        rights = []
-        for y in range(depth):
-            for site in (y * extent + 2 * cell, y * extent + 2 * cell + 1):
-                block = load_site(res_ref, site, sites, rhs, False)
-                turned = pltpu.roll(block, width // 2, 1)
-                lefts.append(jnp.concatenate([block * sign, turned], 0))
-                rights.append(restriction[site])
-        total = lax.dot_general(
-            jnp.concatenate(lefts, -1),
-            jnp.concatenate(rights, -1),
-            (((1,), (1,)), ((), ())),
-            precision=lax.Precision.HIGHEST,
-            preferred_element_type=jnp.float32,
-        )
-        half = total.shape[0] // 2
-        value = jnp.concatenate([total[:half], total[half:]], -1)
-        store_site(coarse_ref, cell, cells, rhs, value, True)
+            at = 2 * ITERS + 2 * i
+            terms = (spread[at] * value, spread[at + 1] * value)
+            straight = terms[0] if straight is None else straight + terms[0]
+            across = terms[1] if across is None else across + terms[1]
+        kept_ref[base : base + period, :] = straight - sign * pltpu.roll(across, half_width, 1)
     for site in range(sites):
         store_site(sol_ref, site, sites, rhs, load_site(kept_ref, site, sites, rhs, False), True)
-
-
-def assemble_kernel(own_ref, *refs):
-    out_ref = refs[-1]
     me = lax.axis_index("narrow")
-    out_ref[me] = own_ref[...]
-    for k, ref in enumerate(refs[:-1]):
-        out_ref[jnp.bitwise_xor(me, k + 1)] = ref[...]
+    slice_rows = slice_ref.shape[0]
+    cells = slice_rows // rhs
+    count = len(groups)
+    for k in range(len(coarse_refs) // count):
+        mine = coarse_refs[k * count : (k + 1) * count]
+        placed = [(ref, part) for ref, stack in zip(mine, groups) for part in range(stack)]
+        for base in range(0, slice_rows, period):
+            straight = None
+            across = None
+            for i, (ref, part) in enumerate(placed):
+                row = part * slice_rows + base
+                value = ref[row : row + period, :]
+                if i == 0:
+                    straight = value
+                    continue
+                terms = (spread[2 * i - 2] * value, spread[2 * i - 1] * value)
+                straight = straight + terms[0]
+                across = terms[1] if across is None else across + terms[1]
+            slice_ref[base : base + period, :] = straight - sign * pltpu.roll(across, half_width, 1)
+        target = coarse_ref.at[jnp.bitwise_xor(me, k)]
+        for cell in range(cells):
+            store_site(target, cell, cells, rhs, load_site(slice_ref, cell, cells, rhs, False), True)
 
 
 def vmem(count):
@@ -468,6 +495,18 @@
     )
     fields = [field]
     grams = []
+    waiting = []
+    sent = []
+    groups = []
+    cells = extent // 2
+    coarse_rows = cells * rhs
+
+    def to_all_times(value):
+        arrived = [value]
+        for k in range(narrow - 1, 0, -1):
+            arrived.insert(1, lax.ppermute(value, "narrow", [(i, i ^ k) for i in range(narrow)]))
+        return arrived
+
     hops = None
     table = pltpu.VMEM((sites, 4 * tile_rows, width), jnp.bfloat16)
     for power in range(ITERS):
@@ -480,21 +519,29 @@
             received += [lax.ppermute(field, "wide", down_z), lax.ppermute(field, "wide", up_z)]
         if power == 0:
             near, hops = call(
-                functools.partial(first_near_kernel, YLOC, rhs, wrap_z),
+                functools.partial(near_kernel, power, YLOC, rhs, wrap_z),
                 [field_shape, jax.ShapeDtypeStruct(hop_blocks.shape, hop_blocks.dtype)],
                 field,
                 hop_blocks,
                 scratch=[table],
             )
         else:
-            near, gram = call(
+            stacked = sum(ref.shape[0] for ref in waiting) + coarse_rows * (2 if power == 1 else 1)
+            near, coarse, gram = call(
                 functools.partial(near_kernel, power, YLOC, rhs, wrap_z),
-                [field_shape, gram_shape],
+                [field_shape, jax.ShapeDtypeStruct((stacked, width), f32), gram_shape],
                 *fields,
                 hops,
+                restriction[0],
+                *waiting,
                 scratch=[table],
             )
             grams.append(gram)
+            waiting = [coarse]
+            if power >= FIRST_SEND:
+                groups.append(stacked // coarse_rows)
+                sent.append(to_all_times(coarse))
+                waiting = []
         last = power + 1 == ITERS
         slots = 2 * sites + 2 * extent + (0 if wrap_z else 2 * sites)
         per_row = width // SLOT
@@ -502,7 +549,11 @@
         outs = call(
             functools.partial(far_kernel, YLOC, rhs, wrap_z, last),
             [field_shape]
-            + ([jax.ShapeDtypeStruct((packed_rows, width), f32)] if last else [half_shape] * 2),
+            + (
+                [jax.ShapeDtypeStruct((wide * narrow, packed_rows, width), f32)]
+                if last
+                else [half_shape] * 2
+            ),
             near,
             hops,
             *received,
@@ -513,31 +564,31 @@
         fields.append(field)
         if not last:
             up_send, down_send = outs[1:]
-    packed = outs[1]
-    copies = jnp.broadcast_to(packed[None], (wide * narrow, packed_rows, width))
-    swapped = lax.all_to_all(copies, ("wide", "narrow"), 0, 0)
+        else:
+            swapped = lax.all_to_all(outs[1], ("wide", "narrow"), 0, 0)
+            coarse = call(
+                functools.partial(tail_kernel, YLOC, rhs),
+                jax.ShapeDtypeStruct((coarse_rows, width), f32),
+                field,
+                restriction[0],
+            )
+            groups.append(1)
+            sent.append(to_all_times(coarse))
     totals = jnp.sum(swapped, axis=0)
-    cells = extent // 2
     square = pltpu.VMEM((width, width), f32)
-    solution_rows, coarse = call(
-        functools.partial(final_kernel, YLOC, rhs),
-        [field_shape, jax.ShapeDtypeStruct((rhs * cells, width), f32)],
-        *fields,
+    solution_rows, slices = call(
+        functools.partial(final_kernel, sites, rhs, tuple(groups)),
+        [field_shape, jax.ShapeDtypeStruct((narrow, coarse_rows, width), f32)],
+        *fields[:ITERS],
         totals,
-        restriction[0],
+        *[arrived[k] for k in range(narrow) for arrived in sent],
         scratch=[
             pltpu.VMEM((total_rows, width), f32),
-            pltpu.VMEM((total_rows, width), f32),
+            pltpu.VMEM((coarse_rows, width), f32),
             square,
             square,
             pltpu.VMEM((period, width), f32),
         ],
-    )
-    others = []
-    for k in range(1, narrow):
-        others.append(lax.ppermute(coarse, "narrow", [(i, i ^ k) for i in range(narrow)]))
-    slices = call(
-        assemble_kernel, jax.ShapeDtypeStruct((narrow,) + coarse.shape, f32), coarse, *others
     )
     coarse_residual = jnp.transpose(slices.reshape(narrow, rhs, cells, width), (0, 2, 1, 3))
     solution_field = jnp.transpose(solution_rows.reshape(rhs, sites, width), (1, 0, 2))

time: 57.9 us -> 53.8 us (0.929)
  blocking collectives: 12.1 us -> 0 us
  starting transfers between devices: 24.1 us -> 30.9 us
  Pallas kernels: 7.73 us -> 9.4 us
    all_to_all x1 -> x0, blocking collectives: 12.1 us -> none  [per_device(): swapped = lax.all_to_all(copies, ('wide', 'narrow'), 0, 0)]
    all_to_all x0 -> x1, starting transfers between devices: none -> 5 us  [per_device(): swapped = lax.all_to_all(outs[1], ('wide', 'narrow'), 0, 0)]
    all_to_all x0 -> x1, waiting for transfers between devices: none -> 4.85 us  [per_device(): swapped = lax.all_to_all(outs[1], ('wide', 'narrow'), 0, 0)]
    ppermute x4, waiting for transfers between devices: 8.26 us -> 5.05 us  [per_device(): side_b = lax.ppermute(down_send, 'wide', swap_pairs(wide, 1, rows_y))]
    ppermute x3 -> x6, waiting for transfers between devices: 2.18 us -> 0.02 us  [to_all_times(): lax.ppermute(value, 'narrow', [(i, i ^ k) for i in range(narrow)])]
    ppermute x3 -> x6, starting transfers between devices: 1.86 us -> 3.65 us  [to_all_times(): lax.ppermute(value, 'narrow', [(i, i ^ k) for i in range(narrow)])]
    pallas_call x11, Pallas kernels: 7.73 us -> 9.4 us  [call(): pl.pallas_call(kernel, out_shape=outs, in_specs=vmem(len(args)), out_spec...]
  transfers between devices with their start and end apart: 19 -> 23, of which waited for: 6 -> 5; matrix products, arithmetic and copies ran while one was open for 0% -> 0% of each run, Pallas kernels for 5% -> 12%
where the time goes in v4:
time: 53.8 us; the launch traced here: 53.6 us
  starting transfers between devices  30.9 us (57%)
  waiting for transfers between devices  9.99 us (19%)
  Pallas kernels  9.4 us (17%)
  local copies, waits for them, and re-layouts  2.55 us (5%)
  between operations  0.76 us (1%)
    ppermute x4, starting transfers between devices, per_device(): side_b = lax.ppermute(down_send, 'wide', swap_pairs(wide, 1, rows_y))  14.3 us
    pallas_call x11, Pallas kernels, call(): pl.pallas_call(kernel, out_shape=outs, in_specs=vmem(len(args)), out_spec...  9.4 us
    ppermute x4, waiting for transfers between devices, per_device(): side_b = lax.ppermute(down_send, 'wide', swap_pairs(wide, 1, rows_y))  5.05 us
    all_to_all x1, starting transfers between devices, per_device(): swapped = lax.all_to_all(outs[1], ('wide', 'narrow'), 0, 0)  5 us
    all_to_all x1, waiting for transfers between devices, per_device(): swapped = lax.all_to_all(outs[1], ('wide', 'narrow'), 0, 0)  4.85 us
    ppermute x6, starting transfers between devices, to_all_times(): lax.ppermute(value, 'narrow', [(i, i ^ k) for i in range(narrow)])  3.65 us
    ppermute x4, starting transfers between devices, per_device(): time_a = lax.ppermute(field, 'narrow', swap_pairs(narrow, 0))  3.51 us
    ppermute x4, starting transfers between devices, per_device(): time_b = lax.ppermute(field, 'narrow', swap_pairs(narrow, 1))  2.7 us
  transfers between devices with their start and end apart: 23, of which 5 were waited for; matrix products, arithmetic and copies ran while one was open for 0% of the time, Pallas kernels for 12%

profile of v4, /device:TPU:0, one launch (start us, length us, event | category | flops | bytes accessed | tf_op | source)
XLA Modules:
  0.0 53.6 jit_solution(11256289506026656205)
XLA Ops:
  0.6 0.0 copy-start.2
  0.6 0.9 %copy-done.2 = f32[1,16,12,128]{3,1,2,0:T(8,128)S(1)} copy-done((f32[1,16,12,128]{3,1,2,0:T(8,128)S(1)}, f32[1,16,12,128]{3,1,2,0:T(8,128)}, u32[]{:S(2)}) %copy-start.2) | copy-done | bytes 98328
  1.5 0.1 shard_map.50
  1.6 2.5 %collective-permute-start.3 = (f32[192,128]{1,0:T(8,128)S(1)}, f32[192,128]{1,0:T(8,128)S(1)}, u32[]{:S(2)}, u32[]{:S(2)}) collective-permute-start(f32[192,128]{1,0:T(8,128)S(1)} %get-tuple-element.29.refs_0_.refs_6_), channel_id=1, source_target_pairs={{1,2},{2,1},{3,0},{0,3},{5,6},{6,5},{7,4},{4,7},{9,10},{10,9},{11,... | collective-permute-start | bytes 294920 | tf_op jit(solution)/shard_map/ppermute | solution.py:515
  4.1 0.7 %collective-permute-start.2 = (f32[192,128]{1,0:T(8,128)S(1)}, f32[192,128]{1,0:T(8,128)S(1)}, u32[]{:S(2)}, u32[]{:S(2)}) collective-permute-start(f32[192,128]{1,0:T(8,128)S(1)} %get-tuple-element.29.refs_0_.refs_6_), channel_id=1, source_target_pairs={{0,1},{1,0},{2,3},{3,2},{4,5},{5,4},{6,7},{7,6},{8,9},{9,8},{10,11... | collective-permute-start | bytes 294920 | tf_op jit(solution)/shard_map/ppermute | solution.py:516
  4.8 1.5 %collective-permute-start = (f32[96,128]{1,0:T(8,128)S(1)}, f32[96,128]{1,0:T(8,128)S(1)}, u32[]{:S(2)}, u32[]{:S(2)}) collective-permute-start(f32[96,128]{1,0:T(8,128)S(1)} %get-tuple-element.32), channel_id=1, source_target_pairs={{0,4},{4,0},{8,12},{12,8},{16,20},{20,16},{24,28},{28,24},{1,5},{5... | collective-permute-start | bytes 147464 | tf_op jit(solution)/shard_map/ppermute | solution.py:514
  6.2 0.0 copy-start
  6.2 3.6 %collective-permute-start.1 = (f32[96,128]{1,0:T(8,128)S(1)}, f32[96,128]{1,0:T(8,128)S(1)}, u32[]{:S(2)}, u32[]{:S(2)}) collective-permute-start(f32[96,128]{1,0:T(8,128)S(1)} %get-tuple-element.33), channel_id=1, source_target_pairs={{4,8},{8,4},{12,16},{16,12},{20,24},{24,20},{28,0},{0,28},{5,9},{9... | collective-permute-start | bytes 147464 | tf_op jit(solution)/shard_map/ppermute | solution.py:513
  9.8 0.0 copy-start.1
  9.8 1.7 %copy-done.1 = bf16[1,16,9,64,128]{4,3,2,1,0:T(8,128)(2,1)S(1)} copy-done((bf16[1,16,9,64,128]{4,3,2,1,0:T(8,128)(2,1)S(1)}, bf16[1,16,9,64,128]{4,3,2,1,0:T(8,128)(2,1)}, u32[]{:S(2)}) %copy-start.1) | copy-done | bytes 2359320
  11.5 0.8 %shard_map.51 = (f32[192,128]{1,0:T(8,128)S(1)}, bf16[1,16,9,64,128]{4,3,2,1,0:T(8,128)(2,1)S(1)}) custom-call(f32[192,128]{1,0:T(8,128)S(1)} %get-tuple-element.29.refs_0_.refs_6_, bf16[1,16,9,64,128]{4,3,2,1,0:T(8,128)(2,1)S(1)} %copy-done.1), custom_call_target="tpu_custom_call" | custom-call | tf_op jit(solution)/shard_map/pallas_call | solution.py:445
  12.3 0.0 collective-permute-done.refs_2_
  12.3 0.8 %collective-permute-done.1.refs_3_ = f32[96,128]{1,0:T(8,128)S(1)} collective-permute-done((f32[96,128]{1,0:T(8,128)S(1)}, f32[96,128]{1,0:T(8,128)S(1)}, u32[]{:S(2)}, u32[]{:S(2)}) %collective-permute-start.1) | collective-permute-done | bytes 49184 | tf_op jit(solution)/shard_map/ppermute | solution.py:513
  13.0 0.0 collective-permute-done.3.refs_5_
  13.0 0.0 collective-permute-done.2.refs_4_
  13.0 0.6 %shard_map.52 = (f32[192,128]{1,0:T(8,128)S(1)}, f32[96,128]{1,0:T(8,128)S(1)}, f32[96,128]{1,0:T(8,128)S(1)}) custom-call(f32[192,128]{1,0:T(8,128)S(1)} %get-tuple-element.30.refs_0_, bf16[1,16,9,64,128]{4,3,2,1,0:T(8,128)(2,1)S(1)} %get-tuple-element.31.refs_1_.refs_2_.refs_3_.refs_4_, f32[96,128]{1,0:T(8,128)S(1)} %collective-permute-done.refs_2_, ...), custom_call_target="tpu_custom_call" | custom-call | tf_op jit(solution)/shard_map/pallas_call | solution.py:445
  13.6 0.1 collective-permute-start.7
  13.7 0.6 %collective-permute-start.6 = (f32[192,128]{1,0:T(8,128)S(1)}, f32[192,128]{1,0:T(8,128)S(1)}, u32[]{:S(2)}, u32[]{:S(2)}) collective-permute-start(f32[192,128]{1,0:T(8,128)S(1)} %get-tuple-element.34.refs_1_.refs_7_), channel_id=1, source_target_pairs={{0,1},{1,0},{2,3},{3,2},{4,5},{5,4},{6,7},{7,6},{8,9},{9,8},{10,11... | collective-permute-start | bytes 294920 | tf_op jit(solution)/shard_map/ppermute | solution.py:516
  14.3 0.0 collective-permute-start.4
  14.3 3.6 %collective-permute-start.5 = (f32[96,128]{1,0:T(8,128)S(1)}, f32[96,128]{1,0:T(8,128)S(1)}, u32[]{:S(2)}, u32[]{:S(2)}) collective-permute-start(f32[96,128]{1,0:T(8,128)S(1)} %get-tuple-element.37), channel_id=1, source_target_pairs={{4,8},{8,4},{12,16},{16,12},{20,24},{24,20},{28,0},{0,28},{5,9},{9... | collective-permute-start | bytes 147464 | tf_op jit(solution)/shard_map/ppermute | solution.py:513
  17.9 0.0 copy-done
  17.9 1.4 %shard_map.53 = (f32[192,128]{1,0:T(8,128)S(1)}, f32[96,128]{1,0:T(8,128)S(1)}, f32[24,128]{1,0:T(8,128)S(1)}) custom-call(f32[192,128]{1,0:T(8,128)S(1)} %get-tuple-element.29.refs_0_.refs_6_, f32[192,128]{1,0:T(8,128)S(1)} %get-tuple-element.34.refs_1_.refs_7_, bf16[1,16,9,64,128]{4,3,2,1,0:T(8,128)(2,1)S(1)} %get-tuple-element.31.refs_1_.refs_2_.refs_3_.refs_4_, ...), custom_call_target="tpu_custom_call" | custom-call | tf_op jit(solution)/shard_map/pallas_call | solution.py:445
  19.3 0.0 collective-permute-done.4.refs_2_
  19.3 1.8 %collective-permute-done.5.refs_3_ = f32[96,128]{1,0:T(8,128)S(1)} collective-permute-done((f32[96,128]{1,0:T(8,128)S(1)}, f32[96,128]{1,0:T(8,128)S(1)}, u32[]{:S(2)}, u32[]{:S(2)}) %collective-permute-start.5) | collective-permute-done | bytes 49184 | tf_op jit(solution)/shard_map/ppermute | solution.py:513
  21.1 0.0 collective-permute-done.7.refs_5_
  21.1 0.0 collective-permute-done.6.refs_4_
  21.1 0.6 %shard_map.54 = (f32[192,128]{1,0:T(8,128)S(1)}, f32[96,128]{1,0:T(8,128)S(1)}, f32[96,128]{1,0:T(8,128)S(1)}) custom-call(f32[192,128]{1,0:T(8,128)S(1)} %get-tuple-element.35.refs_0_, bf16[1,16,9,64,128]{4,3,2,1,0:T(8,128)(2,1)S(1)} %get-tuple-element.31.refs_1_.refs_2_.refs_3_.refs_4_, f32[96,128]{1,0:T(8,128)S(1)} %collective-permute-done.4.refs_2_, ...), custom_call_target="tpu_custom_call" | custom-call | tf_op jit(solution)/shard_map/pallas_call | solution.py:445
  21.6 0.1 collective-permute-start.11
  21.7 1.6 %collective-permute-start.10 = (f32[192,128]{1,0:T(8,128)S(1)}, f32[192,128]{1,0:T(8,128)S(1)}, u32[]{:S(2)}, u32[]{:S(2)}) collective-permute-start(f32[192,128]{1,0:T(8,128)S(1)} %get-tuple-element.38.refs_2_.refs_8_), channel_id=1, source_target_pairs={{0,1},{1,0},{2,3},{3,2},{4,5},{5,4},{6,7},{7,6},{8,9},{9,8},{10,11... | collective-permute-start | bytes 294920 | tf_op jit(solution)/shard_map/ppermute | solution.py:516
  23.3 0.2 collective-permute-start.8
  23.6 3.6 %collective-permute-start.9 = (f32[96,128]{1,0:T(8,128)S(1)}, f32[96,128]{1,0:T(8,128)S(1)}, u32[]{:S(2)}, u32[]{:S(2)}) collective-permute-start(f32[96,128]{1,0:T(8,128)S(1)} %get-tuple-element.42), channel_id=1, source_target_pairs={{4,8},{8,4},{12,16},{16,12},{20,24},{24,20},{28,0},{0,28},{5,9},{9... | collective-permute-start | bytes 147464 | tf_op jit(solution)/shard_map/ppermute | solution.py:513
  27.1 1.1 %shard_map.55 = (f32[192,128]{1,0:T(8,128)S(1)}, f32[144,128]{1,0:T(8,128)S(1)}, f32[24,128]{1,0:T(8,128)S(1)}) custom-call(f32[192,128]{1,0:T(8,128)S(1)} %get-tuple-element.29.refs_0_.refs_6_, f32[192,128]{1,0:T(8,128)S(1)} %get-tuple-element.34.refs_1_.refs_7_, f32[192,128]{1,0:T(8,128)S(1)} %get-tuple-element.38.refs_2_.refs_8_, ...), custom_call_target="tpu_custom_call" | custom-call | tf_op jit(solution)/shard_map/pallas_call | solution.py:445
  28.2 0.0 collective-permute-done.8.refs_2_
  28.3 2.1 %collective-permute-done.9.refs_3_ = f32[96,128]{1,0:T(8,128)S(1)} collective-permute-done((f32[96,128]{1,0:T(8,128)S(1)}, f32[96,128]{1,0:T(8,128)S(1)}, u32[]{:S(2)}, u32[]{:S(2)}) %collective-permute-start.9) | collective-permute-done | bytes 49184 | tf_op jit(solution)/shard_map/ppermute | solution.py:513
  30.4 0.0 collective-permute-done.11.refs_5_
  30.4 0.0 collective-permute-done.10.refs_4_
  30.4 0.6 %shard_map.56 = (f32[192,128]{1,0:T(8,128)S(1)}, f32[96,128]{1,0:T(8,128)S(1)}, f32[96,128]{1,0:T(8,128)S(1)}) custom-call(f32[192,128]{1,0:T(8,128)S(1)} %get-tuple-element.40.refs_0_, bf16[1,16,9,64,128]{4,3,2,1,0:T(8,128)(2,1)S(1)} %get-tuple-element.31.refs_1_.refs_2_.refs_3_.refs_4_, f32[96,128]{1,0:T(8,128)S(1)} %collective-permute-done.8.refs_2_, ...), custom_call_target="tpu_custom_call" | custom-call | tf_op jit(solution)/shard_map/pallas_call | solution.py:445
  30.9 0.1 collective-permute-start.15
  31.0 0.6 %collective-permute-start.14 = (f32[192,128]{1,0:T(8,128)S(1)}, f32[192,128]{1,0:T(8,128)S(1)}, u32[]{:S(2)}, u32[]{:S(2)}) collective-permute-start(f32[192,128]{1,0:T(8,128)S(1)} %get-tuple-element.43.refs_3_.refs_9_), channel_id=1, source_target_pairs={{0,1},{1,0},{2,3},{3,2},{4,5},{5,4},{6,7},{7,6},{8,9},{9,8},{10,11... | collective-permute-start | bytes 294920 | tf_op jit(solution)/shard_map/ppermute | solution.py:516
  31.6 0.0 collective-permute-start.12
  31.6 3.6 %collective-permute-start.13 = (f32[96,128]{1,0:T(8,128)S(1)}, f32[96,128]{1,0:T(8,128)S(1)}, u32[]{:S(2)}, u32[]{:S(2)}) collective-permute-start(f32[96,128]{1,0:T(8,128)S(1)} %get-tuple-element.47), channel_id=1, source_target_pairs={{4,8},{8,4},{12,16},{16,12},{20,24},{24,20},{28,0},{0,28},{5,9},{9... | collective-permute-start | bytes 147464 | tf_op jit(solution)/shard_map/ppermute | solution.py:513
  35.2 1.1 %shard_map.57 = (f32[192,128]{1,0:T(8,128)S(1)}, f32[192,128]{1,0:T(8,128)S(1)}, f32[24,128]{1,0:T(8,128)S(1)}) custom-call(f32[192,128]{1,0:T(8,128)S(1)} %get-tuple-element.29.refs_0_.refs_6_, f32[192,128]{1,0:T(8,128)S(1)} %get-tuple-element.34.refs_1_.refs_7_, f32[192,128]{1,0:T(8,128)S(1)} %get-tuple-element.38.refs_2_.refs_8_, ...), custom_call_target="tpu_custom_call" | custom-call | tf_op jit(solution)/shard_map/pallas_call | solution.py:445
  36.3 0.9 %collective-permute-start.20 = (f32[192,128]{1,0:T(8,128)S(1)}, f32[192,128]{1,0:T(8,128)S(1)}, u32[]{:S(2)}, u32[]{:S(2)}) collective-permute-start(f32[192,128]{1,0:T(8,128)S(1)} %get-tuple-element.52.refs_5_), channel_id=1, source_target_pairs={{0,3},{1,2},{2,1},{3,0},{4,7},{5,6},{6,5},{7,4},{8,11},{9,10},{10,... | collective-permute-start | bytes 294920 | tf_op jit(solution)/shard_map/ppermute | solution.py:507
  37.2 0.0 collective-permute-done.12.refs_2_
  37.2 0.8 %collective-permute-start.18 = (f32[192,128]{1,0:T(8,128)S(1)}, f32[192,128]{1,0:T(8,128)S(1)}, u32[]{:S(2)}, u32[]{:S(2)}) collective-permute-start(f32[192,128]{1,0:T(8,128)S(1)} %get-tuple-element.52.refs_5_), channel_id=1, source_target_pairs={{0,2},{1,3},{2,0},{3,1},{4,6},{5,7},{6,4},{7,5},{8,10},{9,11},{10,... | collective-permute-start | bytes 294920 | tf_op jit(solution)/shard_map/ppermute | solution.py:507
  38.0 0.4 collective-permute-done.13.refs_3_
  38.4 0.0 collective-permute-start.16
  38.4 0.0 collective-permute-done.15.refs_5_
  38.4 0.0 collective-permute-done.14.refs_4_
  38.4 1.4 %shard_map.58 = (f32[192,128]{1,0:T(8,128)S(1)}, f32[32,3,128]{2,1,0:T(4,128)}) custom-call(f32[192,128]{1,0:T(8,128)S(1)} %get-tuple-element.45.refs_0_, bf16[1,16,9,64,128]{4,3,2,1,0:T(8,128)(2,1)S(1)} %get-tuple-element.31.refs_1_.refs_2_.refs_3_.refs_4_, f32[96,128]{1,0:T(8,128)S(1)} %collective-permute-done.12.refs_2_, ...), custom_call_target="tpu_custom_call" | custom-call | tf_op jit(solution)/shard_map/pallas_call | solution.py:445
  39.8 5.0 %all-to-all-start = ((f32[32,3,128]{2,1,0:T(4,128)}), f32[32,3,128]{2,1,0:T(4,128)S(1)}, u32[]{:S(2)}, u32[]{:S(2)}) async-start(f32[32,3,128]{2,1,0:T(4,128)} %get-tuple-element.51), calls=%async_computation | async-start | bytes 131072 | tf_op jit(solution)/shard_map/all_to_all | solution.py:568
  44.8 0.6 %shard_map.59.refs_6_ = f32[48,128]{1,0:T(8,128)S(1)} custom-call(f32[192,128]{1,0:T(8,128)S(1)} %get-tuple-element.53.field_ref, f32[16,64,128]{2,1,0:T(8,128)S(1)} %bitcast.15), custom_call_target="tpu_custom_call" | custom-call | tf_op jit(solution)/shard_map/pallas_call | solution.py:445
  45.4 1.6 %collective-permute-start.21 = (f32[48,128]{1,0:T(8,128)S(1)}, f32[48,128]{1,0:T(8,128)S(1)}, u32[]{:S(2)}, u32[]{:S(2)}) collective-permute-start(f32[48,128]{1,0:T(8,128)S(1)} %shard_map.59.refs_6_), channel_id=1, source_target_pairs={{0,3},{1,2},{2,1},{3,0},{4,7},{5,6},{6,5},{7,4},{8,11},{9,10},{10,... | collective-permute-start | bytes 73736 | tf_op jit(solution)/shard_map/ppermute | solution.py:507
  47.0 0.4 collective-permute-start.19
  47.4 0.0 collective-permute-done.20.refs_11_
  47.4 0.0 collective-permute-start.17
  47.4 4.9 %all-to-all-done = f32[32,3,128]{2,1,0:T(4,128)S(1)} async-done(((f32[32,3,128]{2,1,0:T(4,128)}), f32[32,3,128]{2,1,0:T(4,128)S(1)}, u32[]{:S(2)}, u32[]{:S(2)}) %all-to-all-start) | async-done | bytes 49184 | tf_op jit(solution)/shard_map/all_to_all | solution.py:568
  52.3 0.0 collective-permute-done.18.refs_9_
  52.3 0.0 collective-permute-done.16.refs_7_
  52.3 0.0 collective-permute-done.21.refs_12_
  52.3 0.0 collective-permute-done.19.refs_10_
  52.3 0.0 collective-permute-done.17.refs_8_
  52.3 1.3 %shard_map.60 = (f32[192,128]{1,0:T(8,128)}, f32[4,48,128]{2,1,0:T(8,128)}) custom-call(f32[192,128]{1,0:T(8,128)S(1)} %get-tuple-element.29.refs_0_.refs_6_, f32[192,128]{1,0:T(8,128)S(1)} %get-tuple-element.34.refs_1_.refs_7_, f32[192,128]{1,0:T(8,128)S(1)} %get-tuple-element.38.refs_2_.refs_8_, f32[192,128]{1,0:T(8,128)S(1)} %get-tuple-element.43.refs_3_.refs_9_, ...), custom_call_target="tpu_custom_call" | custom-call | tf_op jit(solution)/shard_map/pallas_call | solution.py:445
  (1 shorter events, 0.0 us)
Async XLA Ops:
  0.6 0.9 %copy-start.2 = (f32[1,16,12,128]{3,1,2,0:T(8,128)S(1)}, f32[1,16,12,128]{3,1,2,0:T(8,128)}, u32[]{:S(2)}) copy-start(f32[1,16,12,128]{3,1,2,0:T(8,128)} %param.3) | copy-start | bytes 294916
  1.6 11.5 %collective-permute-start.3 = (f32[192,128]{1,0:T(8,128)S(1)}, f32[192,128]{1,0:T(8,128)S(1)}, u32[]{:S(2)}, u32[]{:S(2)}) collective-permute-start(f32[192,128]{1,0:T(8,128)S(1)} %get-tuple-element.29.refs_0_.refs_6_), channel_id=1, source_target_pairs={{1,2},{2,1},{3,0},{0,3},{5,6},{6,5},{7,4},{4,7},{9,10},{10,9},{11,... | collective-permute-start | bytes 294920 | tf_op jit(solution)/shard_map/ppermute | solution.py:515
  4.1 9.0 %collective-permute-start.2 = (f32[192,128]{1,0:T(8,128)S(1)}, f32[192,128]{1,0:T(8,128)S(1)}, u32[]{:S(2)}, u32[]{:S(2)}) collective-permute-start(f32[192,128]{1,0:T(8,128)S(1)} %get-tuple-element.29.refs_0_.refs_6_), channel_id=1, source_target_pairs={{0,1},{1,0},{2,3},{3,2},{4,5},{5,4},{6,7},{7,6},{8,9},{9,8},{10,11... | collective-permute-start | bytes 294920 | tf_op jit(solution)/shard_map/ppermute | solution.py:516
  4.8 7.5 %collective-permute-start = (f32[96,128]{1,0:T(8,128)S(1)}, f32[96,128]{1,0:T(8,128)S(1)}, u32[]{:S(2)}, u32[]{:S(2)}) collective-permute-start(f32[96,128]{1,0:T(8,128)S(1)} %get-tuple-element.32), channel_id=1, source_target_pairs={{0,4},{4,0},{8,12},{12,8},{16,20},{20,16},{24,28},{28,24},{1,5},{5... | collective-permute-start | bytes 147464 | tf_op jit(solution)/shard_map/ppermute | solution.py:514
  6.2 11.6 %copy-start = (f32[1,16,64,128]{3,2,1,0:T(8,128)S(1)}, f32[1,16,64,128]{3,2,1,0:T(8,128)}, u32[]{:S(2)}) copy-start(f32[1,16,64,128]{3,2,1,0:T(8,128)} %param.5) | copy-start | bytes 1572868
  6.2 6.8 %collective-permute-start.1 = (f32[96,128]{1,0:T(8,128)S(1)}, f32[96,128]{1,0:T(8,128)S(1)}, u32[]{:S(2)}, u32[]{:S(2)}) collective-permute-start(f32[96,128]{1,0:T(8,128)S(1)} %get-tuple-element.33), channel_id=1, source_target_pairs={{4,8},{8,4},{12,16},{16,12},{20,24},{24,20},{28,0},{0,28},{5,9},{9... | collective-permute-start | bytes 147464 | tf_op jit(solution)/shard_map/ppermute | solution.py:513
  9.8 1.7 %copy-start.1 = (bf16[1,16,9,64,128]{4,3,2,1,0:T(8,128)(2,1)S(1)}, bf16[1,16,9,64,128]{4,3,2,1,0:T(8,128)(2,1)}, u32[]{:S(2)}) copy-start(bf16[1,16,9,64,128]{4,3,2,1,0:T(8,128)(2,1)} %refs_1_.1) | copy-start | bytes 7077892
  13.6 7.5 %collective-permute-start.7 = (f32[192,128]{1,0:T(8,128)S(1)}, f32[192,128]{1,0:T(8,128)S(1)}, u32[]{:S(2)}, u32[]{:S(2)}) collective-permute-start(f32[192,128]{1,0:T(8,128)S(1)} %get-tuple-element.34.refs_1_.refs_7_), channel_id=1, source_target_pairs={{1,2},{2,1},{3,0},{0,3},{5,6},{6,5},{7,4},{4,7},{9,10},{10,9},{11,... | collective-permute-start | bytes 294920 | tf_op jit(solution)/shard_map/ppermute | solution.py:515
  13.7 7.4 %collective-permute-start.6 = (f32[192,128]{1,0:T(8,128)S(1)}, f32[192,128]{1,0:T(8,128)S(1)}, u32[]{:S(2)}, u32[]{:S(2)}) collective-permute-start(f32[192,128]{1,0:T(8,128)S(1)} %get-tuple-element.34.refs_1_.refs_7_), channel_id=1, source_target_pairs={{0,1},{1,0},{2,3},{3,2},{4,5},{5,4},{6,7},{7,6},{8,9},{9,8},{10,11... | collective-permute-start | bytes 294920 | tf_op jit(solution)/shard_map/ppermute | solution.py:516
  14.3 5.0 %collective-permute-start.4 = (f32[96,128]{1,0:T(8,128)S(1)}, f32[96,128]{1,0:T(8,128)S(1)}, u32[]{:S(2)}, u32[]{:S(2)}) collective-permute-start(f32[96,128]{1,0:T(8,128)S(1)} %get-tuple-element.36), channel_id=1, source_target_pairs={{0,4},{4,0},{8,12},{12,8},{16,20},{20,16},{24,28},{28,24},{1,5},{5... | collective-permute-start | bytes 147464 | tf_op jit(solution)/shard_map/ppermute | solution.py:514
  14.3 6.8 %collective-permute-start.5 = (f32[96,128]{1,0:T(8,128)S(1)}, f32[96,128]{1,0:T(8,128)S(1)}, u32[]{:S(2)}, u32[]{:S(2)}) collective-permute-start(f32[96,128]{1,0:T(8,128)S(1)} %get-tuple-element.37), channel_id=1, source_target_pairs={{4,8},{8,4},{12,16},{16,12},{20,24},{24,20},{28,0},{0,28},{5,9},{9... | collective-permute-start | bytes 147464 | tf_op jit(solution)/shard_map/ppermute | solution.py:513
  21.6 8.7 %collective-permute-start.11 = (f32[192,128]{1,0:T(8,128)S(1)}, f32[192,128]{1,0:T(8,128)S(1)}, u32[]{:S(2)}, u32[]{:S(2)}) collective-permute-start(f32[192,128]{1,0:T(8,128)S(1)} %get-tuple-element.38.refs_2_.refs_8_), channel_id=1, source_target_pairs={{1,2},{2,1},{3,0},{0,3},{5,6},{6,5},{7,4},{4,7},{9,10},{10,9},{11,... | collective-permute-start | bytes 294920 | tf_op jit(solution)/shard_map/ppermute | solution.py:515
  21.7 8.6 %collective-permute-start.10 = (f32[192,128]{1,0:T(8,128)S(1)}, f32[192,128]{1,0:T(8,128)S(1)}, u32[]{:S(2)}, u32[]{:S(2)}) collective-permute-start(f32[192,128]{1,0:T(8,128)S(1)} %get-tuple-element.38.refs_2_.refs_8_), channel_id=1, source_target_pairs={{0,1},{1,0},{2,3},{3,2},{4,5},{5,4},{6,7},{7,6},{8,9},{9,8},{10,11... | collective-permute-start | bytes 294920 | tf_op jit(solution)/shard_map/ppermute | solution.py:516
  23.3 4.9 %collective-permute-start.8 = (f32[96,128]{1,0:T(8,128)S(1)}, f32[96,128]{1,0:T(8,128)S(1)}, u32[]{:S(2)}, u32[]{:S(2)}) collective-permute-start(f32[96,128]{1,0:T(8,128)S(1)} %get-tuple-element.41), channel_id=1, source_target_pairs={{0,4},{4,0},{8,12},{12,8},{16,20},{20,16},{24,28},{28,24},{1,5},{5... | collective-permute-start | bytes 147464 | tf_op jit(solution)/shard_map/ppermute | solution.py:514
  23.6 6.8 %collective-permute-start.9 = (f32[96,128]{1,0:T(8,128)S(1)}, f32[96,128]{1,0:T(8,128)S(1)}, u32[]{:S(2)}, u32[]{:S(2)}) collective-permute-start(f32[96,128]{1,0:T(8,128)S(1)} %get-tuple-element.42), channel_id=1, source_target_pairs={{4,8},{8,4},{12,16},{16,12},{20,24},{24,20},{28,0},{0,28},{5,9},{9... | collective-permute-start | bytes 147464 | tf_op jit(solution)/shard_map/ppermute | solution.py:513
  30.9 7.5 %collective-permute-start.15 = (f32[192,128]{1,0:T(8,128)S(1)}, f32[192,128]{1,0:T(8,128)S(1)}, u32[]{:S(2)}, u32[]{:S(2)}) collective-permute-start(f32[192,128]{1,0:T(8,128)S(1)} %get-tuple-element.43.refs_3_.refs_9_), channel_id=1, source_target_pairs={{1,2},{2,1},{3,0},{0,3},{5,6},{6,5},{7,4},{4,7},{9,10},{10,9},{11,... | collective-permute-start | bytes 294920 | tf_op jit(solution)/shard_map/ppermute | solution.py:515
  31.0 7.4 %collective-permute-start.14 = (f32[192,128]{1,0:T(8,128)S(1)}, f32[192,128]{1,0:T(8,128)S(1)}, u32[]{:S(2)}, u32[]{:S(2)}) collective-permute-start(f32[192,128]{1,0:T(8,128)S(1)} %get-tuple-element.43.refs_3_.refs_9_), channel_id=1, source_target_pairs={{0,1},{1,0},{2,3},{3,2},{4,5},{5,4},{6,7},{7,6},{8,9},{9,8},{10,11... | collective-permute-start | bytes 294920 | tf_op jit(solution)/shard_map/ppermute | solution.py:516
  31.6 5.6 %collective-permute-start.12 = (f32[96,128]{1,0:T(8,128)S(1)}, f32[96,128]{1,0:T(8,128)S(1)}, u32[]{:S(2)}, u32[]{:S(2)}) collective-permute-start(f32[96,128]{1,0:T(8,128)S(1)} %get-tuple-element.46), channel_id=1, source_target_pairs={{0,4},{4,0},{8,12},{12,8},{16,20},{20,16},{24,28},{28,24},{1,5},{5... | collective-permute-start | bytes 147464 | tf_op jit(solution)/shard_map/ppermute | solution.py:514
  31.6 6.8 %collective-permute-start.13 = (f32[96,128]{1,0:T(8,128)S(1)}, f32[96,128]{1,0:T(8,128)S(1)}, u32[]{:S(2)}, u32[]{:S(2)}) collective-permute-start(f32[96,128]{1,0:T(8,128)S(1)} %get-tuple-element.47), channel_id=1, source_target_pairs={{4,8},{8,4},{12,16},{16,12},{20,24},{24,20},{28,0},{0,28},{5,9},{9... | collective-permute-start | bytes 147464 | tf_op jit(solution)/shard_map/ppermute | solution.py:513
  36.3 11.1 %collective-permute-start.20 = (f32[192,128]{1,0:T(8,128)S(1)}, f32[192,128]{1,0:T(8,128)S(1)}, u32[]{:S(2)}, u32[]{:S(2)}) collective-permute-start(f32[192,128]{1,0:T(8,128)S(1)} %get-tuple-element.52.refs_5_), channel_id=1, source_target_pairs={{0,3},{1,2},{2,1},{3,0},{4,7},{5,6},{6,5},{7,4},{8,11},{9,10},{10,... | collective-permute-start | bytes 294920 | tf_op jit(solution)/shard_map/ppermute | solution.py:507
  37.2 15.1 %collective-permute-start.18 = (f32[192,128]{1,0:T(8,128)S(1)}, f32[192,128]{1,0:T(8,128)S(1)}, u32[]{:S(2)}, u32[]{:S(2)}) collective-permute-start(f32[192,128]{1,0:T(8,128)S(1)} %get-tuple-element.52.refs_5_), channel_id=1, source_target_pairs={{0,2},{1,3},{2,0},{3,1},{4,6},{5,7},{6,4},{7,5},{8,10},{9,11},{10,... | collective-permute-start | bytes 294920 | tf_op jit(solution)/shard_map/ppermute | solution.py:507
  38.4 13.9 %collective-permute-start.16 = (f32[192,128]{1,0:T(8,128)S(1)}, f32[192,128]{1,0:T(8,128)S(1)}, u32[]{:S(2)}, u32[]{:S(2)}) collective-permute-start(f32[192,128]{1,0:T(8,128)S(1)} %get-tuple-element.52.refs_5_), channel_id=1, source_target_pairs={{0,1},{1,0},{2,3},{3,2},{4,5},{5,4},{6,7},{7,6},{8,9},{9,8},{10,11... | collective-permute-start | bytes 294920 | tf_op jit(solution)/shard_map/ppermute | solution.py:507
  39.8 12.4 %all-to-all-start = ((f32[32,3,128]{2,1,0:T(4,128)}), f32[32,3,128]{2,1,0:T(4,128)S(1)}, u32[]{:S(2)}, u32[]{:S(2)}) async-start(f32[32,3,128]{2,1,0:T(4,128)} %get-tuple-element.51), calls=%async_computation | async-start | bytes 131072 | tf_op jit(solution)/shard_map/all_to_all | solution.py:568
  45.4 6.9 %collective-permute-start.21 = (f32[48,128]{1,0:T(8,128)S(1)}, f32[48,128]{1,0:T(8,128)S(1)}, u32[]{:S(2)}, u32[]{:S(2)}) collective-permute-start(f32[48,128]{1,0:T(8,128)S(1)} %shard_map.59.refs_6_), channel_id=1, source_target_pairs={{0,3},{1,2},{2,1},{3,0},{4,7},{5,6},{6,5},{7,4},{8,11},{9,10},{10,... | collective-permute-start | bytes 73736 | tf_op jit(solution)/shard_map/ppermute | solution.py:507
  47.0 5.3 %collective-permute-start.19 = (f32[48,128]{1,0:T(8,128)S(1)}, f32[48,128]{1,0:T(8,128)S(1)}, u32[]{:S(2)}, u32[]{:S(2)}) collective-permute-start(f32[48,128]{1,0:T(8,128)S(1)} %shard_map.59.refs_6_), channel_id=1, source_target_pairs={{0,2},{1,3},{2,0},{3,1},{4,6},{5,7},{6,4},{7,5},{8,10},{9,11},{10,... | collective-permute-start | bytes 73736 | tf_op jit(solution)/shard_map/ppermute | solution.py:507
  47.4 4.9 %collective-permute-start.17 = (f32[48,128]{1,0:T(8,128)S(1)}, f32[48,128]{1,0:T(8,128)S(1)}, u32[]{:S(2)}, u32[]{:S(2)}) collective-permute-start(f32[48,128]{1,0:T(8,128)S(1)} %shard_map.59.refs_6_), channel_id=1, source_target_pairs={{0,1},{1,0},{2,3},{3,2},{4,5},{5,4},{6,7},{7,6},{8,9},{9,8},{10,11... | collective-permute-start | bytes 73736 | tf_op jit(solution)/shard_map/ppermute | solution.py:507

commit v5 on v4

--- a/solution.py
+++ b/solution.py
@@ -56,27 +56,33 @@
     return jnp.concatenate(highs + lows, 0)
 
 
+def split_operand(block):
+    high = block.astype(jnp.bfloat16)
+    low = (block - high.astype(jnp.float32)).astype(jnp.bfloat16)
+    return jnp.concatenate([high, low], 0)
+
+
 def lane_sign(width):
     lane = lax.broadcasted_iota(jnp.int32, (1, width), 1)
     return jnp.where(lane < width // 2, 1.0, -1.0).astype(jnp.float32)
 
 
-def prepare(field_ref, table_ref, first_slot, sites, rhs, by_rhs):
+def prepare(field_ref, table_ref, first_slot, sites, rhs, dense=False):
     sign = lane_sign(field_ref.shape[-1])
     for site in range(sites):
-        block = load_site(field_ref, site, sites, rhs, by_rhs)
-        table_ref[first_slot + site] = operand(block, sign)
-
-
-def prepare_pair(odd, even_ref, odd_ref, table_ref, first_slot, sites, rhs, by_rhs):
+        block = load_site(field_ref, site, sites, rhs, False)
+        table_ref[first_slot + site] = split_operand(block) if dense else operand(block, sign)
+
+
+def prepare_pair(odd, even_ref, odd_ref, table_ref, first_slot, sites, rhs, dense):
     sign = lane_sign(even_ref.shape[-1])
     for site in range(sites):
         block = jnp.where(
             odd,
-            load_site(odd_ref, site, sites, rhs, by_rhs),
-            load_site(even_ref, site, sites, rhs, by_rhs),
+            load_site(odd_ref, site, sites, rhs, False),
+            load_site(even_ref, site, sites, rhs, False),
         )
-        table_ref[first_slot + site] = operand(block, sign)
+        table_ref[first_slot + site] = split_operand(block) if dense else operand(block, sign)
 
 
 def site_product(slots, blocks):
@@ -157,6 +163,53 @@
             out_ref[row : row + 8, :] = value[8 * at : 8 * at + 8]
 
 
+def dense_product(slots, blocks):
+    total = lax.dot_general(
+        jnp.concatenate(slots, -1), blocks, (((1,), (0,)), ((), ())), preferred_element_type=jnp.float32
+    )
+    rows = total.shape[0] // 2
+    return total[:rows] + total[rows:]
+
+
+def far_list(site, sites, depth, wrap_z, odd_time):
+    extent = sites // depth
+    ahead = 2 * sites
+    behind = ahead + extent
+    above = behind + extent
+    below = above + sites
+    y, x = divmod(site, extent)
+    chosen = [(7 + odd_time, site), (8 - odd_time, sites + site)]
+    if y + 1 == depth:
+        chosen.append((3, ahead + x))
+    if y == 0:
+        chosen.append((4, behind + x))
+    if not wrap_z:
+        chosen += [(5, above + site), (6, below + site)]
+    return chosen
+
+
+def build_dense(hops_ref, dense_ref, depth, wrap_z):
+    sites, _, half, width = hops_ref.shape[1:]
+    odd_time = lax.rem(lax.axis_index("narrow"), 2)
+    row = lax.broadcasted_iota(jnp.int32, (width, 2 * width), 0)
+    col = lax.broadcasted_iota(jnp.int32, (width, 2 * width), 1)
+    signed = jnp.where(row < half, STEP_SCALE, -STEP_SCALE)
+    swapped = jnp.where(row < half, row + half, row - half) + width
+    select = jnp.where(col == row, signed, jnp.where(col == swapped, STEP_SCALE, 0.0))
+    select = select.astype(jnp.bfloat16)
+    empty = jnp.zeros((half, width), jnp.bfloat16)
+    for site in range(sites):
+        for at, (d, _) in enumerate(far_list(site, sites, depth, wrap_z, odd_time)):
+            block = hops_ref[0, site, d]
+            pair = jnp.concatenate(
+                [jnp.concatenate([block, empty], -1), jnp.concatenate([empty, block], -1)], 0
+            )
+            dense = lax.dot_general(
+                select, pair, (((1,), (1,)), ((), ())), preferred_element_type=jnp.float32
+            )
+            dense_ref[site, at * width : (at + 1) * width, :] = dense.astype(jnp.bfloat16)
+
+
 def near_sites(hops_ref, table, near_ref, depth, rhs, wrap_z, ready):
     sites = hops_ref.shape[1]
     extent = sites // depth
@@ -197,61 +250,54 @@
 def near_kernel(power, depth, rhs, wrap_z, *refs):
     fields = refs[: power + 1]
     hops_ref = refs[power + 1]
-    if power:
-        near_ref, coarse_ref, other_ref, table = refs[-4:]
-    else:
-        near_ref, other_ref, table = refs[-3:]
-    prepare(fields[power], table, 0, hops_ref.shape[1], rhs, False)
+    near_ref, other_ref, table = refs[-3:] if power == 0 else (refs[-4], refs[-2], refs[-1])
+    prepare(fields[power], table, 0, hops_ref.shape[1], rhs)
 
     def keep(site):
         if power == 0:
             other_ref[0, site] = hops_ref[0, site]
 
     near_sites(hops_ref, table, near_ref, depth, rhs, wrap_z, keep)
-    if power:
-        restriction = refs[power + 2]
-        earlier = refs[power + 3 : -4]
+    if power == 1:
+        build_dense(hops_ref, refs[-3], depth, wrap_z)
+    elif power > 1:
+        restriction, coarse_ref = refs[power + 2], refs[-3]
         base = 0
-        for ref in earlier:
+        for ref in refs[power + 3 : -4]:
             coarse_ref[base : base + ref.shape[0], :] = ref[...]
             base += ref.shape[0]
-        for field_ref in fields if power == 1 else fields[power:]:
+        for field_ref in fields if power == 2 else fields[power:]:
             restrict_field(field_ref, restriction, depth, rhs, coarse_ref, base)
             base += restriction.shape[0] // depth // 2 * rhs
+    if power:
         other_ref[...] = gram_columns(power, fields, other_ref.shape[0])
 
 
-def far_kernel(depth, rhs, wrap_z, last, *refs):
-    near_ref, hops, side_a, side_b, time_a, time_b = refs[:6]
+def far_kernel(depth, rhs, wrap_z, dense, last, *refs):
+    near_ref, blocks, side_a, side_b, time_a, time_b = refs[:6]
     table = refs[-1]
     extra = refs[6:-1]
-    sites = hops.shape[1]
-    extent = sites // depth
+    extent = side_a.shape[0] // rhs
+    sites = extent * depth
     ahead = 2 * sites
-    behind = ahead + extent
-    above = behind + extent
-    below = above + sites
     odd_row = lax.rem(lax.axis_index("wide"), 2) == 1
     odd_time = lax.rem(lax.axis_index("narrow"), 2)
-    prepare_pair(odd_row, side_a, side_b, table, ahead, extent, rhs, False)
-    prepare_pair(odd_row, side_b, side_a, table, behind, extent, rhs, False)
-    prepare(time_a, table, 0, sites, rhs, False)
-    prepare(time_b, table, sites, sites, rhs, False)
+    prepare_pair(odd_row, side_a, side_b, table, ahead, extent, rhs, dense)
+    prepare_pair(odd_row, side_b, side_a, table, ahead + extent, extent, rhs, dense)
+    prepare(time_a, table, 0, sites, rhs, dense)
+    prepare(time_b, table, sites, sites, rhs, dense)
     if not wrap_z:
-        prepare(extra[0], table, above, sites, rhs, False)
-        prepare(extra[1], table, below, sites, rhs, False)
+        prepare(extra[0], table, ahead + 2 * extent, sites, rhs, dense)
+        prepare(extra[1], table, ahead + 2 * extent + sites, sites, rhs, dense)
         extra = extra[2:]
     out_ref = extra[ITERS * 2 - 1] if last else extra[0]
     for site in range(sites):
-        y, x = divmod(site, extent)
-        chosen = [(7 + odd_time, site), (8 - odd_time, sites + site)]
-        if y + 1 == depth:
-            chosen.append((3, ahead + x))
-        if y == 0:
-            chosen.append((4, behind + x))
-        if not wrap_z:
-            chosen += [(5, above + site), (6, below + site)]
-        value = site_product([table[at] for _, at in chosen], [hops[0, site, d] for d, _ in chosen])
+        chosen = far_list(site, sites, depth, wrap_z, odd_time)
+        slots = [table[at] for _, at in chosen]
+        if dense:
+            value = dense_product(slots, blocks[site, 0 : len(chosen) * out_ref.shape[-1], :])
+        else:
+            value = site_product(slots, [blocks[0, site, d] for d, _ in chosen])
         value = value + load_site(near_ref, site, sites, rhs, False)
         store_site(out_ref, site, sites, rhs, value, False)
     if not last:
@@ -479,6 +525,8 @@
     f32 = jnp.float32
     field_shape = jax.ShapeDtypeStruct((total_rows, width), f32)
     gram_shape = jax.ShapeDtypeStruct((period, width), f32)
+    far_count = max(len(far_list(site, sites, YLOC, wrap_z, 0)) for site in range(sites))
+    dense_shape = jax.ShapeDtypeStruct((sites, far_count * width, width), jnp.bfloat16)
     hops = hop_blocks
 
     if rows_y % 2 or narrow % 2 or narrow & (narrow - 1):
@@ -525,8 +573,18 @@
                 hop_blocks,
                 scratch=[table],
             )
+        elif power == 1:
+            near, dense, gram = call(
+                functools.partial(near_kernel, power, YLOC, rhs, wrap_z),
+                [field_shape, dense_shape, gram_shape],
+                *fields,
+                hops,
+                scratch=[table],
+            )
+            grams.append(gram)
         else:
-            stacked = sum(ref.shape[0] for ref in waiting) + coarse_rows * (2 if power == 1 else 1)
+            fresh = power + 1 if power == 2 else 1
+            stacked = sum(ref.shape[0] for ref in waiting) + coarse_rows * fresh
             near, coarse, gram = call(
                 functools.partial(near_kernel, power, YLOC, rhs, wrap_z),
                 [field_shape, jax.ShapeDtypeStruct((stacked, width), f32), gram_shape],
@@ -547,7 +605,7 @@
         per_row = width // SLOT
         packed_rows = -(-rhs // per_row)
         outs = call(
-            functools.partial(far_kernel, YLOC, rhs, wrap_z, last),
+            functools.partial(far_kernel, YLOC, rhs, wrap_z, power > 0, last),
             [field_shape]
             + (
                 [jax.ShapeDtypeStruct((wide * narrow, packed_rows, width), f32)]
@@ -555,10 +613,10 @@
                 else [half_shape] * 2
             ),
             near,
-            hops,
+            dense if power else hops,
             *received,
             *(fields + grams if last else []),
-            scratch=[pltpu.VMEM((slots, 4 * tile_rows, width), jnp.bfloat16)],
+            scratch=[pltpu.VMEM((slots, (2 if power else 4) * tile_rows, width), jnp.bfloat16)],
         )
         field = outs[0]
         fields.append(field)

time: 53.8 us -> 53.6 us (level)
  waiting for transfers between devices: 9.99 us -> 9.14 us
  Pallas kernels: 9.4 us -> 10 us
    ppermute x4, waiting for transfers between devices: 5.05 us -> 4.2 us  [per_device(): side_b = lax.ppermute(down_send, 'wide', swap_pairs(wide, 1, rows_y))]
    pallas_call x11, Pallas kernels: 9.4 us -> 10 us  [call(): pl.pallas_call(kernel, out_shape=outs, in_specs=vmem(len(args)), out_spec...]
  transfers between devices with their start and end apart: 23 -> 23, of which waited for: 5 -> 5; matrix products, arithmetic and copies ran while one was open for 0% -> 0% of each run, Pallas kernels for 12% -> 13%
where the time goes in v5:
time: 53.6 us; the launch traced here: 53.4 us
  starting transfers between devices  30.9 us (58%)
  Pallas kernels  10 us (19%)
  waiting for transfers between devices  9.14 us (17%)
  local copies, waits for them, and re-layouts  2.55 us (5%)
  between operations  0.77 us (1%)
    ppermute x4, starting transfers between devices, per_device(): side_b = lax.ppermute(down_send, 'wide', swap_pairs(wide, 1, rows_y))  14.3 us
    pallas_call x11, Pallas kernels, call(): pl.pallas_call(kernel, out_shape=outs, in_specs=vmem(len(args)), out_spec...  10 us
    all_to_all x1, starting transfers between devices, per_device(): swapped = lax.all_to_all(outs[1], ('wide', 'narrow'), 0, 0)  5 us
    all_to_all x1, waiting for transfers between devices, per_device(): swapped = lax.all_to_all(outs[1], ('wide', 'narrow'), 0, 0)  4.85 us
    ppermute x4, waiting for transfers between devices, per_device(): side_b = lax.ppermute(down_send, 'wide', swap_pairs(wide, 1, rows_y))  4.2 us
    ppermute x6, starting transfers between devices, to_all_times(): lax.ppermute(value, 'narrow', [(i, i ^ k) for i in range(narrow)])  3.65 us
    ppermute x4, starting transfers between devices, per_device(): time_a = lax.ppermute(field, 'narrow', swap_pairs(narrow, 0))  3.52 us
    ppermute x4, starting transfers between devices, per_device(): time_b = lax.ppermute(field, 'narrow', swap_pairs(narrow, 1))  2.71 us
  transfers between devices with their start and end apart: 23, of which 5 were waited for; matrix products, arithmetic and copies ran while one was open for 0% of the time, Pallas kernels for 13%

profile of v5, /device:TPU:0, one launch (start us, length us, event | category | flops | bytes accessed | tf_op | source)
XLA Modules:
  0.0 53.4 jit_solution(3568550076751030631)
XLA Ops:
  0.6 0.0 copy-start.2
  0.6 0.9 %copy-done.2 = f32[1,16,12,128]{3,1,2,0:T(8,128)S(1)} copy-done((f32[1,16,12,128]{3,1,2,0:T(8,128)S(1)}, f32[1,16,12,128]{3,1,2,0:T(8,128)}, u32[]{:S(2)}) %copy-start.2) | copy-done | bytes 98328
  1.5 0.1 shard_map.50
  1.6 2.5 %collective-permute-start.3 = (f32[192,128]{1,0:T(8,128)S(1)}, f32[192,128]{1,0:T(8,128)S(1)}, u32[]{:S(2)}, u32[]{:S(2)}) collective-permute-start(f32[192,128]{1,0:T(8,128)S(1)} %get-tuple-element.29.refs_0_.refs_6_), channel_id=1, source_target_pairs={{1,2},{2,1},{3,0},{0,3},{5,6},{6,5},{7,4},{4,7},{9,10},{10,9},{11,... | collective-permute-start | bytes 294920 | tf_op jit(solution)/shard_map/ppermute | solution.py:563
  4.1 0.7 %collective-permute-start.2 = (f32[192,128]{1,0:T(8,128)S(1)}, f32[192,128]{1,0:T(8,128)S(1)}, u32[]{:S(2)}, u32[]{:S(2)}) collective-permute-start(f32[192,128]{1,0:T(8,128)S(1)} %get-tuple-element.29.refs_0_.refs_6_), channel_id=1, source_target_pairs={{0,1},{1,0},{2,3},{3,2},{4,5},{5,4},{6,7},{7,6},{8,9},{9,8},{10,11... | collective-permute-start | bytes 294920 | tf_op jit(solution)/shard_map/ppermute | solution.py:564
  4.8 1.5 %collective-permute-start = (f32[96,128]{1,0:T(8,128)S(1)}, f32[96,128]{1,0:T(8,128)S(1)}, u32[]{:S(2)}, u32[]{:S(2)}) collective-permute-start(f32[96,128]{1,0:T(8,128)S(1)} %get-tuple-element.32), channel_id=1, source_target_pairs={{0,4},{4,0},{8,12},{12,8},{16,20},{20,16},{24,28},{28,24},{1,5},{5... | collective-permute-start | bytes 147464 | tf_op jit(solution)/shard_map/ppermute | solution.py:562
  6.2 3.6 %collective-permute-start.1 = (f32[96,128]{1,0:T(8,128)S(1)}, f32[96,128]{1,0:T(8,128)S(1)}, u32[]{:S(2)}, u32[]{:S(2)}) collective-permute-start(f32[96,128]{1,0:T(8,128)S(1)} %get-tuple-element.33), channel_id=1, source_target_pairs={{4,8},{8,4},{12,16},{16,12},{20,24},{24,20},{28,0},{0,28},{5,9},{9... | collective-permute-start | bytes 147464 | tf_op jit(solution)/shard_map/ppermute | solution.py:561
  9.8 0.0 copy-start.1
  9.8 1.7 %copy-done.1 = bf16[1,16,9,64,128]{4,3,2,1,0:T(8,128)(2,1)S(1)} copy-done((bf16[1,16,9,64,128]{4,3,2,1,0:T(8,128)(2,1)S(1)}, bf16[1,16,9,64,128]{4,3,2,1,0:T(8,128)(2,1)}, u32[]{:S(2)}) %copy-start.1) | copy-done | bytes 2359320
  11.5 0.8 %shard_map.51 = (f32[192,128]{1,0:T(8,128)S(1)}, bf16[1,16,9,64,128]{4,3,2,1,0:T(8,128)(2,1)S(1)}) custom-call(f32[192,128]{1,0:T(8,128)S(1)} %get-tuple-element.29.refs_0_.refs_6_, bf16[1,16,9,64,128]{4,3,2,1,0:T(8,128)(2,1)S(1)} %copy-done.1), custom_call_target="tpu_custom_call" | custom-call | tf_op jit(solution)/shard_map/pallas_call | solution.py:491
  12.3 0.0 collective-permute-done.refs_2_
  12.3 0.8 %collective-permute-done.1.refs_3_ = f32[96,128]{1,0:T(8,128)S(1)} collective-permute-done((f32[96,128]{1,0:T(8,128)S(1)}, f32[96,128]{1,0:T(8,128)S(1)}, u32[]{:S(2)}, u32[]{:S(2)}) %collective-permute-start.1) | collective-permute-done | bytes 49184 | tf_op jit(solution)/shard_map/ppermute | solution.py:561
  13.0 0.0 collective-permute-done.3.refs_5_
  13.0 0.0 collective-permute-done.2.refs_4_
  13.0 0.6 %shard_map.52 = (f32[192,128]{1,0:T(8,128)S(1)}, f32[96,128]{1,0:T(8,128)S(1)}, f32[96,128]{1,0:T(8,128)S(1)}) custom-call(f32[192,128]{1,0:T(8,128)S(1)} %get-tuple-element.30.refs_0_, bf16[1,16,9,64,128]{4,3,2,1,0:T(8,128)(2,1)S(1)} %get-tuple-element.31.refs_1_.refs_2_.refs_3_.refs_4_, f32[96,128]{1,0:T(8,128)S(1)} %collective-permute-done.refs_2_, ...), custom_call_target="tpu_custom_call" | custom-call | tf_op jit(solution)/shard_map/pallas_call | solution.py:491
  13.6 0.0 copy-start
  13.6 0.1 collective-permute-start.7
  13.7 0.6 %collective-permute-start.6 = (f32[192,128]{1,0:T(8,128)S(1)}, f32[192,128]{1,0:T(8,128)S(1)}, u32[]{:S(2)}, u32[]{:S(2)}) collective-permute-start(f32[192,128]{1,0:T(8,128)S(1)} %get-tuple-element.34.refs_1_.refs_7_), channel_id=1, source_target_pairs={{0,1},{1,0},{2,3},{3,2},{4,5},{5,4},{6,7},{7,6},{8,9},{9,8},{10,11... | collective-permute-start | bytes 294920 | tf_op jit(solution)/shard_map/ppermute | solution.py:564
  14.3 0.0 collective-permute-start.4
  14.3 3.6 %collective-permute-start.5 = (f32[96,128]{1,0:T(8,128)S(1)}, f32[96,128]{1,0:T(8,128)S(1)}, u32[]{:S(2)}, u32[]{:S(2)}) collective-permute-start(f32[96,128]{1,0:T(8,128)S(1)} %get-tuple-element.38), channel_id=1, source_target_pairs={{4,8},{8,4},{12,16},{16,12},{20,24},{24,20},{28,0},{0,28},{5,9},{9... | collective-permute-start | bytes 147464 | tf_op jit(solution)/shard_map/ppermute | solution.py:561
  17.9 1.5 %shard_map.53 = (f32[192,128]{1,0:T(8,128)S(1)}, bf16[16,384,128]{2,1,0:T(8,128)(2,1)S(1)}, f32[24,128]{1,0:T(8,128)S(1)}) custom-call(f32[192,128]{1,0:T(8,128)S(1)} %get-tuple-element.29.refs_0_.refs_6_, f32[192,128]{1,0:T(8,128)S(1)} %get-tuple-element.34.refs_1_.refs_7_, bf16[1,16,9,64,128]{4,3,2,1,0:T(8,128)(2,1)S(1)} %get-tuple-element.31.refs_1_.refs_2_.refs_3_.refs_4_), custom_call_target="tpu_custom_call" | custom-call | tf_op jit(solution)/shard_map/pallas_call | solution.py:491
  19.3 0.0 collective-permute-done.4.refs_2_
  19.4 1.7 %collective-permute-done.5.refs_3_ = f32[96,128]{1,0:T(8,128)S(1)} collective-permute-done((f32[96,128]{1,0:T(8,128)S(1)}, f32[96,128]{1,0:T(8,128)S(1)}, u32[]{:S(2)}, u32[]{:S(2)}) %collective-permute-start.5) | collective-permute-done | bytes 49184 | tf_op jit(solution)/shard_map/ppermute | solution.py:561
  21.1 0.0 collective-permute-done.7.refs_5_
  21.1 0.0 collective-permute-done.6.refs_4_
  21.1 0.5 shard_map.54
  21.6 0.1 collective-permute-start.11
  21.7 1.6 %collective-permute-start.10 = (f32[192,128]{1,0:T(8,128)S(1)}, f32[192,128]{1,0:T(8,128)S(1)}, u32[]{:S(2)}, u32[]{:S(2)}) collective-permute-start(f32[192,128]{1,0:T(8,128)S(1)} %get-tuple-element.39.refs_2_.refs_8_), channel_id=1, source_target_pairs={{0,1},{1,0},{2,3},{3,2},{4,5},{5,4},{6,7},{7,6},{8,9},{9,8},{10,11... | collective-permute-start | bytes 294920 | tf_op jit(solution)/shard_map/ppermute | solution.py:564
  23.3 0.2 collective-permute-start.8
  23.5 3.6 %collective-permute-start.9 = (f32[96,128]{1,0:T(8,128)S(1)}, f32[96,128]{1,0:T(8,128)S(1)}, u32[]{:S(2)}, u32[]{:S(2)}) collective-permute-start(f32[96,128]{1,0:T(8,128)S(1)} %get-tuple-element.42), channel_id=1, source_target_pairs={{4,8},{8,4},{12,16},{16,12},{20,24},{24,20},{28,0},{0,28},{5,9},{9... | collective-permute-start | bytes 147464 | tf_op jit(solution)/shard_map/ppermute | solution.py:561
  27.1 0.0 copy-done
  27.1 1.9 %shard_map.55 = (f32[192,128]{1,0:T(8,128)S(1)}, f32[144,128]{1,0:T(8,128)S(1)}, f32[24,128]{1,0:T(8,128)S(1)}) custom-call(f32[192,128]{1,0:T(8,128)S(1)} %get-tuple-element.29.refs_0_.refs_6_, f32[192,128]{1,0:T(8,128)S(1)} %get-tuple-element.34.refs_1_.refs_7_, f32[192,128]{1,0:T(8,128)S(1)} %get-tuple-element.39.refs_2_.refs_8_, ...), custom_call_target="tpu_custom_call" | custom-call | tf_op jit(solution)/shard_map/pallas_call | solution.py:491
  29.0 0.0 collective-permute-done.8.refs_2_
  29.0 1.3 %collective-permute-done.9.refs_3_ = f32[96,128]{1,0:T(8,128)S(1)} collective-permute-done((f32[96,128]{1,0:T(8,128)S(1)}, f32[96,128]{1,0:T(8,128)S(1)}, u32[]{:S(2)}, u32[]{:S(2)}) %collective-permute-start.9) | collective-permute-done | bytes 49184 | tf_op jit(solution)/shard_map/ppermute | solution.py:561
  30.3 0.0 collective-permute-done.11.refs_5_
  30.3 0.0 collective-permute-done.10.refs_4_
  30.3 0.5 shard_map.56
  30.8 0.1 collective-permute-start.15
  30.9 0.6 %collective-permute-start.14 = (f32[192,128]{1,0:T(8,128)S(1)}, f32[192,128]{1,0:T(8,128)S(1)}, u32[]{:S(2)}, u32[]{:S(2)}) collective-permute-start(f32[192,128]{1,0:T(8,128)S(1)} %get-tuple-element.43.refs_3_.refs_9_), channel_id=1, source_target_pairs={{0,1},{1,0},{2,3},{3,2},{4,5},{5,4},{6,7},{7,6},{8,9},{9,8},{10,11... | collective-permute-start | bytes 294920 | tf_op jit(solution)/shard_map/ppermute | solution.py:564
  31.5 0.0 collective-permute-start.12
  31.5 3.6 %collective-permute-start.13 = (f32[96,128]{1,0:T(8,128)S(1)}, f32[96,128]{1,0:T(8,128)S(1)}, u32[]{:S(2)}, u32[]{:S(2)}) collective-permute-start(f32[96,128]{1,0:T(8,128)S(1)} %get-tuple-element.47), channel_id=1, source_target_pairs={{4,8},{8,4},{12,16},{16,12},{20,24},{24,20},{28,0},{0,28},{5,9},{9... | collective-permute-start | bytes 147464 | tf_op jit(solution)/shard_map/ppermute | solution.py:561
  35.0 1.1 %shard_map.57 = (f32[192,128]{1,0:T(8,128)S(1)}, f32[192,128]{1,0:T(8,128)S(1)}, f32[24,128]{1,0:T(8,128)S(1)}) custom-call(f32[192,128]{1,0:T(8,128)S(1)} %get-tuple-element.29.refs_0_.refs_6_, f32[192,128]{1,0:T(8,128)S(1)} %get-tuple-element.34.refs_1_.refs_7_, f32[192,128]{1,0:T(8,128)S(1)} %get-tuple-element.39.refs_2_.refs_8_, ...), custom_call_target="tpu_custom_call" | custom-call | tf_op jit(solution)/shard_map/pallas_call | solution.py:491
  36.1 0.9 %collective-permute-start.20 = (f32[192,128]{1,0:T(8,128)S(1)}, f32[192,128]{1,0:T(8,128)S(1)}, u32[]{:S(2)}, u32[]{:S(2)}) collective-permute-start(f32[192,128]{1,0:T(8,128)S(1)} %get-tuple-element.52.refs_5_), channel_id=1, source_target_pairs={{0,3},{1,2},{2,1},{3,0},{4,7},{5,6},{6,5},{7,4},{8,11},{9,10},{10,... | collective-permute-start | bytes 294920 | tf_op jit(solution)/shard_map/ppermute | solution.py:555
  37.0 0.0 collective-permute-done.12.refs_2_
  37.0 0.8 %collective-permute-start.18 = (f32[192,128]{1,0:T(8,128)S(1)}, f32[192,128]{1,0:T(8,128)S(1)}, u32[]{:S(2)}, u32[]{:S(2)}) collective-permute-start(f32[192,128]{1,0:T(8,128)S(1)} %get-tuple-element.52.refs_5_), channel_id=1, source_target_pairs={{0,2},{1,3},{2,0},{3,1},{4,6},{5,7},{6,4},{7,5},{8,10},{9,11},{10,... | collective-permute-start | bytes 294920 | tf_op jit(solution)/shard_map/ppermute | solution.py:555
  37.8 0.4 collective-permute-done.13.refs_3_
  38.3 0.0 collective-permute-start.16
  38.3 0.0 collective-permute-done.15.refs_5_
  38.3 0.0 collective-permute-done.14.refs_4_
  38.3 1.3 %shard_map.58 = (f32[192,128]{1,0:T(8,128)S(1)}, f32[32,3,128]{2,1,0:T(4,128)}) custom-call(f32[192,128]{1,0:T(8,128)S(1)} %get-tuple-element.45.refs_0_, bf16[16,384,128]{2,1,0:T(8,128)(2,1)S(1)} %get-tuple-element.36.refs_1_, f32[96,128]{1,0:T(8,128)S(1)} %collective-permute-done.12.refs_2_, f32[96,128]{1,0:T(8,128)S(1)} %collective-permute-done.13.refs_3_, ...), custom_call_target="tpu_custom_call" | custom-call | tf_op jit(solution)/shard_map/pallas_call | solution.py:491
  39.6 5.0 %all-to-all-start = ((f32[32,3,128]{2,1,0:T(4,128)}), f32[32,3,128]{2,1,0:T(4,128)S(1)}, u32[]{:S(2)}, u32[]{:S(2)}) async-start(f32[32,3,128]{2,1,0:T(4,128)} %get-tuple-element.51), calls=%async_computation | async-start | bytes 131072 | tf_op jit(solution)/shard_map/all_to_all | solution.py:626
  44.6 0.6 %shard_map.59.refs_6_ = f32[48,128]{1,0:T(8,128)S(1)} custom-call(f32[192,128]{1,0:T(8,128)S(1)} %get-tuple-element.53.field_ref, f32[16,64,128]{2,1,0:T(8,128)S(1)} %bitcast.14), custom_call_target="tpu_custom_call" | custom-call | tf_op jit(solution)/shard_map/pallas_call | solution.py:491
  45.2 1.6 %collective-permute-start.21 = (f32[48,128]{1,0:T(8,128)S(1)}, f32[48,128]{1,0:T(8,128)S(1)}, u32[]{:S(2)}, u32[]{:S(2)}) collective-permute-start(f32[48,128]{1,0:T(8,128)S(1)} %shard_map.59.refs_6_), channel_id=1, source_target_pairs={{0,3},{1,2},{2,1},{3,0},{4,7},{5,6},{6,5},{7,4},{8,11},{9,10},{10,... | collective-permute-start | bytes 73736 | tf_op jit(solution)/shard_map/ppermute | solution.py:555
  46.8 0.4 collective-permute-start.19
  47.2 0.0 collective-permute-done.20.refs_11_
  47.2 0.0 collective-permute-start.17
  47.2 4.9 %all-to-all-done = f32[32,3,128]{2,1,0:T(4,128)S(1)} async-done(((f32[32,3,128]{2,1,0:T(4,128)}), f32[32,3,128]{2,1,0:T(4,128)S(1)}, u32[]{:S(2)}, u32[]{:S(2)}) %all-to-all-start) | async-done | bytes 49184 | tf_op jit(solution)/shard_map/all_to_all | solution.py:626
  52.1 0.0 collective-permute-done.18.refs_9_
  52.1 0.0 collective-permute-done.16.refs_7_
  52.1 0.0 collective-permute-done.21.refs_12_
  52.1 0.0 collective-permute-done.19.refs_10_
  52.1 0.0 collective-permute-done.17.refs_8_
  52.1 1.3 %shard_map.60 = (f32[192,128]{1,0:T(8,128)}, f32[4,48,128]{2,1,0:T(8,128)}) custom-call(f32[192,128]{1,0:T(8,128)S(1)} %get-tuple-element.29.refs_0_.refs_6_, f32[192,128]{1,0:T(8,128)S(1)} %get-tuple-element.34.refs_1_.refs_7_, f32[192,128]{1,0:T(8,128)S(1)} %get-tuple-element.39.refs_2_.refs_8_, f32[192,128]{1,0:T(8,128)S(1)} %get-tuple-element.43.refs_3_.refs_9_, ...), custom_call_target="tpu_custom_call" | custom-call | tf_op jit(solution)/shard_map/pallas_call | solution.py:491
  (1 shorter events, 0.0 us)
Async XLA Ops:
  0.6 0.9 %copy-start.2 = (f32[1,16,12,128]{3,1,2,0:T(8,128)S(1)}, f32[1,16,12,128]{3,1,2,0:T(8,128)}, u32[]{:S(2)}) copy-start(f32[1,16,12,128]{3,1,2,0:T(8,128)} %param.3) | copy-start | bytes 294916
  1.6 11.5 %collective-permute-start.3 = (f32[192,128]{1,0:T(8,128)S(1)}, f32[192,128]{1,0:T(8,128)S(1)}, u32[]{:S(2)}, u32[]{:S(2)}) collective-permute-start(f32[192,128]{1,0:T(8,128)S(1)} %get-tuple-element.29.refs_0_.refs_6_), channel_id=1, source_target_pairs={{1,2},{2,1},{3,0},{0,3},{5,6},{6,5},{7,4},{4,7},{9,10},{10,9},{11,... | collective-permute-start | bytes 294920 | tf_op jit(solution)/shard_map/ppermute | solution.py:563
  4.1 9.0 %collective-permute-start.2 = (f32[192,128]{1,0:T(8,128)S(1)}, f32[192,128]{1,0:T(8,128)S(1)}, u32[]{:S(2)}, u32[]{:S(2)}) collective-permute-start(f32[192,128]{1,0:T(8,128)S(1)} %get-tuple-element.29.refs_0_.refs_6_), channel_id=1, source_target_pairs={{0,1},{1,0},{2,3},{3,2},{4,5},{5,4},{6,7},{7,6},{8,9},{9,8},{10,11... | collective-permute-start | bytes 294920 | tf_op jit(solution)/shard_map/ppermute | solution.py:564
  4.8 7.5 %collective-permute-start = (f32[96,128]{1,0:T(8,128)S(1)}, f32[96,128]{1,0:T(8,128)S(1)}, u32[]{:S(2)}, u32[]{:S(2)}) collective-permute-start(f32[96,128]{1,0:T(8,128)S(1)} %get-tuple-element.32), channel_id=1, source_target_pairs={{0,4},{4,0},{8,12},{12,8},{16,20},{20,16},{24,28},{28,24},{1,5},{5... | collective-permute-start | bytes 147464 | tf_op jit(solution)/shard_map/ppermute | solution.py:562
  6.2 6.8 %collective-permute-start.1 = (f32[96,128]{1,0:T(8,128)S(1)}, f32[96,128]{1,0:T(8,128)S(1)}, u32[]{:S(2)}, u32[]{:S(2)}) collective-permute-start(f32[96,128]{1,0:T(8,128)S(1)} %get-tuple-element.33), channel_id=1, source_target_pairs={{4,8},{8,4},{12,16},{16,12},{20,24},{24,20},{28,0},{0,28},{5,9},{9... | collective-permute-start | bytes 147464 | tf_op jit(solution)/shard_map/ppermute | solution.py:561
  9.8 1.7 %copy-start.1 = (bf16[1,16,9,64,128]{4,3,2,1,0:T(8,128)(2,1)S(1)}, bf16[1,16,9,64,128]{4,3,2,1,0:T(8,128)(2,1)}, u32[]{:S(2)}) copy-start(bf16[1,16,9,64,128]{4,3,2,1,0:T(8,128)(2,1)} %refs_1_.1) | copy-start | bytes 7077892
  13.6 13.5 %copy-start = (f32[1,16,64,128]{3,2,1,0:T(8,128)S(1)}, f32[1,16,64,128]{3,2,1,0:T(8,128)}, u32[]{:S(2)}) copy-start(f32[1,16,64,128]{3,2,1,0:T(8,128)} %param.5) | copy-start | bytes 1572868
  13.6 7.5 %collective-permute-start.7 = (f32[192,128]{1,0:T(8,128)S(1)}, f32[192,128]{1,0:T(8,128)S(1)}, u32[]{:S(2)}, u32[]{:S(2)}) collective-permute-start(f32[192,128]{1,0:T(8,128)S(1)} %get-tuple-element.34.refs_1_.refs_7_), channel_id=1, source_target_pairs={{1,2},{2,1},{3,0},{0,3},{5,6},{6,5},{7,4},{4,7},{9,10},{10,9},{11,... | collective-permute-start | bytes 294920 | tf_op jit(solution)/shard_map/ppermute | solution.py:563
  13.7 7.4 %collective-permute-start.6 = (f32[192,128]{1,0:T(8,128)S(1)}, f32[192,128]{1,0:T(8,128)S(1)}, u32[]{:S(2)}, u32[]{:S(2)}) collective-permute-start(f32[192,128]{1,0:T(8,128)S(1)} %get-tuple-element.34.refs_1_.refs_7_), channel_id=1, source_target_pairs={{0,1},{1,0},{2,3},{3,2},{4,5},{5,4},{6,7},{7,6},{8,9},{9,8},{10,11... | collective-permute-start | bytes 294920 | tf_op jit(solution)/shard_map/ppermute | solution.py:564
  14.3 5.1 %collective-permute-start.4 = (f32[96,128]{1,0:T(8,128)S(1)}, f32[96,128]{1,0:T(8,128)S(1)}, u32[]{:S(2)}, u32[]{:S(2)}) collective-permute-start(f32[96,128]{1,0:T(8,128)S(1)} %get-tuple-element.37), channel_id=1, source_target_pairs={{0,4},{4,0},{8,12},{12,8},{16,20},{20,16},{24,28},{28,24},{1,5},{5... | collective-permute-start | bytes 147464 | tf_op jit(solution)/shard_map/ppermute | solution.py:562
  14.3 6.8 %collective-permute-start.5 = (f32[96,128]{1,0:T(8,128)S(1)}, f32[96,128]{1,0:T(8,128)S(1)}, u32[]{:S(2)}, u32[]{:S(2)}) collective-permute-start(f32[96,128]{1,0:T(8,128)S(1)} %get-tuple-element.38), channel_id=1, source_target_pairs={{4,8},{8,4},{12,16},{16,12},{20,24},{24,20},{28,0},{0,28},{5,9},{9... | collective-permute-start | bytes 147464 | tf_op jit(solution)/shard_map/ppermute | solution.py:561
  21.6 8.7 %collective-permute-start.11 = (f32[192,128]{1,0:T(8,128)S(1)}, f32[192,128]{1,0:T(8,128)S(1)}, u32[]{:S(2)}, u32[]{:S(2)}) collective-permute-start(f32[192,128]{1,0:T(8,128)S(1)} %get-tuple-element.39.refs_2_.refs_8_), channel_id=1, source_target_pairs={{1,2},{2,1},{3,0},{0,3},{5,6},{6,5},{7,4},{4,7},{9,10},{10,9},{11,... | collective-permute-start | bytes 294920 | tf_op jit(solution)/shard_map/ppermute | solution.py:563
  21.7 8.6 %collective-permute-start.10 = (f32[192,128]{1,0:T(8,128)S(1)}, f32[192,128]{1,0:T(8,128)S(1)}, u32[]{:S(2)}, u32[]{:S(2)}) collective-permute-start(f32[192,128]{1,0:T(8,128)S(1)} %get-tuple-element.39.refs_2_.refs_8_), channel_id=1, source_target_pairs={{0,1},{1,0},{2,3},{3,2},{4,5},{5,4},{6,7},{7,6},{8,9},{9,8},{10,11... | collective-permute-start | bytes 294920 | tf_op jit(solution)/shard_map/ppermute | solution.py:564
  23.3 5.7 %collective-permute-start.8 = (f32[96,128]{1,0:T(8,128)S(1)}, f32[96,128]{1,0:T(8,128)S(1)}, u32[]{:S(2)}, u32[]{:S(2)}) collective-permute-start(f32[96,128]{1,0:T(8,128)S(1)} %get-tuple-element.41), channel_id=1, source_target_pairs={{0,4},{4,0},{8,12},{12,8},{16,20},{20,16},{24,28},{28,24},{1,5},{5... | collective-permute-start | bytes 147464 | tf_op jit(solution)/shard_map/ppermute | solution.py:562
  23.5 6.8 %collective-permute-start.9 = (f32[96,128]{1,0:T(8,128)S(1)}, f32[96,128]{1,0:T(8,128)S(1)}, u32[]{:S(2)}, u32[]{:S(2)}) collective-permute-start(f32[96,128]{1,0:T(8,128)S(1)} %get-tuple-element.42), channel_id=1, source_target_pairs={{4,8},{8,4},{12,16},{16,12},{20,24},{24,20},{28,0},{0,28},{5,9},{9... | collective-permute-start | bytes 147464 | tf_op jit(solution)/shard_map/ppermute | solution.py:561
  30.8 7.5 %collective-permute-start.15 = (f32[192,128]{1,0:T(8,128)S(1)}, f32[192,128]{1,0:T(8,128)S(1)}, u32[]{:S(2)}, u32[]{:S(2)}) collective-permute-start(f32[192,128]{1,0:T(8,128)S(1)} %get-tuple-element.43.refs_3_.refs_9_), channel_id=1, source_target_pairs={{1,2},{2,1},{3,0},{0,3},{5,6},{6,5},{7,4},{4,7},{9,10},{10,9},{11,... | collective-permute-start | bytes 294920 | tf_op jit(solution)/shard_map/ppermute | solution.py:563
  30.9 7.4 %collective-permute-start.14 = (f32[192,128]{1,0:T(8,128)S(1)}, f32[192,128]{1,0:T(8,128)S(1)}, u32[]{:S(2)}, u32[]{:S(2)}) collective-permute-start(f32[192,128]{1,0:T(8,128)S(1)} %get-tuple-element.43.refs_3_.refs_9_), channel_id=1, source_target_pairs={{0,1},{1,0},{2,3},{3,2},{4,5},{5,4},{6,7},{7,6},{8,9},{9,8},{10,11... | collective-permute-start | bytes 294920 | tf_op jit(solution)/shard_map/ppermute | solution.py:564
  31.5 5.6 %collective-permute-start.12 = (f32[96,128]{1,0:T(8,128)S(1)}, f32[96,128]{1,0:T(8,128)S(1)}, u32[]{:S(2)}, u32[]{:S(2)}) collective-permute-start(f32[96,128]{1,0:T(8,128)S(1)} %get-tuple-element.46), channel_id=1, source_target_pairs={{0,4},{4,0},{8,12},{12,8},{16,20},{20,16},{24,28},{28,24},{1,5},{5... | collective-permute-start | bytes 147464 | tf_op jit(solution)/shard_map/ppermute | solution.py:562
  31.5 6.8 %collective-permute-start.13 = (f32[96,128]{1,0:T(8,128)S(1)}, f32[96,128]{1,0:T(8,128)S(1)}, u32[]{:S(2)}, u32[]{:S(2)}) collective-permute-start(f32[96,128]{1,0:T(8,128)S(1)} %get-tuple-element.47), channel_id=1, source_target_pairs={{4,8},{8,4},{12,16},{16,12},{20,24},{24,20},{28,0},{0,28},{5,9},{9... | collective-permute-start | bytes 147464 | tf_op jit(solution)/shard_map/ppermute | solution.py:561
  36.1 11.1 %collective-permute-start.20 = (f32[192,128]{1,0:T(8,128)S(1)}, f32[192,128]{1,0:T(8,128)S(1)}, u32[]{:S(2)}, u32[]{:S(2)}) collective-permute-start(f32[192,128]{1,0:T(8,128)S(1)} %get-tuple-element.52.refs_5_), channel_id=1, source_target_pairs={{0,3},{1,2},{2,1},{3,0},{4,7},{5,6},{6,5},{7,4},{8,11},{9,10},{10,... | collective-permute-start | bytes 294920 | tf_op jit(solution)/shard_map/ppermute | solution.py:555
  37.0 15.0 %collective-permute-start.18 = (f32[192,128]{1,0:T(8,128)S(1)}, f32[192,128]{1,0:T(8,128)S(1)}, u32[]{:S(2)}, u32[]{:S(2)}) collective-permute-start(f32[192,128]{1,0:T(8,128)S(1)} %get-tuple-element.52.refs_5_), channel_id=1, source_target_pairs={{0,2},{1,3},{2,0},{3,1},{4,6},{5,7},{6,4},{7,5},{8,10},{9,11},{10,... | collective-permute-start | bytes 294920 | tf_op jit(solution)/shard_map/ppermute | solution.py:555
  38.3 13.8 %collective-permute-start.16 = (f32[192,128]{1,0:T(8,128)S(1)}, f32[192,128]{1,0:T(8,128)S(1)}, u32[]{:S(2)}, u32[]{:S(2)}) collective-permute-start(f32[192,128]{1,0:T(8,128)S(1)} %get-tuple-element.52.refs_5_), channel_id=1, source_target_pairs={{0,1},{1,0},{2,3},{3,2},{4,5},{5,4},{6,7},{7,6},{8,9},{9,8},{10,11... | collective-permute-start | bytes 294920 | tf_op jit(solution)/shard_map/ppermute | solution.py:555
  39.6 12.4 %all-to-all-start = ((f32[32,3,128]{2,1,0:T(4,128)}), f32[32,3,128]{2,1,0:T(4,128)S(1)}, u32[]{:S(2)}, u32[]{:S(2)}) async-start(f32[32,3,128]{2,1,0:T(4,128)} %get-tuple-element.51), calls=%async_computation | async-start | bytes 131072 | tf_op jit(solution)/shard_map/all_to_all | solution.py:626
  45.2 6.9 %collective-permute-start.21 = (f32[48,128]{1,0:T(8,128)S(1)}, f32[48,128]{1,0:T(8,128)S(1)}, u32[]{:S(2)}, u32[]{:S(2)}) collective-permute-start(f32[48,128]{1,0:T(8,128)S(1)} %shard_map.59.refs_6_), channel_id=1, source_target_pairs={{0,3},{1,2},{2,1},{3,0},{4,7},{5,6},{6,5},{7,4},{8,11},{9,10},{10,... | collective-permute-start | bytes 73736 | tf_op jit(solution)/shard_map/ppermute | solution.py:555
  46.8 5.3 %collective-permute-start.19 = (f32[48,128]{1,0:T(8,128)S(1)}, f32[48,128]{1,0:T(8,128)S(1)}, u32[]{:S(2)}, u32[]{:S(2)}) collective-permute-start(f32[48,128]{1,0:T(8,128)S(1)} %shard_map.59.refs_6_), channel_id=1, source_target_pairs={{0,2},{1,3},{2,0},{3,1},{4,6},{5,7},{6,4},{7,5},{8,10},{9,11},{10,... | collective-permute-start | bytes 73736 | tf_op jit(solution)/shard_map/ppermute | solution.py:555
  47.2 4.9 %collective-permute-start.17 = (f32[48,128]{1,0:T(8,128)S(1)}, f32[48,128]{1,0:T(8,128)S(1)}, u32[]{:S(2)}, u32[]{:S(2)}) collective-permute-start(f32[48,128]{1,0:T(8,128)S(1)} %shard_map.59.refs_6_), channel_id=1, source_target_pairs={{0,1},{1,0},{2,3},{3,2},{4,5},{5,4},{6,7},{7,6},{8,9},{9,8},{10,11... | collective-permute-start | bytes 73736 | tf_op jit(solution)/shard_map/ppermute | solution.py:555

commit v6 on v5

--- a/solution.py
+++ b/solution.py
@@ -113,26 +113,24 @@
 
 
 def gram_columns(power, refs, period):
-    width = refs[0].shape[-1]
-    rows = refs[0].shape[0]
+    rows, width = refs[0].shape
     lanes = lax.broadcasted_iota(jnp.int32, (period, width), 1)
     sign = lane_sign(width)
+    sums = {}
+    for base in range(0, rows, period):
+        mine = refs[power][base : base + period, :]
+        turned = pltpu.roll(mine, width // 2, 1)
+        for other, real_lane, imag_lane in pair_slots(power):
+            theirs = mine if other == power else refs[other][base : base + period, :]
+            for lane, factor in ((real_lane, mine), (imag_lane, turned)):
+                if lane is not None:
+                    term = factor * theirs
+                    sums[lane] = sums[lane] + term if lane in sums else term
     out = jnp.zeros((period, width), jnp.float32)
-    for other, real_lane, imag_lane in pair_slots(power):
-        real_sum = None
-        imag_sum = None
-        for base in range(0, rows, period):
-            mine = refs[power][base : base + period, :]
-            theirs = refs[other][base : base + period, :]
-            real_term = mine * theirs
-            real_sum = real_term if real_sum is None else real_sum + real_term
-            if imag_lane is not None:
-                turned = pltpu.roll(theirs, width // 2, 1)
-                imag_term = mine * turned
-                imag_sum = imag_term if imag_sum is None else imag_sum + imag_term
-        out = out + columns_of(real_sum, lanes, real_lane)
+    for _, real_lane, imag_lane in pair_slots(power):
+        out = out + columns_of(sums[real_lane], lanes, real_lane)
         if imag_lane is not None:
-            out = out + columns_of(imag_sum * sign, lanes, imag_lane)
+            out = out - columns_of(sums[imag_lane] * sign, lanes, imag_lane)
     return out
 
 
@@ -404,16 +402,13 @@
         period *= 2
     per_row = width // SLOT
     packed_rows = packed.shape[0]
-    turn_ref[...] = jnp.zeros_like(turn_ref)
+    turn_ref[0:LANES_EACH, :] = jnp.zeros((LANES_EACH, width), jnp.float32)
     turn_ref[0:packed_rows, :] = packed[...]
-    turned = jnp.transpose(turn_ref[...])
-    lane = lax.broadcasted_iota(jnp.int32, (SLOT, width), 1)
-    quantities = jnp.zeros((SLOT, width), jnp.float32)
+    turned = jnp.transpose(turn_ref[0:LANES_EACH, :])
+    line_ref[...] = jnp.zeros_like(line_ref)
     for m in range(per_row):
-        part = turned[SLOT * m : SLOT * m + SLOT]
-        moved = pltpu.roll(part, LANES_EACH * m, 1) if m else part
-        inside = (lane >= LANES_EACH * m) & (lane < LANES_EACH * m + LANES_EACH)
-        quantities = jnp.where(inside, moved, quantities)
+        line_ref[:, LANES_EACH * m : LANES_EACH * m + LANES_EACH] = turned[SLOT * m : SLOT * m + SLOT]
+    quantities = line_ref[...]
 
     def quantity(at):
         return jnp.broadcast_to(quantities[at : at + 1], (8, width))
@@ -435,7 +430,7 @@
     line_ref[...] = jnp.zeros_like(line_ref)
     for at, part in enumerate(parts):
         line_ref[at : at + 1, :] = part[0:1]
-    turn_ref[...] = jnp.transpose(line_ref[...])
+    turn_ref[:, 0:SLOT] = jnp.transpose(line_ref[...])
     for r in range(rhs):
         j, m = divmod(r, per_row)
         source = turn_ref[LANES_EACH * m + j : LANES_EACH * m + j + 1, :]
@@ -623,7 +618,7 @@
         if not last:
             up_send, down_send = outs[1:]
         else:
-            swapped = lax.all_to_all(outs[1], ("wide", "narrow"), 0, 0)
+            swapped = lax.all_to_all(outs[1], ("narrow", "wide"), 0, 0)
             coarse = call(
                 functools.partial(tail_kernel, YLOC, rhs),
                 jax.ShapeDtypeStruct((coarse_rows, width), f32),
@@ -633,7 +628,6 @@
             groups.append(1)
             sent.append(to_all_times(coarse))
     totals = jnp.sum(swapped, axis=0)
-    square = pltpu.VMEM((width, width), f32)
     solution_rows, slices = call(
         functools.partial(final_kernel, sites, rhs, tuple(groups)),
         [field_shape, jax.ShapeDtypeStruct((narrow, coarse_rows, width), f32)],
@@ -643,8 +637,8 @@
         scratch=[
             pltpu.VMEM((total_rows, width), f32),
             pltpu.VMEM((coarse_rows, width), f32),
-            square,
-            square,
+            pltpu.VMEM((width, width), f32),
+            pltpu.VMEM((SLOT, width), f32),
             pltpu.VMEM((period, width), f32),
         ],
     )

time: 53.6 us -> 53.5 us (level)
  no operation moved by 1% of the time
where the time goes in v6:
time: 53.5 us; the launch traced here: 53.3 us
  starting transfers between devices  30.9 us (58%)
  Pallas kernels  10 us (19%)
  waiting for transfers between devices  9.08 us (17%)
  local copies, waits for them, and re-layouts  2.55 us (5%)
  between operations  0.78 us (1%)
    ppermute x4, starting transfers between devices, per_device(): side_b = lax.ppermute(down_send, 'wide', swap_pairs(wide, 1, rows_y))  14.3 us
    pallas_call x11, Pallas kernels, call(): pl.pallas_call(kernel, out_shape=outs, in_specs=vmem(len(args)), out_spec...  10 us
    all_to_all x1, starting transfers between devices, per_device(): swapped = lax.all_to_all(outs[1], ('narrow', 'wide'), 0, 0)  5 us
    all_to_all x1, waiting for transfers between devices, per_device(): swapped = lax.all_to_all(outs[1], ('narrow', 'wide'), 0, 0)  4.72 us
    ppermute x4, waiting for transfers between devices, per_device(): side_b = lax.ppermute(down_send, 'wide', swap_pairs(wide, 1, rows_y))  4.31 us
    ppermute x6, starting transfers between devices, to_all_times(): lax.ppermute(value, 'narrow', [(i, i ^ k) for i in range(narrow)])  3.63 us
    ppermute x4, starting transfers between devices, per_device(): time_a = lax.ppermute(field, 'narrow', swap_pairs(narrow, 0))  3.52 us
    ppermute x4, starting transfers between devices, per_device(): time_b = lax.ppermute(field, 'narrow', swap_pairs(narrow, 1))  2.71 us
  transfers between devices with their start and end apart: 23, of which 5 were waited for; matrix products, arithmetic and copies ran while one was open for 0% of the time, Pallas kernels for 13%

profile of v6, /device:TPU:0, one launch (start us, length us, event | category | flops | bytes accessed | tf_op | source)
XLA Modules:
  0.0 53.3 jit_solution(14245389783489893959)
XLA Ops:
  0.6 0.0 copy-start.2
  0.6 0.9 %copy-done.2 = f32[1,16,12,128]{3,1,2,0:T(8,128)S(1)} copy-done((f32[1,16,12,128]{3,1,2,0:T(8,128)S(1)}, f32[1,16,12,128]{3,1,2,0:T(8,128)}, u32[]{:S(2)}) %copy-start.2) | copy-done | bytes 98328
  1.5 0.1 shard_map.50
  1.6 2.5 %collective-permute-start.3 = (f32[192,128]{1,0:T(8,128)S(1)}, f32[192,128]{1,0:T(8,128)S(1)}, u32[]{:S(2)}, u32[]{:S(2)}) collective-permute-start(f32[192,128]{1,0:T(8,128)S(1)} %get-tuple-element.29.refs_0_.refs_6_), channel_id=1, source_target_pairs={{1,2},{2,1},{3,0},{0,3},{5,6},{6,5},{7,4},{4,7},{9,10},{10,9},{11,... | collective-permute-start | bytes 294920 | tf_op jit(solution)/shard_map/ppermute | solution.py:558
  4.1 0.7 %collective-permute-start.2 = (f32[192,128]{1,0:T(8,128)S(1)}, f32[192,128]{1,0:T(8,128)S(1)}, u32[]{:S(2)}, u32[]{:S(2)}) collective-permute-start(f32[192,128]{1,0:T(8,128)S(1)} %get-tuple-element.29.refs_0_.refs_6_), channel_id=1, source_target_pairs={{0,1},{1,0},{2,3},{3,2},{4,5},{5,4},{6,7},{7,6},{8,9},{9,8},{10,11... | collective-permute-start | bytes 294920 | tf_op jit(solution)/shard_map/ppermute | solution.py:559
  4.8 1.5 %collective-permute-start = (f32[96,128]{1,0:T(8,128)S(1)}, f32[96,128]{1,0:T(8,128)S(1)}, u32[]{:S(2)}, u32[]{:S(2)}) collective-permute-start(f32[96,128]{1,0:T(8,128)S(1)} %get-tuple-element.32), channel_id=1, source_target_pairs={{0,4},{4,0},{8,12},{12,8},{16,20},{20,16},{24,28},{28,24},{1,5},{5... | collective-permute-start | bytes 147464 | tf_op jit(solution)/shard_map/ppermute | solution.py:557
  6.2 3.6 %collective-permute-start.1 = (f32[96,128]{1,0:T(8,128)S(1)}, f32[96,128]{1,0:T(8,128)S(1)}, u32[]{:S(2)}, u32[]{:S(2)}) collective-permute-start(f32[96,128]{1,0:T(8,128)S(1)} %get-tuple-element.33), channel_id=1, source_target_pairs={{4,8},{8,4},{12,16},{16,12},{20,24},{24,20},{28,0},{0,28},{5,9},{9... | collective-permute-start | bytes 147464 | tf_op jit(solution)/shard_map/ppermute | solution.py:556
  9.8 0.0 copy-start.1
  9.8 1.7 %copy-done.1 = bf16[1,16,9,64,128]{4,3,2,1,0:T(8,128)(2,1)S(1)} copy-done((bf16[1,16,9,64,128]{4,3,2,1,0:T(8,128)(2,1)S(1)}, bf16[1,16,9,64,128]{4,3,2,1,0:T(8,128)(2,1)}, u32[]{:S(2)}) %copy-start.1) | copy-done | bytes 2359320
  11.5 0.8 %shard_map.51 = (f32[192,128]{1,0:T(8,128)S(1)}, bf16[1,16,9,64,128]{4,3,2,1,0:T(8,128)(2,1)S(1)}) custom-call(f32[192,128]{1,0:T(8,128)S(1)} %get-tuple-element.29.refs_0_.refs_6_, bf16[1,16,9,64,128]{4,3,2,1,0:T(8,128)(2,1)S(1)} %copy-done.1), custom_call_target="tpu_custom_call" | custom-call | tf_op jit(solution)/shard_map/pallas_call | solution.py:486
  12.3 0.0 collective-permute-done.refs_2_
  12.3 0.8 %collective-permute-done.1.refs_3_ = f32[96,128]{1,0:T(8,128)S(1)} collective-permute-done((f32[96,128]{1,0:T(8,128)S(1)}, f32[96,128]{1,0:T(8,128)S(1)}, u32[]{:S(2)}, u32[]{:S(2)}) %collective-permute-start.1) | collective-permute-done | bytes 49184 | tf_op jit(solution)/shard_map/ppermute | solution.py:556
  13.0 0.0 collective-permute-done.3.refs_5_
  13.0 0.0 collective-permute-done.2.refs_4_
  13.0 0.6 %shard_map.52 = (f32[192,128]{1,0:T(8,128)S(1)}, f32[96,128]{1,0:T(8,128)S(1)}, f32[96,128]{1,0:T(8,128)S(1)}) custom-call(f32[192,128]{1,0:T(8,128)S(1)} %get-tuple-element.30.refs_0_, bf16[1,16,9,64,128]{4,3,2,1,0:T(8,128)(2,1)S(1)} %get-tuple-element.31.refs_1_.refs_2_.refs_3_.refs_4_, f32[96,128]{1,0:T(8,128)S(1)} %collective-permute-done.refs_2_, ...), custom_call_target="tpu_custom_call" | custom-call | tf_op jit(solution)/shard_map/pallas_call | solution.py:486
  13.6 0.0 copy-start
  13.6 0.1 collective-permute-start.7
  13.7 0.6 %collective-permute-start.6 = (f32[192,128]{1,0:T(8,128)S(1)}, f32[192,128]{1,0:T(8,128)S(1)}, u32[]{:S(2)}, u32[]{:S(2)}) collective-permute-start(f32[192,128]{1,0:T(8,128)S(1)} %get-tuple-element.34.refs_1_.refs_7_), channel_id=1, source_target_pairs={{0,1},{1,0},{2,3},{3,2},{4,5},{5,4},{6,7},{7,6},{8,9},{9,8},{10,11... | collective-permute-start | bytes 294920 | tf_op jit(solution)/shard_map/ppermute | solution.py:559
  14.3 0.0 collective-permute-start.4
  14.3 3.6 %collective-permute-start.5 = (f32[96,128]{1,0:T(8,128)S(1)}, f32[96,128]{1,0:T(8,128)S(1)}, u32[]{:S(2)}, u32[]{:S(2)}) collective-permute-start(f32[96,128]{1,0:T(8,128)S(1)} %get-tuple-element.38), channel_id=1, source_target_pairs={{4,8},{8,4},{12,16},{16,12},{20,24},{24,20},{28,0},{0,28},{5,9},{9... | collective-permute-start | bytes 147464 | tf_op jit(solution)/shard_map/ppermute | solution.py:556
  17.9 1.5 %shard_map.53 = (f32[192,128]{1,0:T(8,128)S(1)}, bf16[16,384,128]{2,1,0:T(8,128)(2,1)S(1)}, f32[24,128]{1,0:T(8,128)S(1)}) custom-call(f32[192,128]{1,0:T(8,128)S(1)} %get-tuple-element.29.refs_0_.refs_6_, f32[192,128]{1,0:T(8,128)S(1)} %get-tuple-element.34.refs_1_.refs_7_, bf16[1,16,9,64,128]{4,3,2,1,0:T(8,128)(2,1)S(1)} %get-tuple-element.31.refs_1_.refs_2_.refs_3_.refs_4_), custom_call_target="tpu_custom_call" | custom-call | tf_op jit(solution)/shard_map/pallas_call | solution.py:486
  19.4 0.0 collective-permute-done.4.refs_2_
  19.4 1.7 %collective-permute-done.5.refs_3_ = f32[96,128]{1,0:T(8,128)S(1)} collective-permute-done((f32[96,128]{1,0:T(8,128)S(1)}, f32[96,128]{1,0:T(8,128)S(1)}, u32[]{:S(2)}, u32[]{:S(2)}) %collective-permute-start.5) | collective-permute-done | bytes 49184 | tf_op jit(solution)/shard_map/ppermute | solution.py:556
  21.1 0.0 collective-permute-done.7.refs_5_
  21.1 0.0 collective-permute-done.6.refs_4_
  21.1 0.5 shard_map.54
  21.6 0.1 collective-permute-start.11
  21.7 1.6 %collective-permute-start.10 = (f32[192,128]{1,0:T(8,128)S(1)}, f32[192,128]{1,0:T(8,128)S(1)}, u32[]{:S(2)}, u32[]{:S(2)}) collective-permute-start(f32[192,128]{1,0:T(8,128)S(1)} %get-tuple-element.39.refs_2_.refs_8_), channel_id=1, source_target_pairs={{0,1},{1,0},{2,3},{3,2},{4,5},{5,4},{6,7},{7,6},{8,9},{9,8},{10,11... | collective-permute-start | bytes 294920 | tf_op jit(solution)/shard_map/ppermute | solution.py:559
  23.3 0.2 collective-permute-start.8
  23.5 3.6 %collective-permute-start.9 = (f32[96,128]{1,0:T(8,128)S(1)}, f32[96,128]{1,0:T(8,128)S(1)}, u32[]{:S(2)}, u32[]{:S(2)}) collective-permute-start(f32[96,128]{1,0:T(8,128)S(1)} %get-tuple-element.42), channel_id=1, source_target_pairs={{4,8},{8,4},{12,16},{16,12},{20,24},{24,20},{28,0},{0,28},{5,9},{9... | collective-permute-start | bytes 147464 | tf_op jit(solution)/shard_map/ppermute | solution.py:556
  27.1 0.0 copy-done
  27.1 1.8 %shard_map.55 = (f32[192,128]{1,0:T(8,128)S(1)}, f32[144,128]{1,0:T(8,128)S(1)}, f32[24,128]{1,0:T(8,128)S(1)}) custom-call(f32[192,128]{1,0:T(8,128)S(1)} %get-tuple-element.29.refs_0_.refs_6_, f32[192,128]{1,0:T(8,128)S(1)} %get-tuple-element.34.refs_1_.refs_7_, f32[192,128]{1,0:T(8,128)S(1)} %get-tuple-element.39.refs_2_.refs_8_, ...), custom_call_target="tpu_custom_call" | custom-call | tf_op jit(solution)/shard_map/pallas_call | solution.py:486
  28.9 0.0 collective-permute-done.8.refs_2_
  28.9 1.3 %collective-permute-done.9.refs_3_ = f32[96,128]{1,0:T(8,128)S(1)} collective-permute-done((f32[96,128]{1,0:T(8,128)S(1)}, f32[96,128]{1,0:T(8,128)S(1)}, u32[]{:S(2)}, u32[]{:S(2)}) %collective-permute-start.9) | collective-permute-done | bytes 49184 | tf_op jit(solution)/shard_map/ppermute | solution.py:556
  30.3 0.0 collective-permute-done.11.refs_5_
  30.3 0.0 collective-permute-done.10.refs_4_
  30.3 0.5 shard_map.56
  30.8 0.1 collective-permute-start.15
  30.9 0.6 %collective-permute-start.14 = (f32[192,128]{1,0:T(8,128)S(1)}, f32[192,128]{1,0:T(8,128)S(1)}, u32[]{:S(2)}, u32[]{:S(2)}) collective-permute-start(f32[192,128]{1,0:T(8,128)S(1)} %get-tuple-element.43.refs_3_.refs_9_), channel_id=1, source_target_pairs={{0,1},{1,0},{2,3},{3,2},{4,5},{5,4},{6,7},{7,6},{8,9},{9,8},{10,11... | collective-permute-start | bytes 294920 | tf_op jit(solution)/shard_map/ppermute | solution.py:559
  31.5 0.0 collective-permute-start.12
  31.5 3.6 %collective-permute-start.13 = (f32[96,128]{1,0:T(8,128)S(1)}, f32[96,128]{1,0:T(8,128)S(1)}, u32[]{:S(2)}, u32[]{:S(2)}) collective-permute-start(f32[96,128]{1,0:T(8,128)S(1)} %get-tuple-element.47), channel_id=1, source_target_pairs={{4,8},{8,4},{12,16},{16,12},{20,24},{24,20},{28,0},{0,28},{5,9},{9... | collective-permute-start | bytes 147464 | tf_op jit(solution)/shard_map/ppermute | solution.py:556
  35.0 1.0 %shard_map.57 = (f32[192,128]{1,0:T(8,128)S(1)}, f32[192,128]{1,0:T(8,128)S(1)}, f32[24,128]{1,0:T(8,128)S(1)}) custom-call(f32[192,128]{1,0:T(8,128)S(1)} %get-tuple-element.29.refs_0_.refs_6_, f32[192,128]{1,0:T(8,128)S(1)} %get-tuple-element.34.refs_1_.refs_7_, f32[192,128]{1,0:T(8,128)S(1)} %get-tuple-element.39.refs_2_.refs_8_, ...), custom_call_target="tpu_custom_call" | custom-call | tf_op jit(solution)/shard_map/pallas_call | solution.py:486
  36.1 0.9 %collective-permute-start.20 = (f32[192,128]{1,0:T(8,128)S(1)}, f32[192,128]{1,0:T(8,128)S(1)}, u32[]{:S(2)}, u32[]{:S(2)}) collective-permute-start(f32[192,128]{1,0:T(8,128)S(1)} %get-tuple-element.52.refs_5_), channel_id=1, source_target_pairs={{0,3},{1,2},{2,1},{3,0},{4,7},{5,6},{6,5},{7,4},{8,11},{9,10},{10,... | collective-permute-start | bytes 294920 | tf_op jit(solution)/shard_map/ppermute | solution.py:550
  37.0 0.0 collective-permute-done.12.refs_2_
  37.0 0.8 %collective-permute-start.18 = (f32[192,128]{1,0:T(8,128)S(1)}, f32[192,128]{1,0:T(8,128)S(1)}, u32[]{:S(2)}, u32[]{:S(2)}) collective-permute-start(f32[192,128]{1,0:T(8,128)S(1)} %get-tuple-element.52.refs_5_), channel_id=1, source_target_pairs={{0,2},{1,3},{2,0},{3,1},{4,6},{5,7},{6,4},{7,5},{8,10},{9,11},{10,... | collective-permute-start | bytes 294920 | tf_op jit(solution)/shard_map/ppermute | solution.py:550
  37.8 0.5 collective-permute-done.13.refs_3_
  38.3 0.0 collective-permute-start.16
  38.3 0.0 collective-permute-done.15.refs_5_
  38.3 0.0 collective-permute-done.14.refs_4_
  38.3 1.4 %shard_map.58 = (f32[192,128]{1,0:T(8,128)S(1)}, f32[32,3,128]{2,1,0:T(4,128)}) custom-call(f32[192,128]{1,0:T(8,128)S(1)} %get-tuple-element.45.refs_0_, bf16[16,384,128]{2,1,0:T(8,128)(2,1)S(1)} %get-tuple-element.36.refs_1_, f32[96,128]{1,0:T(8,128)S(1)} %collective-permute-done.12.refs_2_, f32[96,128]{1,0:T(8,128)S(1)} %collective-permute-done.13.refs_3_, ...), custom_call_target="tpu_custom_call" | custom-call | tf_op jit(solution)/shard_map/pallas_call | solution.py:486
  39.6 5.0 %all-to-all-start = ((f32[32,3,128]{2,1,0:T(4,128)}), f32[32,3,128]{2,1,0:T(4,128)S(1)}, u32[]{:S(2)}, u32[]{:S(2)}) async-start(f32[32,3,128]{2,1,0:T(4,128)} %get-tuple-element.51), calls=%async_computation | async-start | bytes 131072 | tf_op jit(solution)/shard_map/all_to_all | solution.py:621
  44.7 0.6 %shard_map.59.refs_6_ = f32[48,128]{1,0:T(8,128)S(1)} custom-call(f32[192,128]{1,0:T(8,128)S(1)} %get-tuple-element.53.field_ref, f32[16,64,128]{2,1,0:T(8,128)S(1)} %bitcast.14), custom_call_target="tpu_custom_call" | custom-call | tf_op jit(solution)/shard_map/pallas_call | solution.py:486
  45.3 1.6 %collective-permute-start.21 = (f32[48,128]{1,0:T(8,128)S(1)}, f32[48,128]{1,0:T(8,128)S(1)}, u32[]{:S(2)}, u32[]{:S(2)}) collective-permute-start(f32[48,128]{1,0:T(8,128)S(1)} %shard_map.59.refs_6_), channel_id=1, source_target_pairs={{0,3},{1,2},{2,1},{3,0},{4,7},{5,6},{6,5},{7,4},{8,11},{9,10},{10,... | collective-permute-start | bytes 73736 | tf_op jit(solution)/shard_map/ppermute | solution.py:550
  46.8 0.4 collective-permute-start.19
  47.2 0.0 collective-permute-done.20.refs_11_
  47.2 0.0 collective-permute-start.17
  47.2 4.7 %all-to-all-done = f32[32,3,128]{2,1,0:T(4,128)S(1)} async-done(((f32[32,3,128]{2,1,0:T(4,128)}), f32[32,3,128]{2,1,0:T(4,128)S(1)}, u32[]{:S(2)}, u32[]{:S(2)}) %all-to-all-start) | async-done | bytes 49184 | tf_op jit(solution)/shard_map/all_to_all | solution.py:621
  52.0 0.0 collective-permute-done.18.refs_9_
  52.0 0.0 collective-permute-done.16.refs_7_
  52.0 0.0 collective-permute-done.21.refs_12_
  52.0 0.0 collective-permute-done.19.refs_10_
  52.0 0.0 collective-permute-done.17.refs_8_
  52.0 1.3 %shard_map.60 = (f32[192,128]{1,0:T(8,128)}, f32[4,48,128]{2,1,0:T(8,128)}) custom-call(f32[192,128]{1,0:T(8,128)S(1)} %get-tuple-element.29.refs_0_.refs_6_, f32[192,128]{1,0:T(8,128)S(1)} %get-tuple-element.34.refs_1_.refs_7_, f32[192,128]{1,0:T(8,128)S(1)} %get-tuple-element.39.refs_2_.refs_8_, f32[192,128]{1,0:T(8,128)S(1)} %get-tuple-element.43.refs_3_.refs_9_, ...), custom_call_target="tpu_custom_call" | custom-call | tf_op jit(solution)/shard_map/pallas_call | solution.py:486
  (1 shorter events, 0.0 us)
Async XLA Ops:
  0.6 0.9 %copy-start.2 = (f32[1,16,12,128]{3,1,2,0:T(8,128)S(1)}, f32[1,16,12,128]{3,1,2,0:T(8,128)}, u32[]{:S(2)}) copy-start(f32[1,16,12,128]{3,1,2,0:T(8,128)} %param.3) | copy-start | bytes 294916
  1.6 11.5 %collective-permute-start.3 = (f32[192,128]{1,0:T(8,128)S(1)}, f32[192,128]{1,0:T(8,128)S(1)}, u32[]{:S(2)}, u32[]{:S(2)}) collective-permute-start(f32[192,128]{1,0:T(8,128)S(1)} %get-tuple-element.29.refs_0_.refs_6_), channel_id=1, source_target_pairs={{1,2},{2,1},{3,0},{0,3},{5,6},{6,5},{7,4},{4,7},{9,10},{10,9},{11,... | collective-permute-start | bytes 294920 | tf_op jit(solution)/shard_map/ppermute | solution.py:558
  4.1 9.0 %collective-permute-start.2 = (f32[192,128]{1,0:T(8,128)S(1)}, f32[192,128]{1,0:T(8,128)S(1)}, u32[]{:S(2)}, u32[]{:S(2)}) collective-permute-start(f32[192,128]{1,0:T(8,128)S(1)} %get-tuple-element.29.refs_0_.refs_6_), channel_id=1, source_target_pairs={{0,1},{1,0},{2,3},{3,2},{4,5},{5,4},{6,7},{7,6},{8,9},{9,8},{10,11... | collective-permute-start | bytes 294920 | tf_op jit(solution)/shard_map/ppermute | solution.py:559
  4.8 7.5 %collective-permute-start = (f32[96,128]{1,0:T(8,128)S(1)}, f32[96,128]{1,0:T(8,128)S(1)}, u32[]{:S(2)}, u32[]{:S(2)}) collective-permute-start(f32[96,128]{1,0:T(8,128)S(1)} %get-tuple-element.32), channel_id=1, source_target_pairs={{0,4},{4,0},{8,12},{12,8},{16,20},{20,16},{24,28},{28,24},{1,5},{5... | collective-permute-start | bytes 147464 | tf_op jit(solution)/shard_map/ppermute | solution.py:557
  6.2 6.8 %collective-permute-start.1 = (f32[96,128]{1,0:T(8,128)S(1)}, f32[96,128]{1,0:T(8,128)S(1)}, u32[]{:S(2)}, u32[]{:S(2)}) collective-permute-start(f32[96,128]{1,0:T(8,128)S(1)} %get-tuple-element.33), channel_id=1, source_target_pairs={{4,8},{8,4},{12,16},{16,12},{20,24},{24,20},{28,0},{0,28},{5,9},{9... | collective-permute-start | bytes 147464 | tf_op jit(solution)/shard_map/ppermute | solution.py:556
  9.8 1.7 %copy-start.1 = (bf16[1,16,9,64,128]{4,3,2,1,0:T(8,128)(2,1)S(1)}, bf16[1,16,9,64,128]{4,3,2,1,0:T(8,128)(2,1)}, u32[]{:S(2)}) copy-start(bf16[1,16,9,64,128]{4,3,2,1,0:T(8,128)(2,1)} %refs_1_.1) | copy-start | bytes 7077892
  13.6 13.5 %copy-start = (f32[1,16,64,128]{3,2,1,0:T(8,128)S(1)}, f32[1,16,64,128]{3,2,1,0:T(8,128)}, u32[]{:S(2)}) copy-start(f32[1,16,64,128]{3,2,1,0:T(8,128)} %param.5) | copy-start | bytes 1572868
  13.6 7.5 %collective-permute-start.7 = (f32[192,128]{1,0:T(8,128)S(1)}, f32[192,128]{1,0:T(8,128)S(1)}, u32[]{:S(2)}, u32[]{:S(2)}) collective-permute-start(f32[192,128]{1,0:T(8,128)S(1)} %get-tuple-element.34.refs_1_.refs_7_), channel_id=1, source_target_pairs={{1,2},{2,1},{3,0},{0,3},{5,6},{6,5},{7,4},{4,7},{9,10},{10,9},{11,... | collective-permute-start | bytes 294920 | tf_op jit(solution)/shard_map/ppermute | solution.py:558
  13.7 7.4 %collective-permute-start.6 = (f32[192,128]{1,0:T(8,128)S(1)}, f32[192,128]{1,0:T(8,128)S(1)}, u32[]{:S(2)}, u32[]{:S(2)}) collective-permute-start(f32[192,128]{1,0:T(8,128)S(1)} %get-tuple-element.34.refs_1_.refs_7_), channel_id=1, source_target_pairs={{0,1},{1,0},{2,3},{3,2},{4,5},{5,4},{6,7},{7,6},{8,9},{9,8},{10,11... | collective-permute-start | bytes 294920 | tf_op jit(solution)/shard_map/ppermute | solution.py:559
  14.3 5.1 %collective-permute-start.4 = (f32[96,128]{1,0:T(8,128)S(1)}, f32[96,128]{1,0:T(8,128)S(1)}, u32[]{:S(2)}, u32[]{:S(2)}) collective-permute-start(f32[96,128]{1,0:T(8,128)S(1)} %get-tuple-element.37), channel_id=1, source_target_pairs={{0,4},{4,0},{8,12},{12,8},{16,20},{20,16},{24,28},{28,24},{1,5},{5... | collective-permute-start | bytes 147464 | tf_op jit(solution)/shard_map/ppermute | solution.py:557
  14.3 6.8 %collective-permute-start.5 = (f32[96,128]{1,0:T(8,128)S(1)}, f32[96,128]{1,0:T(8,128)S(1)}, u32[]{:S(2)}, u32[]{:S(2)}) collective-permute-start(f32[96,128]{1,0:T(8,128)S(1)} %get-tuple-element.38), channel_id=1, source_target_pairs={{4,8},{8,4},{12,16},{16,12},{20,24},{24,20},{28,0},{0,28},{5,9},{9... | collective-permute-start | bytes 147464 | tf_op jit(solution)/shard_map/ppermute | solution.py:556
  21.6 8.7 %collective-permute-start.11 = (f32[192,128]{1,0:T(8,128)S(1)}, f32[192,128]{1,0:T(8,128)S(1)}, u32[]{:S(2)}, u32[]{:S(2)}) collective-permute-start(f32[192,128]{1,0:T(8,128)S(1)} %get-tuple-element.39.refs_2_.refs_8_), channel_id=1, source_target_pairs={{1,2},{2,1},{3,0},{0,3},{5,6},{6,5},{7,4},{4,7},{9,10},{10,9},{11,... | collective-permute-start | bytes 294920 | tf_op jit(solution)/shard_map/ppermute | solution.py:558
  21.7 8.6 %collective-permute-start.10 = (f32[192,128]{1,0:T(8,128)S(1)}, f32[192,128]{1,0:T(8,128)S(1)}, u32[]{:S(2)}, u32[]{:S(2)}) collective-permute-start(f32[192,128]{1,0:T(8,128)S(1)} %get-tuple-element.39.refs_2_.refs_8_), channel_id=1, source_target_pairs={{0,1},{1,0},{2,3},{3,2},{4,5},{5,4},{6,7},{7,6},{8,9},{9,8},{10,11... | collective-permute-start | bytes 294920 | tf_op jit(solution)/shard_map/ppermute | solution.py:559
  23.3 5.7 %collective-permute-start.8 = (f32[96,128]{1,0:T(8,128)S(1)}, f32[96,128]{1,0:T(8,128)S(1)}, u32[]{:S(2)}, u32[]{:S(2)}) collective-permute-start(f32[96,128]{1,0:T(8,128)S(1)} %get-tuple-element.41), channel_id=1, source_target_pairs={{0,4},{4,0},{8,12},{12,8},{16,20},{20,16},{24,28},{28,24},{1,5},{5... | collective-permute-start | bytes 147464 | tf_op jit(solution)/shard_map/ppermute | solution.py:557
  23.5 6.8 %collective-permute-start.9 = (f32[96,128]{1,0:T(8,128)S(1)}, f32[96,128]{1,0:T(8,128)S(1)}, u32[]{:S(2)}, u32[]{:S(2)}) collective-permute-start(f32[96,128]{1,0:T(8,128)S(1)} %get-tuple-element.42), channel_id=1, source_target_pairs={{4,8},{8,4},{12,16},{16,12},{20,24},{24,20},{28,0},{0,28},{5,9},{9... | collective-permute-start | bytes 147464 | tf_op jit(solution)/shard_map/ppermute | solution.py:556
  30.8 7.5 %collective-permute-start.15 = (f32[192,128]{1,0:T(8,128)S(1)}, f32[192,128]{1,0:T(8,128)S(1)}, u32[]{:S(2)}, u32[]{:S(2)}) collective-permute-start(f32[192,128]{1,0:T(8,128)S(1)} %get-tuple-element.43.refs_3_.refs_9_), channel_id=1, source_target_pairs={{1,2},{2,1},{3,0},{0,3},{5,6},{6,5},{7,4},{4,7},{9,10},{10,9},{11,... | collective-permute-start | bytes 294920 | tf_op jit(solution)/shard_map/ppermute | solution.py:558
  30.9 7.4 %collective-permute-start.14 = (f32[192,128]{1,0:T(8,128)S(1)}, f32[192,128]{1,0:T(8,128)S(1)}, u32[]{:S(2)}, u32[]{:S(2)}) collective-permute-start(f32[192,128]{1,0:T(8,128)S(1)} %get-tuple-element.43.refs_3_.refs_9_), channel_id=1, source_target_pairs={{0,1},{1,0},{2,3},{3,2},{4,5},{5,4},{6,7},{7,6},{8,9},{9,8},{10,11... | collective-permute-start | bytes 294920 | tf_op jit(solution)/shard_map/ppermute | solution.py:559
  31.5 5.5 %collective-permute-start.12 = (f32[96,128]{1,0:T(8,128)S(1)}, f32[96,128]{1,0:T(8,128)S(1)}, u32[]{:S(2)}, u32[]{:S(2)}) collective-permute-start(f32[96,128]{1,0:T(8,128)S(1)} %get-tuple-element.46), channel_id=1, source_target_pairs={{0,4},{4,0},{8,12},{12,8},{16,20},{20,16},{24,28},{28,24},{1,5},{5... | collective-permute-start | bytes 147464 | tf_op jit(solution)/shard_map/ppermute | solution.py:557
  31.5 6.8 %collective-permute-start.13 = (f32[96,128]{1,0:T(8,128)S(1)}, f32[96,128]{1,0:T(8,128)S(1)}, u32[]{:S(2)}, u32[]{:S(2)}) collective-permute-start(f32[96,128]{1,0:T(8,128)S(1)} %get-tuple-element.47), channel_id=1, source_target_pairs={{4,8},{8,4},{12,16},{16,12},{20,24},{24,20},{28,0},{0,28},{5,9},{9... | collective-permute-start | bytes 147464 | tf_op jit(solution)/shard_map/ppermute | solution.py:556
  36.1 11.1 %collective-permute-start.20 = (f32[192,128]{1,0:T(8,128)S(1)}, f32[192,128]{1,0:T(8,128)S(1)}, u32[]{:S(2)}, u32[]{:S(2)}) collective-permute-start(f32[192,128]{1,0:T(8,128)S(1)} %get-tuple-element.52.refs_5_), channel_id=1, source_target_pairs={{0,3},{1,2},{2,1},{3,0},{4,7},{5,6},{6,5},{7,4},{8,11},{9,10},{10,... | collective-permute-start | bytes 294920 | tf_op jit(solution)/shard_map/ppermute | solution.py:550
  37.0 15.0 %collective-permute-start.18 = (f32[192,128]{1,0:T(8,128)S(1)}, f32[192,128]{1,0:T(8,128)S(1)}, u32[]{:S(2)}, u32[]{:S(2)}) collective-permute-start(f32[192,128]{1,0:T(8,128)S(1)} %get-tuple-element.52.refs_5_), channel_id=1, source_target_pairs={{0,2},{1,3},{2,0},{3,1},{4,6},{5,7},{6,4},{7,5},{8,10},{9,11},{10,... | collective-permute-start | bytes 294920 | tf_op jit(solution)/shard_map/ppermute | solution.py:550
  38.3 13.7 %collective-permute-start.16 = (f32[192,128]{1,0:T(8,128)S(1)}, f32[192,128]{1,0:T(8,128)S(1)}, u32[]{:S(2)}, u32[]{:S(2)}) collective-permute-start(f32[192,128]{1,0:T(8,128)S(1)} %get-tuple-element.52.refs_5_), channel_id=1, source_target_pairs={{0,1},{1,0},{2,3},{3,2},{4,5},{5,4},{6,7},{7,6},{8,9},{9,8},{10,11... | collective-permute-start | bytes 294920 | tf_op jit(solution)/shard_map/ppermute | solution.py:550
  39.6 12.3 %all-to-all-start = ((f32[32,3,128]{2,1,0:T(4,128)}), f32[32,3,128]{2,1,0:T(4,128)S(1)}, u32[]{:S(2)}, u32[]{:S(2)}) async-start(f32[32,3,128]{2,1,0:T(4,128)} %get-tuple-element.51), calls=%async_computation | async-start | bytes 131072 | tf_op jit(solution)/shard_map/all_to_all | solution.py:621
  45.3 6.7 %collective-permute-start.21 = (f32[48,128]{1,0:T(8,128)S(1)}, f32[48,128]{1,0:T(8,128)S(1)}, u32[]{:S(2)}, u32[]{:S(2)}) collective-permute-start(f32[48,128]{1,0:T(8,128)S(1)} %shard_map.59.refs_6_), channel_id=1, source_target_pairs={{0,3},{1,2},{2,1},{3,0},{4,7},{5,6},{6,5},{7,4},{8,11},{9,10},{10,... | collective-permute-start | bytes 73736 | tf_op jit(solution)/shard_map/ppermute | solution.py:550
  46.8 5.2 %collective-permute-start.19 = (f32[48,128]{1,0:T(8,128)S(1)}, f32[48,128]{1,0:T(8,128)S(1)}, u32[]{:S(2)}, u32[]{:S(2)}) collective-permute-start(f32[48,128]{1,0:T(8,128)S(1)} %shard_map.59.refs_6_), channel_id=1, source_target_pairs={{0,2},{1,3},{2,0},{3,1},{4,6},{5,7},{6,4},{7,5},{8,10},{9,11},{10,... | collective-permute-start | bytes 73736 | tf_op jit(solution)/shard_map/ppermute | solution.py:550
  47.2 4.8 %collective-permute-start.17 = (f32[48,128]{1,0:T(8,128)S(1)}, f32[48,128]{1,0:T(8,128)S(1)}, u32[]{:S(2)}, u32[]{:S(2)}) collective-permute-start(f32[48,128]{1,0:T(8,128)S(1)} %shard_map.59.refs_6_), channel_id=1, source_target_pairs={{0,1},{1,0},{2,3},{3,2},{4,5},{5,4},{6,7},{7,6},{8,9},{9,8},{10,11... | collective-permute-start | bytes 73736 | tf_op jit(solution)/shard_map/ppermute | solution.py:550
